TPU v7x, 32 devices: a whole 2x2x4 slice. The times are simulated.
32 devices in a mesh: grp: 2 (over y), wa: 4 (over z), ta: 4 (over x, core).
Axes of the slice: x: 2, y: 2, z: 4, core: 2. Of those that a mesh axis runs over, the one named last changes fastest.
Arguments:
- node_features: float32 [8, 512, 1024], P(('grp', 'wa'), 'ta'), parts along dimension 0, may hold values from -21 to 21
- sensor_adjoint: float32 [8, 512, 1024], P(('grp', 'wa'), 'ta'), parts along dimension 0, may hold values from -6 to 6
- sensor_node: int32 [512], P('ta'), may hold values from 0 to 511, as said below
- neighbours: int32 [4, 2], replicated, may hold values from 0 to 3, as said below
- w_query: float32 [1024, 1024], P('wa', 'ta'), may hold values from -0.1875 to 0.1875
- w_key: float32 [1024, 1024], P('wa', 'ta'), may hold values from -0.1875 to 0.1875
- w_value: float32 [1024, 1024], P('wa', 'ta'), may hold values from -0.1875 to 0.1875
Outputs:
- input_adjoint: float32 [8, 512, 1024], P(('grp', 'wa'), 'ta'), parts along dimension 0
- query_weight_grad: float32 [2048, 1024], P(('grp', 'wa'), 'ta'), parts along dimension 0
- key_weight_grad: float32 [2048, 1024], P(('grp', 'wa'), 'ta'), parts along dimension 0
- value_weight_grad: float32 [2048, 1024], P(('grp', 'wa'), 'ta'), parts along dimension 0
There are 2 independent parts, one for each index of `grp`. A program takes and returns all parts, laid end to end along the dimension named above; an argument that names none is the same for every part. Nothing has to cross between parts.
Inputs may be any that keep to these rules, and one draw needn't show every extreme that they name: `sensor_node`: each aligned block of 128 entries is a permutation of that block's node numbers. `neighbours`: each row names 2 different blocks.
All inputs are finite; a program needn't handle non-finite values.
Results may differ from a plain program's by a relative error of at most 0.0003.
Values sent between devices are 32-bit elements; how exact they have to be, the bound alone decides.
No kernel may reach another device: no remote copies, remote signals or barrier semaphores. Data moves between devices by JAX's collectives and lax.ppermute only.
A program may use at most 64 MiB of HBM per device.

v0:
```python
import functools

import jax
import jax.numpy as jnp
from jax import lax
from jax.experimental import pallas as pl
from jax.experimental.pallas import tpu as pltpu
from jax.sharding import PartitionSpec as P

DH = 64
BLOCK = 128
KB = 2
LANES = 128
F32 = jnp.float32
NN = ((1,), (0,))
NT = ((1,), (1,))
TN = ((0,), (0,))


def dot(left, right, dims):
    return lax.dot_general(
        left, right, (dims, ((), ())), precision=lax.Precision.HIGHEST, preferred_element_type=F32
    )


def local_call(body, outs, args, scalars=(), scratch=(), flops=0, vmem_mib=24):
    vmem = pl.BlockSpec(memory_space=pltpu.VMEM)
    smem = pl.BlockSpec(memory_space=pltpu.SMEM)
    moved = sum(4 * a.size for a in args) + sum(4 * o.size for o in outs)
    return pl.pallas_call(
        body,
        out_shape=outs,
        in_specs=[smem] * len(scalars) + [vmem] * len(args),
        out_specs=[vmem] * len(outs),
        scratch_shapes=scratch,
        cost_estimate=pl.CostEstimate(flops=flops, bytes_accessed=moved, transcendentals=0),
        compiler_params=pltpu.CompilerParams(vmem_limit_bytes=vmem_mib << 20),
    )(*scalars, *args)


def shaped(*shape):
    return jax.ShapeDtypeStruct(shape, F32)


def swap(value, axis, size, step):
    return lax.ppermute(value, axis, [(i, i ^ step) for i in range(size)])


def halves_body(chunks, wq, wk, wv, *outs):
    for c in range(chunks):
        cols = slice(c * LANES, (c + 1) * LANES)
        outs[c][:, 0:LANES] = wq[:, cols]
        outs[c][:, LANES : 2 * LANES] = wk[:, cols]
        outs[c][:, 2 * LANES : 3 * LANES] = wv[:, cols]


def weight_halves(info, w_query, w_key, w_value, rows, chunks):
    columns = w_query.shape[1]
    spec = pl.BlockSpec((rows, columns), lambda i, info: (info[1], 0))
    out = pl.BlockSpec((rows, 3 * LANES), lambda i, info: (0, 0))
    return pl.pallas_call(
        functools.partial(halves_body_prefetch, chunks),
        out_shape=[shaped(rows, 3 * LANES)] * chunks,
        grid_spec=pltpu.PrefetchScalarGridSpec(
            num_scalar_prefetch=1, grid=(1,), in_specs=[spec] * 3, out_specs=[out] * chunks
        ),
    )(info, w_query, w_key, w_value)


def halves_body_prefetch(chunks, info, *refs):
    halves_body(chunks, *refs)


def adjoint_body(parts, info, ids, sensors, *refs):
    outs, rows = refs[:parts], refs[parts]
    count = sensors.shape[0]
    columns = outs[0].shape[1]
    local = ids[...] - info[2] * count
    chosen = lax.broadcasted_iota(jnp.int32, (count, count), 0) == local
    rows[...] = dot(chosen.astype(F32), sensors[...], NN)
    for r in range(parts):
        start = pl.multiple_of((info[2] ^ r) * columns, LANES)
        outs[r][...] = rows[:, pl.ds(start, columns)]


def stack_body(parts, *refs):
    rows = refs[0].shape[0]
    for r in range(parts):
        refs[parts][r * rows : (r + 1) * rows, :] = refs[r][...]


def attention_body(chunk, blocks, pieces, info, neighbours, *refs):
    x, wq, wk, wv = refs[:4]
    halves = refs[4 : 4 + len(pieces)]
    adjoints = refs[4 + len(pieces) : 4 + len(pieces) + blocks]
    out, panel, proj = refs[4 + len(pieces) + blocks :]
    z, y, t = info[0], info[1], info[2]
    cols = slice(chunk * LANES, (chunk + 1) * LANES)
    own = wq.shape[0]
    rows = pl.ds(pl.multiple_of(z * own, 8), own)
    panel[rows, 0:LANES] = wq[:, cols]
    panel[rows, LANES : 2 * LANES] = wk[:, cols]
    panel[rows, 2 * LANES : 3 * LANES] = wv[:, cols]
    for (r, g), half in zip(pieces, halves):
        count = half.shape[0]
        start = (z ^ r) * own + (y ^ g) * count
        panel[pl.ds(pl.multiple_of(start, 8), count), :] = half[...]
    attention_core(cols, blocks, t, neighbours, x, panel, adjoints, out, proj)


def attention_panel_body(chunk, blocks, info, neighbours, x, panel, *refs):
    cols = slice(chunk * LANES, (chunk + 1) * LANES)
    attention_core(
        cols, blocks, info[2], neighbours, x, panel, refs[:blocks], refs[blocks], refs[blocks + 1]
    )


def attention_core(cols, blocks, t, neighbours, x, panel, adjoints, out, proj):
    proj[...] = dot(x[...], panel[...], NN)
    out[:, LANES:] = jnp.zeros((out.shape[0], 2 * LANES), F32)
    first = lax.broadcasted_iota(jnp.int32, (BLOCK, LANES), 1) < DH
    scale = DH ** (-0.5)

    def by_head(value):
        return jnp.concatenate(
            [jnp.where(first, value, 0.0), jnp.where(first, 0.0, value)], axis=0
        )

    for r in range(blocks):
        here = slice(r * BLOCK, (r + 1) * BLOCK)
        there = [
            pl.ds(pl.multiple_of((neighbours[t ^ r, j] ^ t) * BLOCK, BLOCK), BLOCK)
            for j in range(KB)
        ]
        query = by_head(proj[here, 0:LANES])
        adjoint = by_head(adjoints[r][:, cols])
        key = jnp.concatenate([proj[w, LANES : 2 * LANES] for w in there], axis=0)
        value = jnp.concatenate([proj[w, 2 * LANES :] for w in there], axis=0)
        scores = dot(query, key, NT) * scale
        raised = jnp.exp(scores - jnp.max(scores, axis=1, keepdims=True))
        attention = raised / jnp.sum(raised, axis=1, keepdims=True)
        weight_adjoint = dot(adjoint, value, NT)
        row_dots = jnp.sum(attention * weight_adjoint, axis=1, keepdims=True)
        score_adjoint = attention * (weight_adjoint - row_dots) * scale
        both = dot(score_adjoint, key, NN)
        out[here, 0:LANES] = jnp.where(first, both[:BLOCK], both[BLOCK:])
        dkey = dot(score_adjoint, query, TN)
        dvalue = dot(attention, adjoint, TN)
        for j, w in enumerate(there):
            part = slice(j * BLOCK, (j + 1) * BLOCK)
            out[w, LANES : 2 * LANES] += dkey[part]
            out[w, 2 * LANES :] += dvalue[part]


def weight_grad_body(shares, rows, info, x, stacked, out):
    for j, r in enumerate(shares):
        start = pl.multiple_of((info[0] ^ r) * rows, LANES)
        out[j * rows : (j + 1) * rows, :] = dot(x[:, pl.ds(start, rows)], stacked[...], TN)


def whole_grad_body(x, stacked, out):
    out[...] = dot(x[...], stacked[...], TN)


def back_body(shares, chunks, *refs):
    stacked, panels, out = refs[:chunks], refs[chunks : 2 * chunks], refs[2 * chunks]
    total = None
    for c in range(chunks):
        rows = jnp.concatenate(
            [stacked[c][r * BLOCK : (r + 1) * BLOCK, :] for r in shares], axis=0
        )
        term = dot(rows, panels[c][...], NT)
        total = term if total is None else total + term
    out[...] = total


def scatter_halving(send, keep, axis, size, rows):
    step = 1
    while True:
        got = swap(send, axis, size, step)
        step *= 2
        if step == size:
            return keep, got
        total = (keep + got).reshape(-1, 2, rows, keep.shape[1])
        send, keep = total[:, 1].reshape(-1, keep.shape[1]), total[:, 0].reshape(-1, keep.shape[1])


def per_device(sizes, node_features, sensor_adjoint, sensor_node, neighbours, *weights):
    grp, wa, ta = sizes
    hour_rows = node_features[0]
    nodes_here, width = hour_rows.shape
    rows_here, columns = weights[0].shape
    chunks = columns // LANES
    blocks = ta
    nodes = nodes_here * ta
    z, y, t = lax.axis_index("wa"), lax.axis_index("grp"), lax.axis_index("ta")
    info = jnp.stack([z, y, t]).astype(jnp.int32)
    direct = rows_here % LANES == 0 and rows_here % (8 * grp) == 0 and wa > 1

    held = {0: hour_rows}
    step = ta
    while step > 1:
        step //= 2
        held.update({r | step: swap(v, "ta", ta, step) for r, v in list(held.items())})
    inputs = local_call(
        functools.partial(stack_body, ta), [shaped(nodes, width)], [held[r] for r in range(ta)]
    )[0]

    blocks_out = local_call(
        functools.partial(adjoint_body, ta),
        [shaped(nodes_here, columns)] * ta,
        [sensor_node.reshape(1, -1), sensor_adjoint[0]],
        scalars=[info],
        scratch=[pltpu.VMEM((nodes_here, width), F32)],
        flops=12 * nodes_here * nodes_here * width,
    )
    adjoints = [blocks_out[0]] + [swap(blocks_out[r], "ta", ta, r) for r in range(1, ta)]

    stacked, panels, owned = [], [], []
    if direct:
        half = rows_here // grp
        halves = weight_halves(info, *weights, half, chunks)
    for c in range(chunks):
        proj_flops = 12 * nodes * width * 3 * LANES + 60 * 2 * nodes * 4 * BLOCK * LANES
        scratch = [pltpu.VMEM((nodes, 3 * LANES), F32)]
        if direct:
            mine = {0: halves[c]}
            step = wa
            while step > 1:
                step //= 2
                mine.update({r | step: swap(v, "wa", wa, step) for r, v in list(mine.items())})
            pieces = {(r, 0): mine[r] for r in range(1, wa)}
            for g in range(1, grp):
                pieces.update({(r, g): swap(mine[r], "grp", grp, g) for r in range(1, wa)})
            names = sorted(pieces)
            dqkv, panel = local_call(
                functools.partial(attention_body, c, blocks, names),
                [shaped(nodes, 3 * LANES), shaped(width, 3 * LANES)],
                [inputs, *weights, *[pieces[n] for n in names], *adjoints],
                scalars=[info, neighbours],
                scratch=scratch,
                flops=proj_flops,
            )
        else:
            cols = slice(c * LANES, (c + 1) * LANES)
            local = jnp.concatenate([w[:, cols] for w in weights], axis=1)
            panel = lax.all_gather(local, "wa", axis=0, tiled=True)
            dqkv = local_call(
                functools.partial(attention_panel_body, c, blocks),
                [shaped(nodes, 3 * LANES)],
                [inputs, panel, *adjoints],
                scalars=[info, neighbours],
                scratch=scratch,
                flops=proj_flops,
            )[0]
        stacked.append(dqkv)
        panels.append(panel)
        if direct:
            sends = [
                local_call(
                    functools.partial(weight_grad_body, range(odd, wa, 2), rows_here),
                    [shaped(rows_here * wa // 2, 3 * LANES)],
                    [inputs, dqkv],
                    scalars=[info],
                    flops=12 * nodes * rows_here * wa // 2 * 3 * LANES,
                )[0]
                for odd in (1, 0)
            ]
            kept, got = scatter_halving(*sends, "wa", wa, rows_here)
            owned.append(kept + got)
        else:
            full = local_call(
                whole_grad_body,
                [shaped(width, 3 * LANES)],
                [inputs, dqkv],
                flops=12 * nodes * width * 3 * LANES,
            )[0]
            owned.append(lax.psum_scatter(full, "wa", scatter_dimension=0, tiled=True))

    backs = [
        local_call(
            functools.partial(back_body, range(odd, ta, 2), chunks),
            [shaped(nodes // 2, width)],
            [*stacked, *panels],
            flops=12 * nodes // 2 * width * columns * 3,
        )[0]
        for odd in (1, 0)
    ]
    kept, got = scatter_halving(*backs, "ta", ta, nodes_here)
    grads = [
        jnp.concatenate([o[:, i * LANES : (i + 1) * LANES] for o in owned], axis=1)
        for i in range(3)
    ]
    return ((kept + got)[None], *grads)


def solution(mesh):
    sizes = tuple(mesh.shape[name] for name in ("grp", "wa", "ta"))
    return jax.shard_map(
        functools.partial(per_device, sizes),
        mesh=mesh,
        in_specs=(
            P(("grp", "wa"), "ta", None),
            P(("grp", "wa"), "ta", None),
            P("ta"),
            P(),
            P("wa", "ta"),
            P("wa", "ta"),
            P("wa", "ta"),
        ),
        out_specs=(
            P(("grp", "wa"), "ta", None),
            P(("grp", "wa"), "ta"),
            P(("grp", "wa"), "ta"),
            P(("grp", "wa"), "ta"),
        ),
        check_vma=False,
    )
```

profile of v0, /device:TPU:0, one launch (start us, length us, event | category | flops | bytes accessed | tf_op | source)
XLA Modules:
  0.0 148.7 jit_solution(16987170409448508874)
XLA Ops:
  0.6 3.0 %collective-permute-start.1 = (f32[128,1024]{1,0:T(8,128)}, f32[128,1024]{1,0:T(8,128)S(1)}, u32[]{:S(2)}, u32[]{:S(2)}) collective-permute-start(f32[128,1024]{1,0:T(8,128)} %bitcast.31), channel_id=1, source_target_pairs={{0,2},{1,3},{2,0},{3,1},{4,6},{5,7},{6,4},{7,5},{8,10},{9,11},{10,... | collective-permute-start | bytes 1572872 | tf_op jit(solution)/shard_map/ppermute | solution.py:46
  3.6 0.0 collective-permute-start
  3.6 12.1 %collective-permute-done.1.refs_2_ = f32[128,1024]{1,0:T(8,128)S(1)} collective-permute-done((f32[128,1024]{1,0:T(8,128)}, f32[128,1024]{1,0:T(8,128)S(1)}, u32[]{:S(2)}, u32[]{:S(2)}) %collective-permute-start.1) | collective-permute-done | bytes 524320 | tf_op jit(solution)/shard_map/ppermute | solution.py:46
  15.8 0.1 pad_add_fusion.info
  15.9 1.0 copy-done.6
  16.9 0.7 copy-done.13
  17.6 1.2 shard_map.104
  18.7 0.0 copy-start.14
  18.7 0.6 copy-done.14
  19.4 0.5 collective-permute-start.9
  19.9 2.4 %shard_map.103 = (f32[128,384]{1,0:T(8,128)}, f32[128,384]{1,0:T(8,128)}) custom-call(s32[3]{0:T(128)} %copy-done.4, f32[256,256]{1,0:T(8,128)} %refs_1_.5, f32[256,256]{1,0:T(8,128)} %refs_2_.5, f32[256,256]{1,0:T(8,128)} %refs_3_.3), custom_call_target="tpu_custom_call" | custom-call | tf_op jit(solution)/shard_map/pallas_call | solution.py:61
  22.3 2.8 %collective-permute-start.14 = (f32[128,384]{1,0:T(8,128)}, f32[128,384]{1,0:T(8,128)S(1)}, u32[]{:S(2)}, u32[]{:S(2)}) collective-permute-start(f32[128,384]{1,0:T(8,128)} %get-tuple-element.20), channel_id=1, source_target_pairs={{0,8},{4,12},{8,0},{12,4},{1,9},{5,13},{9,1},{13,5},{2,10},{6,14},... | collective-permute-start | bytes 589832 | tf_op jit(solution)/shard_map/ppermute | solution.py:46
  25.2 1.5 %collective-permute-start.10 = (f32[128,256]{1,0:T(8,128)S(1)}, f32[128,256]{1,0:T(8,128)S(1)}, u32[]{:S(2)}, u32[]{:S(2)}) collective-permute-start(f32[128,256]{1,0:T(8,128)S(1)} %get-tuple-element.17), channel_id=1, source_target_pairs={{0,2},{1,3},{2,0},{3,1},{4,6},{5,7},{6,4},{7,5},{8,10},{9,11},{10,... | collective-permute-start | bytes 393224 | tf_op jit(solution)/shard_map/ppermute | solution.py:46
  26.7 0.7 copy-done.7
  27.3 0.0 collective-permute-start.11
  27.3 3.0 %collective-permute-done.10.refs_12_ = f32[128,256]{1,0:T(8,128)S(1)} collective-permute-done((f32[128,256]{1,0:T(8,128)S(1)}, f32[128,256]{1,0:T(8,128)S(1)}, u32[]{:S(2)}, u32[]{:S(2)}) %collective-permute-start.10) | collective-permute-done | bytes 131104 | tf_op jit(solution)/shard_map/ppermute | solution.py:46
  30.3 0.7 copy-done.9
  31.0 0.5 collective-permute-start.5
  31.5 1.6 %collective-permute-done.11.refs_13_ = f32[128,256]{1,0:T(8,128)S(1)} collective-permute-done((f32[128,256]{1,0:T(8,128)S(1)}, f32[128,256]{1,0:T(8,128)S(1)}, u32[]{:S(2)}, u32[]{:S(2)}) %collective-permute-start.11) | collective-permute-done | bytes 131104 | tf_op jit(solution)/shard_map/ppermute | solution.py:46
  33.1 0.7 copy-done.11
  33.8 1.6 %collective-permute-start.12 = (f32[128,384]{1,0:T(8,128)}, f32[128,384]{1,0:T(8,128)S(1)}, u32[]{:S(2)}, u32[]{:S(2)}) collective-permute-start(f32[128,384]{1,0:T(8,128)} %get-tuple-element.20), channel_id=1, source_target_pairs={{0,4},{4,0},{8,12},{12,8},{1,5},{5,1},{9,13},{13,9},{2,6},{6,2},{1... | collective-permute-start | bytes 589832 | tf_op jit(solution)/shard_map/ppermute | solution.py:46
  35.3 3.0 %collective-permute-done.14.refs_6_ = f32[128,384]{1,0:T(8,128)S(1)} collective-permute-done((f32[128,384]{1,0:T(8,128)}, f32[128,384]{1,0:T(8,128)S(1)}, u32[]{:S(2)}, u32[]{:S(2)}) %collective-permute-start.14) | collective-permute-done | bytes 196640 | tf_op jit(solution)/shard_map/ppermute | solution.py:46
  38.3 1.6 %collective-permute-start.16 = (f32[128,384]{1,0:T(8,128)S(1)}, f32[128,384]{1,0:T(8,128)S(1)}, u32[]{:S(2)}, u32[]{:S(2)}) collective-permute-start(f32[128,384]{1,0:T(8,128)S(1)} %collective-permute-done.14.refs_6_), channel_id=1, source_target_pairs={{0,4},{4,0},{8,12},{12,8},{1,5},{5,1},{9,13},{13,9},{2,6},{6,2},{1... | collective-permute-start | bytes 589832 | tf_op jit(solution)/shard_map/ppermute | solution.py:46
  39.8 3.3 %collective-permute-done.5.refs_6_ = f32[128,384]{1,0:T(8,128)S(1)} collective-permute-done((f32[128,384]{1,0:T(8,128)}, f32[128,384]{1,0:T(8,128)S(1)}, u32[]{:S(2)}, u32[]{:S(2)}) %collective-permute-start.5) | collective-permute-done | bytes 196640 | tf_op jit(solution)/shard_map/ppermute | solution.py:46
  43.2 0.8 collective-permute-start.3
  44.0 1.6 %collective-permute-done.12.refs_4_ = f32[128,384]{1,0:T(8,128)S(1)} collective-permute-done((f32[128,384]{1,0:T(8,128)}, f32[128,384]{1,0:T(8,128)S(1)}, u32[]{:S(2)}, u32[]{:S(2)}) %collective-permute-start.12) | collective-permute-done | bytes 196640 | tf_op jit(solution)/shard_map/ppermute | solution.py:46
  45.6 0.0 collective-permute-start.7
  45.6 4.2 %collective-permute-done.16.refs_8_ = f32[128,384]{1,0:T(8,128)S(1)} collective-permute-done((f32[128,384]{1,0:T(8,128)S(1)}, f32[128,384]{1,0:T(8,128)S(1)}, u32[]{:S(2)}, u32[]{:S(2)}) %collective-permute-start.16) | collective-permute-done | bytes 196640 | tf_op jit(solution)/shard_map/ppermute | solution.py:46
  49.8 1.6 %collective-permute-start.13 = (f32[128,384]{1,0:T(8,128)S(1)}, f32[128,384]{1,0:T(8,128)S(1)}, u32[]{:S(2)}, u32[]{:S(2)}) collective-permute-start(f32[128,384]{1,0:T(8,128)S(1)} %collective-permute-done.12.refs_4_), channel_id=1, source_target_pairs={{0,16},{16,0},{1,17},{17,1},{2,18},{18,2},{3,19},{19,3},{4,20},{20... | collective-permute-start | bytes 589832 | tf_op jit(solution)/shard_map/ppermute | solution.py:46
  51.4 0.0 collective-permute-done.refs_1_
  51.4 0.5 collective-permute-start.15
  51.9 1.5 %collective-permute-start.17 = (f32[128,384]{1,0:T(8,128)S(1)}, f32[128,384]{1,0:T(8,128)}, u32[]{:S(2)}, u32[]{:S(2)}) collective-permute-start(f32[128,384]{1,0:T(8,128)S(1)} %collective-permute-done.16.refs_8_), channel_id=1, source_target_pairs={{0,16},{16,0},{1,17},{17,1},{2,18},{18,2},{3,19},{19,3},{4,20},{20... | collective-permute-start | bytes 589832 | tf_op jit(solution)/shard_map/ppermute | solution.py:46
  53.4 0.8 copy.11.neighbours
  54.2 0.0 copy-start.8
  54.2 0.0 copy-start.15
  54.3 0.1 shard_map.102.refs_0_.x
  54.4 1.2 collective-permute-start.6
  55.6 2.1 %collective-permute-done.7.refs_8_ = f32[128,384]{1,0:T(8,128)S(1)} collective-permute-done((f32[128,384]{1,0:T(8,128)S(1)}, f32[128,384]{1,0:T(8,128)S(1)}, u32[]{:S(2)}, u32[]{:S(2)}) %collective-permute-start.7) | collective-permute-done | bytes 196640 | tf_op jit(solution)/shard_map/ppermute | solution.py:46
  57.7 1.6 %collective-permute-start.4 = (f32[128,384]{1,0:T(8,128)S(1)}, f32[128,384]{1,0:T(8,128)S(1)}, u32[]{:S(2)}, u32[]{:S(2)}) collective-permute-start(f32[128,384]{1,0:T(8,128)S(1)} %collective-permute-done.3.refs_4_), channel_id=1, source_target_pairs={{0,16},{16,0},{1,17},{17,1},{2,18},{18,2},{3,19},{19,3},{4,20},{20... | collective-permute-start | bytes 589832 | tf_op jit(solution)/shard_map/ppermute | solution.py:46
  59.3 0.5 collective-permute-start.8
  59.8 2.2 %collective-permute-done.15.refs_7_ = f32[128,384]{1,0:T(8,128)} collective-permute-done((f32[128,384]{1,0:T(8,128)S(1)}, f32[128,384]{1,0:T(8,128)}, u32[]{:S(2)}, u32[]{:S(2)}) %collective-permute-start.15) | collective-permute-done | bytes 196640 | tf_op jit(solution)/shard_map/ppermute | solution.py:46
  62.0 4.2 %collective-permute-done.17.refs_9_ = f32[128,384]{1,0:T(8,128)} collective-permute-done((f32[128,384]{1,0:T(8,128)S(1)}, f32[128,384]{1,0:T(8,128)}, u32[]{:S(2)}, u32[]{:S(2)}) %collective-permute-start.17) | collective-permute-done | bytes 196640 | tf_op jit(solution)/shard_map/ppermute | solution.py:46
  66.3 10.4 %shard_map.106 = (f32[512,384]{1,0:T(8,128)S(1)}, f32[1024,384]{1,0:T(8,128)S(1)}) custom-call(s32[3]{0:T(128)S(1)} %copy-done.5, s32[4,2]{1,0:T(4,128)S(1)} %copy.11.neighbours, f32[512,1024]{1,0:T(8,128)S(1)} %shard_map.102.refs_0_.x, f32[256,256]{1,0:T(8,128)S(1)} %copy-done.1, f32[256,256]{1,0:T(8,128)S(1)} %copy-done.2, f32[256,256]{1,0:T(8,128)S(1)} %copy-done.3, ...), custom_call_target="tpu_custom_call" | custom-call | flops 6442450944 | bytes 6946816 | tf_op jit(solution)/shard_map/pallas_call | solution.py:30
  76.6 2.6 %shard_map.112 = f32[512,384]{1,0:T(8,128)S(1)} custom-call(s32[3]{0:T(128)S(1)} %copy-done.5, f32[512,1024]{1,0:T(8,128)S(1)} %shard_map.102.refs_0_.x, f32[512,384]{1,0:T(8,128)S(1)} %get-tuple-element.21.refs_1_.stacked), custom_call_target="tpu_custom_call" | custom-call | flops 1207959552 | bytes 3670016 | tf_op jit(solution)/shard_map/pallas_call | solution.py:30
  79.3 0.1 collective-permute-start.22
  79.4 9.9 %shard_map.105 = (f32[512,384]{1,0:T(8,128)S(1)}, f32[1024,384]{1,0:T(8,128)S(1)}) custom-call(s32[3]{0:T(128)S(1)} %copy-done.5, s32[4,2]{1,0:T(4,128)S(1)} %copy.11.neighbours, f32[512,1024]{1,0:T(8,128)S(1)} %shard_map.102.refs_0_.x, f32[256,256]{1,0:T(8,128)S(1)} %copy-done.1, f32[256,256]{1,0:T(8,128)S(1)} %copy-done.2, f32[256,256]{1,0:T(8,128)S(1)} %copy-done.3, ...), custom_call_target="tpu_custom_call" | custom-call | flops 6442450944 | bytes 6946816 | tf_op jit(solution)/shard_map/pallas_call | solution.py:30
  89.3 3.8 %shard_map.108 = f32[256,1024]{1,0:T(8,128)S(1)} custom-call(f32[512,384]{1,0:T(8,128)S(1)} %get-tuple-element.19.refs_0_.stacked, f32[512,384]{1,0:T(8,128)S(1)} %get-tuple-element.21.refs_1_.stacked, f32[1024,384]{1,0:T(8,128)S(1)} %get-tuple-element.22.refs_2_, f32[1024,384]{1,0:T(8,128)S(1)} %get-tuple-element.23.refs_3_), custom_call_target="tpu_custom_call" | custom-call | flops 2415919104 | bytes 5767168 | tf_op jit(solution)/shard_map/pallas_call | solution.py:30
  93.0 0.1 collective-permute-start.18
  93.1 2.4 %shard_map.110 = f32[512,384]{1,0:T(8,128)S(1)} custom-call(s32[3]{0:T(128)S(1)} %copy-done.5, f32[512,1024]{1,0:T(8,128)S(1)} %shard_map.102.refs_0_.x, f32[512,384]{1,0:T(8,128)S(1)} %get-tuple-element.19.refs_0_.stacked), custom_call_target="tpu_custom_call" | custom-call | flops 1207959552 | bytes 3670016 | tf_op jit(solution)/shard_map/pallas_call | solution.py:30
  95.5 2.1 %collective-permute-start.20 = (f32[512,384]{1,0:T(8,128)S(1)}, f32[512,384]{1,0:T(8,128)S(1)}, u32[]{:S(2)}, u32[]{:S(2)}) collective-permute-start(f32[512,384]{1,0:T(8,128)S(1)} %shard_map.110), channel_id=1, source_target_pairs={{0,4},{4,0},{8,12},{12,8},{1,5},{5,1},{9,13},{13,9},{2,6},{6,2},{1... | collective-permute-start | bytes 2359304 | tf_op jit(solution)/shard_map/ppermute | solution.py:46
  97.6 2.4 %shard_map.111 = f32[512,384]{1,0:T(8,128)S(1)} custom-call(s32[3]{0:T(128)S(1)} %copy-done.5, f32[512,1024]{1,0:T(8,128)S(1)} %shard_map.102.refs_0_.x, f32[512,384]{1,0:T(8,128)S(1)} %get-tuple-element.21.refs_1_.stacked), custom_call_target="tpu_custom_call" | custom-call | flops 1207959552 | bytes 3670016 | tf_op jit(solution)/shard_map/pallas_call | solution.py:30
  100.1 2.5 %shard_map.109 = f32[512,384]{1,0:T(8,128)S(1)} custom-call(s32[3]{0:T(128)S(1)} %copy-done.5, f32[512,1024]{1,0:T(8,128)S(1)} %shard_map.102.refs_0_.x, f32[512,384]{1,0:T(8,128)S(1)} %get-tuple-element.19.refs_0_.stacked), custom_call_target="tpu_custom_call" | custom-call | flops 1207959552 | bytes 3670016 | tf_op jit(solution)/shard_map/pallas_call | solution.py:30
  102.5 3.5 %shard_map.107 = f32[256,1024]{1,0:T(8,128)S(1)} custom-call(f32[512,384]{1,0:T(8,128)S(1)} %get-tuple-element.19.refs_0_.stacked, f32[512,384]{1,0:T(8,128)S(1)} %get-tuple-element.21.refs_1_.stacked, f32[1024,384]{1,0:T(8,128)S(1)} %get-tuple-element.22.refs_2_, f32[1024,384]{1,0:T(8,128)S(1)} %get-tuple-element.23.refs_3_), custom_call_target="tpu_custom_call" | custom-call | flops 2415919104 | bytes 5767168 | tf_op jit(solution)/shard_map/pallas_call | solution.py:30
  106.1 0.1 add.22
  106.2 4.0 %collective-permute-start.23 = (f32[256,384]{1,0:T(8,128)S(1)}, f32[256,384]{1,0:T(8,128)S(1)}, u32[]{:S(2)}, u32[]{:S(2)}) collective-permute-start(f32[256,384]{1,0:T(8,128)S(1)} %slice_bitcast_fusion.2), channel_id=1, source_target_pairs={{0,8},{4,12},{8,0},{12,4},{1,9},{5,13},{9,1},{13,5},{2,10},{6,14},... | collective-permute-start | bytes 1179656 | tf_op jit(solution)/shard_map/ppermute | solution.py:46
  110.2 14.0 %collective-permute-done.20 = f32[512,384]{1,0:T(8,128)S(1)} collective-permute-done((f32[512,384]{1,0:T(8,128)S(1)}, f32[512,384]{1,0:T(8,128)S(1)}, u32[]{:S(2)}, u32[]{:S(2)}) %collective-permute-start.20) | collective-permute-done | bytes 786464 | tf_op jit(solution)/shard_map/ppermute | solution.py:46
  124.3 0.1 add.20
  124.4 0.1 collective-permute-start.21
  124.5 0.1 add.18
  124.7 1.2 collective-permute-start.19
  126.0 20.2 %collective-permute-done.21 = f32[256,384]{1,0:T(8,128)S(1)} collective-permute-done((f32[256,384]{1,0:T(8,128)S(1)}, f32[256,384]{1,0:T(8,128)S(1)}, u32[]{:S(2)}, u32[]{:S(2)}) %collective-permute-start.21) | collective-permute-done | bytes 393248 | tf_op jit(solution)/shard_map/ppermute | solution.py:46
  146.3 0.7 pad_maximum_fusion.2
  147.0 0.8 pad_maximum_fusion
  147.8 0.9 fusion.1
  (42 shorter events, 0.3 us)
Async XLA Ops:
  0.6 53.6 %copy-start = (f32[1,128,1024]{2,1,0:T(8,128)S(1)}, f32[1,128,1024]{2,1,0:T(8,128)}, u32[]{:S(2)}) copy-start(f32[1,128,1024]{2,1,0:T(8,128)} %param.7) | copy-start | bytes 1572868
  0.6 15.1 %collective-permute-start.1 = (f32[128,1024]{1,0:T(8,128)}, f32[128,1024]{1,0:T(8,128)S(1)}, u32[]{:S(2)}, u32[]{:S(2)}) collective-permute-start(f32[128,1024]{1,0:T(8,128)} %bitcast.31), channel_id=1, source_target_pairs={{0,2},{1,3},{2,0},{3,1},{4,6},{5,7},{6,4},{7,5},{8,10},{9,11},{10,... | collective-permute-start | bytes 1572872 | tf_op jit(solution)/shard_map/ppermute | solution.py:46
  3.6 47.7 %collective-permute-start = (f32[128,1024]{1,0:T(8,128)}, f32[128,1024]{1,0:T(8,128)S(1)}, u32[]{:S(2)}, u32[]{:S(2)}) collective-permute-start(f32[128,1024]{1,0:T(8,128)} %bitcast.32), channel_id=1, source_target_pairs={{0,1},{1,0},{2,3},{3,2},{4,5},{5,4},{6,7},{7,6},{8,9},{9,8},{10,11... | collective-permute-start | bytes 1572872 | tf_op jit(solution)/shard_map/ppermute | solution.py:46
  15.8 36.1 %collective-permute-start.2 = (f32[128,1024]{1,0:T(8,128)S(1)}, f32[128,1024]{1,0:T(8,128)S(1)}, u32[]{:S(2)}, u32[]{:S(2)}) collective-permute-start(f32[128,1024]{1,0:T(8,128)S(1)} %collective-permute-done.1.refs_2_), channel_id=1, source_target_pairs={{0,1},{1,0},{2,3},{3,2},{4,5},{5,4},{6,7},{7,6},{8,9},{9,8},{10,11... | collective-permute-start | bytes 1572872 | tf_op jit(solution)/shard_map/ppermute | solution.py:46
  15.9 4.0 %copy-start.4 = (s32[3]{0:T(128)}, s32[3]{0:T(128)S(1)}, u32[]{:S(2)}) copy-start(s32[3]{0:T(128)S(1)} %pad_add_fusion.info) | copy-start | bytes 40
  15.9 1.0 copy-start.6
  16.9 0.7 copy-start.13
  18.7 0.7 copy-start.14
  19.4 7.3 %collective-permute-start.9 = (f32[128,256]{1,0:T(8,128)S(1)}, f32[128,256]{1,0:T(8,128)S(1)}, u32[]{:S(2)}, u32[]{:S(2)}) collective-permute-start(f32[128,256]{1,0:T(8,128)S(1)} %get-tuple-element.16), channel_id=1, source_target_pairs={{0,1},{1,0},{2,3},{3,2},{4,5},{5,4},{6,7},{7,6},{8,9},{9,8},{10,11... | collective-permute-start | bytes 393224 | tf_op jit(solution)/shard_map/ppermute | solution.py:46
  22.3 16.0 %collective-permute-start.14 = (f32[128,384]{1,0:T(8,128)}, f32[128,384]{1,0:T(8,128)S(1)}, u32[]{:S(2)}, u32[]{:S(2)}) collective-permute-start(f32[128,384]{1,0:T(8,128)} %get-tuple-element.20), channel_id=1, source_target_pairs={{0,8},{4,12},{8,0},{12,4},{1,9},{5,13},{9,1},{13,5},{2,10},{6,14},... | collective-permute-start | bytes 589832 | tf_op jit(solution)/shard_map/ppermute | solution.py:46
  25.2 5.1 %collective-permute-start.10 = (f32[128,256]{1,0:T(8,128)S(1)}, f32[128,256]{1,0:T(8,128)S(1)}, u32[]{:S(2)}, u32[]{:S(2)}) collective-permute-start(f32[128,256]{1,0:T(8,128)S(1)} %get-tuple-element.17), channel_id=1, source_target_pairs={{0,2},{1,3},{2,0},{3,1},{4,6},{5,7},{6,4},{7,5},{8,10},{9,11},{10,... | collective-permute-start | bytes 393224 | tf_op jit(solution)/shard_map/ppermute | solution.py:46
  26.7 0.7 copy-start.7
  27.3 5.8 %collective-permute-start.11 = (f32[128,256]{1,0:T(8,128)S(1)}, f32[128,256]{1,0:T(8,128)S(1)}, u32[]{:S(2)}, u32[]{:S(2)}) collective-permute-start(f32[128,256]{1,0:T(8,128)S(1)} %get-tuple-element.18), channel_id=1, source_target_pairs={{0,3},{1,2},{2,1},{3,0},{4,7},{5,6},{6,5},{7,4},{8,11},{9,10},{10,... | collective-permute-start | bytes 393224 | tf_op jit(solution)/shard_map/ppermute | solution.py:46
  30.3 0.7 copy-start.9
  31.0 12.2 %collective-permute-start.5 = (f32[128,384]{1,0:T(8,128)}, f32[128,384]{1,0:T(8,128)S(1)}, u32[]{:S(2)}, u32[]{:S(2)}) collective-permute-start(f32[128,384]{1,0:T(8,128)} %get-tuple-element.14), channel_id=1, source_target_pairs={{0,8},{4,12},{8,0},{12,4},{1,9},{5,13},{9,1},{13,5},{2,10},{6,14},... | collective-permute-start | bytes 589832 | tf_op jit(solution)/shard_map/ppermute | solution.py:46
  33.1 0.7 copy-start.11
  33.8 11.8 %collective-permute-start.12 = (f32[128,384]{1,0:T(8,128)}, f32[128,384]{1,0:T(8,128)S(1)}, u32[]{:S(2)}, u32[]{:S(2)}) collective-permute-start(f32[128,384]{1,0:T(8,128)} %get-tuple-element.20), channel_id=1, source_target_pairs={{0,4},{4,0},{8,12},{12,8},{1,5},{5,1},{9,13},{13,9},{2,6},{6,2},{1... | collective-permute-start | bytes 589832 | tf_op jit(solution)/shard_map/ppermute | solution.py:46
  38.3 11.5 %collective-permute-start.16 = (f32[128,384]{1,0:T(8,128)S(1)}, f32[128,384]{1,0:T(8,128)S(1)}, u32[]{:S(2)}, u32[]{:S(2)}) collective-permute-start(f32[128,384]{1,0:T(8,128)S(1)} %collective-permute-done.14.refs_6_), channel_id=1, source_target_pairs={{0,4},{4,0},{8,12},{12,8},{1,5},{5,1},{9,13},{13,9},{2,6},{6,2},{1... | collective-permute-start | bytes 589832 | tf_op jit(solution)/shard_map/ppermute | solution.py:46
  43.2 11.2 %collective-permute-start.3 = (f32[128,384]{1,0:T(8,128)}, f32[128,384]{1,0:T(8,128)S(1)}, u32[]{:S(2)}, u32[]{:S(2)}) collective-permute-start(f32[128,384]{1,0:T(8,128)} %get-tuple-element.14), channel_id=1, source_target_pairs={{0,4},{4,0},{8,12},{12,8},{1,5},{5,1},{9,13},{13,9},{2,6},{6,2},{1... | collective-permute-start | bytes 589832 | tf_op jit(solution)/shard_map/ppermute | solution.py:46
  45.6 12.1 %collective-permute-start.7 = (f32[128,384]{1,0:T(8,128)S(1)}, f32[128,384]{1,0:T(8,128)S(1)}, u32[]{:S(2)}, u32[]{:S(2)}) collective-permute-start(f32[128,384]{1,0:T(8,128)S(1)} %collective-permute-done.5.refs_6_), channel_id=1, source_target_pairs={{0,4},{4,0},{8,12},{12,8},{1,5},{5,1},{9,13},{13,9},{2,6},{6,2},{1... | collective-permute-start | bytes 589832 | tf_op jit(solution)/shard_map/ppermute | solution.py:46
  49.8 9.5 %collective-permute-start.13 = (f32[128,384]{1,0:T(8,128)S(1)}, f32[128,384]{1,0:T(8,128)S(1)}, u32[]{:S(2)}, u32[]{:S(2)}) collective-permute-start(f32[128,384]{1,0:T(8,128)S(1)} %collective-permute-done.12.refs_4_), channel_id=1, source_target_pairs={{0,16},{16,0},{1,17},{17,1},{2,18},{18,2},{3,19},{19,3},{4,20},{20... | collective-permute-start | bytes 589832 | tf_op jit(solution)/shard_map/ppermute | solution.py:46
  51.4 10.6 %collective-permute-start.15 = (f32[128,384]{1,0:T(8,128)S(1)}, f32[128,384]{1,0:T(8,128)}, u32[]{:S(2)}, u32[]{:S(2)}) collective-permute-start(f32[128,384]{1,0:T(8,128)S(1)} %collective-permute-done.14.refs_6_), channel_id=1, source_target_pairs={{0,16},{16,0},{1,17},{17,1},{2,18},{18,2},{3,19},{19,3},{4,20},{20... | collective-permute-start | bytes 589832 | tf_op jit(solution)/shard_map/ppermute | solution.py:46
  51.9 14.3 %collective-permute-start.17 = (f32[128,384]{1,0:T(8,128)S(1)}, f32[128,384]{1,0:T(8,128)}, u32[]{:S(2)}, u32[]{:S(2)}) collective-permute-start(f32[128,384]{1,0:T(8,128)S(1)} %collective-permute-done.16.refs_8_), channel_id=1, source_target_pairs={{0,16},{16,0},{1,17},{17,1},{2,18},{18,2},{3,19},{19,3},{4,20},{20... | collective-permute-start | bytes 589832 | tf_op jit(solution)/shard_map/ppermute | solution.py:46
  54.2 12.0 %copy-start.1 = (f32[256,256]{1,0:T(8,128)S(1)}, f32[256,256]{1,0:T(8,128)}, u32[]{:S(2)}) copy-start(f32[256,256]{1,0:T(8,128)} %refs_1_.5) | copy-start | bytes 786436
  54.2 12.0 %copy-start.2 = (f32[256,256]{1,0:T(8,128)S(1)}, f32[256,256]{1,0:T(8,128)}, u32[]{:S(2)}) copy-start(f32[256,256]{1,0:T(8,128)} %refs_2_.5) | copy-start | bytes 786436
  54.2 12.0 %copy-start.3 = (f32[256,256]{1,0:T(8,128)S(1)}, f32[256,256]{1,0:T(8,128)}, u32[]{:S(2)}) copy-start(f32[256,256]{1,0:T(8,128)} %refs_3_.3) | copy-start | bytes 786436
  54.2 12.0 %copy-start.5 = (s32[3]{0:T(128)S(1)}, s32[3]{0:T(128)}, u32[]{:S(2)}) copy-start(s32[3]{0:T(128)} %copy-done.4) | copy-start | bytes 40
  54.2 12.0 %copy-start.8 = (f32[128,256]{1,0:T(8,128)S(1)}, f32[128,256]{1,0:T(8,128)}, u32[]{:S(2)}) copy-start(f32[128,256]{1,0:T(8,128)} %copy-done.7) | copy-start | bytes 393220
  54.2 12.0 %copy-start.10 = (f32[128,256]{1,0:T(8,128)S(1)}, f32[128,256]{1,0:T(8,128)}, u32[]{:S(2)}) copy-start(f32[128,256]{1,0:T(8,128)} %copy-done.9) | copy-start | bytes 393220
  54.2 12.0 %copy-start.12 = (f32[128,256]{1,0:T(8,128)S(1)}, f32[128,256]{1,0:T(8,128)}, u32[]{:S(2)}) copy-start(f32[128,256]{1,0:T(8,128)} %copy-done.11) | copy-start | bytes 393220
  54.2 12.0 %copy-start.15 = (f32[128,256]{1,0:T(8,128)S(1)}, f32[128,256]{1,0:T(8,128)}, u32[]{:S(2)}) copy-start(f32[128,256]{1,0:T(8,128)} %copy-done.14) | copy-start | bytes 393220
  54.4 24.9 %collective-permute-start.6 = (f32[128,384]{1,0:T(8,128)S(1)}, f32[128,384]{1,0:T(8,128)S(1)}, u32[]{:S(2)}, u32[]{:S(2)}) collective-permute-start(f32[128,384]{1,0:T(8,128)S(1)} %collective-permute-done.5.refs_6_), channel_id=1, source_target_pairs={{0,16},{16,0},{1,17},{17,1},{2,18},{18,2},{3,19},{19,3},{4,20},{20... | collective-permute-start | bytes 589832 | tf_op jit(solution)/shard_map/ppermute | solution.py:46
  57.7 21.6 %collective-permute-start.4 = (f32[128,384]{1,0:T(8,128)S(1)}, f32[128,384]{1,0:T(8,128)S(1)}, u32[]{:S(2)}, u32[]{:S(2)}) collective-permute-start(f32[128,384]{1,0:T(8,128)S(1)} %collective-permute-done.3.refs_4_), channel_id=1, source_target_pairs={{0,16},{16,0},{1,17},{17,1},{2,18},{18,2},{3,19},{19,3},{4,20},{20... | collective-permute-start | bytes 589832 | tf_op jit(solution)/shard_map/ppermute | solution.py:46
  59.3 20.1 %collective-permute-start.8 = (f32[128,384]{1,0:T(8,128)S(1)}, f32[128,384]{1,0:T(8,128)S(1)}, u32[]{:S(2)}, u32[]{:S(2)}) collective-permute-start(f32[128,384]{1,0:T(8,128)S(1)} %collective-permute-done.7.refs_8_), channel_id=1, source_target_pairs={{0,16},{16,0},{1,17},{17,1},{2,18},{18,2},{3,19},{19,3},{4,20},{20... | collective-permute-start | bytes 589832 | tf_op jit(solution)/shard_map/ppermute | solution.py:46
  79.3 26.8 %collective-permute-start.22 = (f32[512,384]{1,0:T(8,128)S(1)}, f32[512,384]{1,0:T(8,128)S(1)}, u32[]{:S(2)}, u32[]{:S(2)}) collective-permute-start(f32[512,384]{1,0:T(8,128)S(1)} %shard_map.112), channel_id=1, source_target_pairs={{0,4},{4,0},{8,12},{12,8},{1,5},{5,1},{9,13},{13,9},{2,6},{6,2},{1... | collective-permute-start | bytes 2359304 | tf_op jit(solution)/shard_map/ppermute | solution.py:46
  93.0 31.4 %collective-permute-start.18 = (f32[256,1024]{1,0:T(8,128)S(1)}, f32[256,1024]{1,0:T(8,128)S(1)}, u32[]{:S(2)}, u32[]{:S(2)}) collective-permute-start(f32[256,1024]{1,0:T(8,128)S(1)} %shard_map.108), channel_id=1, source_target_pairs={{0,1},{1,0},{2,3},{3,2},{4,5},{5,4},{6,7},{7,6},{8,9},{9,8},{10,11... | collective-permute-start | bytes 3145736 | tf_op jit(solution)/shard_map/ppermute | solution.py:46
  95.5 28.7 %collective-permute-start.20 = (f32[512,384]{1,0:T(8,128)S(1)}, f32[512,384]{1,0:T(8,128)S(1)}, u32[]{:S(2)}, u32[]{:S(2)}) collective-permute-start(f32[512,384]{1,0:T(8,128)S(1)} %shard_map.110), channel_id=1, source_target_pairs={{0,4},{4,0},{8,12},{12,8},{1,5},{5,1},{9,13},{13,9},{2,6},{6,2},{1... | collective-permute-start | bytes 2359304 | tf_op jit(solution)/shard_map/ppermute | solution.py:46
  106.2 19.7 %collective-permute-start.23 = (f32[256,384]{1,0:T(8,128)S(1)}, f32[256,384]{1,0:T(8,128)S(1)}, u32[]{:S(2)}, u32[]{:S(2)}) collective-permute-start(f32[256,384]{1,0:T(8,128)S(1)} %slice_bitcast_fusion.2), channel_id=1, source_target_pairs={{0,8},{4,12},{8,0},{12,4},{1,9},{5,13},{9,1},{13,5},{2,10},{6,14},... | collective-permute-start | bytes 1179656 | tf_op jit(solution)/shard_map/ppermute | solution.py:46
  124.4 21.8 %collective-permute-start.21 = (f32[256,384]{1,0:T(8,128)S(1)}, f32[256,384]{1,0:T(8,128)S(1)}, u32[]{:S(2)}, u32[]{:S(2)}) collective-permute-start(f32[256,384]{1,0:T(8,128)S(1)} %slice_bitcast_fusion.4), channel_id=1, source_target_pairs={{0,8},{4,12},{8,0},{12,4},{1,9},{5,13},{9,1},{13,5},{2,10},{6,14},... | collective-permute-start | bytes 1179656 | tf_op jit(solution)/shard_map/ppermute | solution.py:46
  124.7 23.2 %collective-permute-start.19 = (f32[128,1024]{1,0:T(8,128)S(1)}, f32[128,1024]{1,0:T(8,128)S(1)}, u32[]{:S(2)}, u32[]{:S(2)}) collective-permute-start(f32[128,1024]{1,0:T(8,128)S(1)} %slice_bitcast_fusion), channel_id=1, source_target_pairs={{0,2},{1,3},{2,0},{3,1},{4,6},{5,7},{6,4},{7,5},{8,10},{9,11},{10,... | collective-permute-start | bytes 1572872 | tf_op jit(solution)/shard_map/ppermute | solution.py:46
where the time goes:
time: 149 us
  waiting for transfers between devices  71.7 us (48%)
  Pallas kernels  41.2 us (28%)
  starting transfers between devices  26.7 us (18%)
  local copies, waits for them, and re-layouts  5.27 us (4%)
  other arithmetic  2.9 us (2%)
    ppermute x24, waiting for transfers between devices, swap(): return lax.ppermute(value, axis, [(i, i ^ step) for i in range(size)])  71.7 us
    pallas_call x10, Pallas kernels, local_call(): pl.pallas_call(body, out_shape=outs, in_specs=[smem] * len(scalars) + [vm...  38.7 us
    ppermute x24, starting transfers between devices, swap(): return lax.ppermute(value, axis, [(i, i ^ step) for i in range(size)])  26.7 us
    unnamed x33, local copies, waits for them, and re-layouts  5.12 us
  transfers between devices with their start and end apart: 24, of which 12 were waited for; matrix products, arithmetic and copies ran while one was open for 2% of the time, Pallas kernels for 28%

commit v1 on v0

--- a/solution.py
+++ b/solution.py
@@ -26,14 +26,13 @@
 def local_call(body, outs, args, scalars=(), scratch=(), flops=0, vmem_mib=24):
     vmem = pl.BlockSpec(memory_space=pltpu.VMEM)
     smem = pl.BlockSpec(memory_space=pltpu.SMEM)
-    moved = sum(4 * a.size for a in args) + sum(4 * o.size for o in outs)
     return pl.pallas_call(
         body,
         out_shape=outs,
         in_specs=[smem] * len(scalars) + [vmem] * len(args),
         out_specs=[vmem] * len(outs),
         scratch_shapes=scratch,
-        cost_estimate=pl.CostEstimate(flops=flops, bytes_accessed=moved, transcendentals=0),
+        cost_estimate=pl.CostEstimate(flops=flops, bytes_accessed=flops // 256, transcendentals=0),
         compiler_params=pltpu.CompilerParams(vmem_limit_bytes=vmem_mib << 20),
     )(*scalars, *args)
 
@@ -44,6 +43,10 @@
 
 def swap(value, axis, size, step):
     return lax.ppermute(value, axis, [(i, i ^ step) for i in range(size)])
+
+
+def after(value, *others):
+    return lax.optimization_barrier((value, *others))[0]
 
 
 def halves_body(chunks, wq, wk, wv, *outs):
@@ -174,15 +177,33 @@
     out[...] = total
 
 
-def scatter_halving(send, keep, axis, size, rows):
-    step = 1
+def halve_body(rows, keep, got, send, kept):
+    for j in range(keep.shape[0] // rows):
+        out = send if j % 2 else kept
+        place = slice(j // 2 * rows, (j // 2 + 1) * rows)
+        here = slice(j * rows, (j + 1) * rows)
+        out[place, :] = keep[here, :] + got[here, :]
+
+
+def scatter_halving(send, keep, axis, size, rows, wait=()):
+    step, first = 1, None
     while True:
         got = swap(send, axis, size, step)
         step *= 2
         if step == size:
-            return keep, got
-        total = (keep + got).reshape(-1, 2, rows, keep.shape[1])
-        send, keep = total[:, 1].reshape(-1, keep.shape[1]), total[:, 0].reshape(-1, keep.shape[1])
+            return keep, got, first
+        got = after(got, *wait) if wait else got
+        shape = shaped(keep.shape[0] // 2, keep.shape[1])
+        send, keep = local_call(functools.partial(halve_body, rows), [shape] * 2, [keep, got])
+        first = keep if first is None else first
+
+
+def join_body(chunks, *refs):
+    for c in range(chunks):
+        for i in range(3):
+            part = slice(i * LANES, (i + 1) * LANES)
+            term = refs[2 * c][:, part] + refs[2 * c + 1][:, part]
+            refs[2 * chunks + i][:, c * LANES : (c + 1) * LANES] = term
 
 
 def per_device(sizes, node_features, sensor_adjoint, sensor_node, neighbours, *weights):
@@ -197,11 +218,35 @@
     info = jnp.stack([z, y, t]).astype(jnp.int32)
     direct = rows_here % LANES == 0 and rows_here % (8 * grp) == 0 and wa > 1
 
+    first = []
+    if direct:
+        half = rows_here // grp
+        halves = weight_halves(info, *weights, half, chunks)
+        gathered, crossed, last = [], [], None
+        for c in range(chunks):
+            mine = {0: halves[c] if last is None else after(halves[c], last)}
+            step = wa
+            while step > 1:
+                step //= 2
+                mine.update({r | step: swap(v, "wa", wa, step) for r, v in list(mine.items())})
+            last = mine[wa // 2]
+            gathered.append(mine)
+            crossed.append(
+                {(r, g): swap(mine[r], "grp", grp, g) for g in range(1, grp) for r in range(1, wa)}
+            )
+
+        first = [gathered[0][1]]
+
     held = {0: hour_rows}
     step = ta
     while step > 1:
         step //= 2
-        held.update({r | step: swap(v, "ta", ta, step) for r, v in list(held.items())})
+        held.update(
+            {
+                r | step: swap(after(v, *first) if r else v, "ta", ta, step)
+                for r, v in list(held.items())
+            }
+        )
     inputs = local_call(
         functools.partial(stack_body, ta), [shaped(nodes, width)], [held[r] for r in range(ta)]
     )[0]
@@ -214,30 +259,27 @@
         scratch=[pltpu.VMEM((nodes_here, width), F32)],
         flops=12 * nodes_here * nodes_here * width,
     )
-    adjoints = [blocks_out[0]] + [swap(blocks_out[r], "ta", ta, r) for r in range(1, ta)]
-
-    stacked, panels, owned = [], [], []
-    if direct:
-        half = rows_here // grp
-        halves = weight_halves(info, *weights, half, chunks)
+    adjoints = [blocks_out[0]] + [
+        swap(after(blocks_out[r], held[ta // 2]), "ta", ta, r) for r in range(1, ta)
+    ]
+
+    stacked, panels, owned, firsts = [], [], [], []
     for c in range(chunks):
+        turn = after(info, stacked[-1]) if stacked else info
+        more = direct and c + 1 < chunks
+        if more:
+            turn = after(turn, *[gathered[c + 1][r] for r in range(1, wa)])
         proj_flops = 12 * nodes * width * 3 * LANES + 60 * 2 * nodes * 4 * BLOCK * LANES
         scratch = [pltpu.VMEM((nodes, 3 * LANES), F32)]
         if direct:
-            mine = {0: halves[c]}
-            step = wa
-            while step > 1:
-                step //= 2
-                mine.update({r | step: swap(v, "wa", wa, step) for r, v in list(mine.items())})
-            pieces = {(r, 0): mine[r] for r in range(1, wa)}
-            for g in range(1, grp):
-                pieces.update({(r, g): swap(mine[r], "grp", grp, g) for r in range(1, wa)})
+            pieces = {(r, 0): gathered[c][r] for r in range(1, wa)}
+            pieces.update(crossed[c])
             names = sorted(pieces)
             dqkv, panel = local_call(
                 functools.partial(attention_body, c, blocks, names),
                 [shaped(nodes, 3 * LANES), shaped(width, 3 * LANES)],
                 [inputs, *weights, *[pieces[n] for n in names], *adjoints],
-                scalars=[info, neighbours],
+                scalars=[turn, neighbours],
                 scratch=scratch,
                 flops=proj_flops,
             )
@@ -249,25 +291,26 @@
                 functools.partial(attention_panel_body, c, blocks),
                 [shaped(nodes, 3 * LANES)],
                 [inputs, panel, *adjoints],
-                scalars=[info, neighbours],
+                scalars=[turn, neighbours],
                 scratch=scratch,
                 flops=proj_flops,
             )[0]
         stacked.append(dqkv)
         panels.append(panel)
         if direct:
+            later = after(info, dqkv, *crossed[c + 1].values()) if more else info
             sends = [
                 local_call(
                     functools.partial(weight_grad_body, range(odd, wa, 2), rows_here),
                     [shaped(rows_here * wa // 2, 3 * LANES)],
                     [inputs, dqkv],
-                    scalars=[info],
-                    flops=12 * nodes * rows_here * wa // 2 * 3 * LANES,
+                    scalars=[later],
                 )[0]
                 for odd in (1, 0)
             ]
-            kept, got = scatter_halving(*sends, "wa", wa, rows_here)
-            owned.append(kept + got)
+            kept, got, early = scatter_halving(*sends, "wa", wa, rows_here, owned[-1:])
+            owned += [kept, got]
+            firsts = (firsts or [early]) if more else [*firsts, sends[0]]
         else:
             full = local_call(
                 whole_grad_body,
@@ -281,16 +324,20 @@
         local_call(
             functools.partial(back_body, range(odd, ta, 2), chunks),
             [shaped(nodes // 2, width)],
-            [*stacked, *panels],
-            flops=12 * nodes // 2 * width * columns * 3,
+            [*stacked, *[after(p, *firsts) for p in panels]],
         )[0]
         for odd in (1, 0)
     ]
-    kept, got = scatter_halving(*backs, "ta", ta, nodes_here)
-    grads = [
-        jnp.concatenate([o[:, i * LANES : (i + 1) * LANES] for o in owned], axis=1)
-        for i in range(3)
-    ]
+    kept, got, _ = scatter_halving(*backs, "ta", ta, nodes_here)
+    if direct:
+        grads = local_call(
+            functools.partial(join_body, chunks), [shaped(rows_here, columns)] * 3, owned
+        )
+    else:
+        grads = [
+            jnp.concatenate([o[:, i * LANES : (i + 1) * LANES] for o in owned], axis=1)
+            for i in range(3)
+        ]
     return ((kept + got)[None], *grads)
 
 

time: 149 us -> 138 us (0.926)
  waiting for transfers between devices: 71.7 us -> 63.3 us
  Pallas kernels: 41.2 us -> 43.8 us
  local copies, waits for them, and re-layouts: 5.27 us -> 3.14 us
  starting transfers between devices: 26.7 us -> 25.1 us
    ppermute x24, waiting for transfers between devices: 71.7 us -> 63.3 us  [swap(): return lax.ppermute(value, axis, [(i, i ^ step) for i in range(size)])]
    pallas_call x10 -> x14, Pallas kernels: 38.7 us -> 41.3 us  [local_call(): pl.pallas_call(body, out_shape=outs, in_specs=[smem] * len(scalars) + [vm...]
    unnamed x33 -> x23, local copies, waits for them, and re-layouts: 5.12 us -> 3.14 us
    ppermute x24, starting transfers between devices: 26.7 us -> 25.1 us  [swap(): return lax.ppermute(value, axis, [(i, i ^ step) for i in range(size)])]
    concatenate x2 -> x0, other arithmetic: 1.54 us -> none  [per_device(): jnp.concatenate([o[:, i * LANES:(i + 1) * LANES] for o in owned], axis=1)]
  transfers between devices with their start and end apart: 24 -> 24, of which waited for: 12 -> 11; matrix products, arithmetic and copies ran while one was open for 2% -> 1% of each run, Pallas kernels for 28% -> 27%
where the time goes in v1:
time: 138 us
  waiting for transfers between devices  63.3 us (46%)
  Pallas kernels  43.8 us (32%)
  starting transfers between devices  25.1 us (18%)
  local copies, waits for them, and re-layouts  3.14 us (2%)
  other arithmetic  1.51 us (1%)
    ppermute x24, waiting for transfers between devices, swap(): return lax.ppermute(value, axis, [(i, i ^ step) for i in range(size)])  63.3 us
    pallas_call x14, Pallas kernels, local_call(): pl.pallas_call(body, out_shape=outs, in_specs=[smem] * len(scalars) + [vm...  41.3 us
    ppermute x24, starting transfers between devices, swap(): return lax.ppermute(value, axis, [(i, i ^ step) for i in range(size)])  25.1 us
    unnamed x23, local copies, waits for them, and re-layouts  3.14 us
  transfers between devices with their start and end apart: 24, of which 11 were waited for; matrix products, arithmetic and copies ran while one was open for 1% of the time, Pallas kernels for 27%

profile of v1, /device:TPU:0, one launch (start us, length us, event | category | flops | bytes accessed | tf_op | source)
XLA Modules:
  0.0 137.7 jit_solution(3288469860104201158)
XLA Ops:
  0.6 0.0 copy-start
  0.7 3.0 %collective-permute-start.5 = (f32[128,1024]{1,0:T(8,128)}, f32[128,1024]{1,0:T(8,128)S(1)}, u32[]{:S(2)}, u32[]{:S(2)}) collective-permute-start(f32[128,1024]{1,0:T(8,128)} %bitcast.8), channel_id=1, source_target_pairs={{0,2},{1,3},{2,0},{3,1},{4,6},{5,7},{6,4},{7,5},{8,10},{9,11},{10,... | collective-permute-start | bytes 1572872 | tf_op jit(solution)/shard_map/ppermute | solution.py:45
  3.7 0.6 pad_add_fusion.info
  4.3 2.4 %shard_map.102 = (f32[128,384]{1,0:T(8,128)}, f32[128,384]{1,0:T(8,128)}) custom-call(s32[3]{0:T(128)} %pad_add_fusion.info, f32[256,256]{1,0:T(8,128)} %refs_1_.5, f32[256,256]{1,0:T(8,128)} %refs_2_.5, f32[256,256]{1,0:T(8,128)} %refs_3_.3), custom_call_target="tpu_custom_call" | custom-call | tf_op jit(solution)/shard_map/pallas_call | solution.py:64
  6.8 1.6 %collective-permute-start.6 = (f32[128,384]{1,0:T(8,128)}, f32[128,384]{1,0:T(8,128)S(1)}, u32[]{:S(2)}, u32[]{:S(2)}) collective-permute-start(f32[128,384]{1,0:T(8,128)} %get-tuple-element.35), channel_id=1, source_target_pairs={{0,4},{4,0},{8,12},{12,8},{1,5},{5,1},{9,13},{13,9},{2,6},{6,2},{1... | collective-permute-start | bytes 589832 | tf_op jit(solution)/shard_map/ppermute | solution.py:45
  8.3 2.6 %collective-permute-start = (f32[128,384]{1,0:T(8,128)}, f32[128,384]{1,0:T(8,128)S(1)}, u32[]{:S(2)}, u32[]{:S(2)}) collective-permute-start(f32[128,384]{1,0:T(8,128)} %get-tuple-element.35), channel_id=1, source_target_pairs={{0,8},{4,12},{8,0},{12,4},{1,9},{5,13},{9,1},{13,5},{2,10},{6,14},... | collective-permute-start | bytes 589832 | tf_op jit(solution)/shard_map/ppermute | solution.py:45
  10.9 6.5 %collective-permute-done.6.refs_4_ = f32[128,384]{1,0:T(8,128)S(1)} collective-permute-done((f32[128,384]{1,0:T(8,128)}, f32[128,384]{1,0:T(8,128)S(1)}, u32[]{:S(2)}, u32[]{:S(2)}) %collective-permute-start.6) | collective-permute-done | bytes 196640 | tf_op jit(solution)/shard_map/ppermute | solution.py:45
  17.4 1.5 %collective-permute-start.8 = (f32[128,384]{1,0:T(8,128)S(1)}, f32[128,384]{1,0:T(8,128)S(1)}, u32[]{:S(2)}, u32[]{:S(2)}) collective-permute-start(f32[128,384]{1,0:T(8,128)S(1)} %collective-permute-done.6.refs_4_), channel_id=1, source_target_pairs={{0,16},{16,0},{1,17},{17,1},{2,18},{18,2},{3,19},{19,3},{4,20},{20... | collective-permute-start | bytes 589832 | tf_op jit(solution)/shard_map/ppermute | solution.py:45
  18.9 0.9 collective-permute-done.refs_6_
  19.8 0.4 collective-permute-start.2
  20.2 2.7 %collective-permute-start.1 = (f32[128,384]{1,0:T(8,128)}, f32[128,384]{1,0:T(8,128)S(1)}, u32[]{:S(2)}, u32[]{:S(2)}) collective-permute-start(f32[128,384]{1,0:T(8,128)} %get-tuple-element.36), channel_id=1, source_target_pairs={{0,4},{4,0},{8,12},{12,8},{1,5},{5,1},{9,13},{13,9},{2,6},{6,2},{1... | collective-permute-start | bytes 589832 | tf_op jit(solution)/shard_map/ppermute | solution.py:45
  22.8 1.9 %collective-permute-done.8.refs_5_ = f32[128,384]{1,0:T(8,128)S(1)} collective-permute-done((f32[128,384]{1,0:T(8,128)S(1)}, f32[128,384]{1,0:T(8,128)S(1)}, u32[]{:S(2)}, u32[]{:S(2)}) %collective-permute-start.8) | collective-permute-done | bytes 196640 | tf_op jit(solution)/shard_map/ppermute | solution.py:45
  24.7 0.2 collective-permute-start.10
  24.9 6.3 %collective-permute-done.2.refs_6_ = f32[128,384]{1,0:T(8,128)S(1)} collective-permute-done((f32[128,384]{1,0:T(8,128)}, f32[128,384]{1,0:T(8,128)S(1)}, u32[]{:S(2)}, u32[]{:S(2)}) %collective-permute-start.2) | collective-permute-done | bytes 196640 | tf_op jit(solution)/shard_map/ppermute | solution.py:45
  31.3 0.0 collective-permute-start.3
  31.3 1.2 collective-permute-done.1.refs_4_
  32.5 0.2 collective-permute-start.9
  32.7 4.0 %collective-permute-done.10.refs_8_ = f32[128,384]{1,0:T(8,128)S(1)} collective-permute-done((f32[128,384]{1,0:T(8,128)S(1)}, f32[128,384]{1,0:T(8,128)S(1)}, u32[]{:S(2)}, u32[]{:S(2)}) %collective-permute-start.10) | collective-permute-done | bytes 196640 | tf_op jit(solution)/shard_map/ppermute | solution.py:45
  36.7 0.2 collective-permute-start.11
  36.9 0.7 copy-done.4
  37.6 1.0 copy-done.6
  38.6 0.7 copy-done.7
  39.3 1.9 %shard_map.104 = (f32[128,256]{1,0:T(8,128)S(1)}, f32[128,256]{1,0:T(8,128)}, f32[128,256]{1,0:T(8,128)}, f32[128,256]{1,0:T(8,128)}) custom-call(s32[3]{0:T(128)S(1)} %copy-done.4, s32[1,128]{1,0:T(1,128)S(1)} %bitcast.12, f32[128,1024]{1,0:T(8,128)S(1)} %bitcast.11), custom_call_target="tpu_custom_call" | custom-call | flops 201326592 | bytes 786432 | tf_op jit(solution)/shard_map/pallas_call | solution.py:29
  41.2 0.7 copy-done.8
  41.8 0.0 collective-permute-start.12
  41.8 0.0 collective-permute-done.3.refs_8_
  41.8 0.8 collective-permute-start.13
  42.7 1.0 collective-permute-start.14
  43.7 0.1 copy.11.neighbours
  43.8 0.0 copy-start.9
  43.8 0.1 shard_map.103.refs_0_.x
  44.0 1.9 %collective-permute-start.16 = (f32[128,384]{1,0:T(8,128)S(1)}, f32[128,384]{1,0:T(8,128)S(1)}, u32[]{:S(2)}, u32[]{:S(2)}) collective-permute-start(f32[128,384]{1,0:T(8,128)S(1)} %collective-permute-done.2.refs_6_), channel_id=1, source_target_pairs={{0,16},{16,0},{1,17},{17,1},{2,18},{18,2},{3,19},{19,3},{4,20},{20... | collective-permute-start | bytes 589832 | tf_op jit(solution)/shard_map/ppermute | solution.py:45
  45.8 0.0 collective-permute-done.11.refs_9_
  45.9 0.2 collective-permute-start.15
  46.1 1.8 %collective-permute-start.17 = (f32[128,384]{1,0:T(8,128)S(1)}, f32[128,384]{1,0:T(8,128)S(1)}, u32[]{:S(2)}, u32[]{:S(2)}) collective-permute-start(f32[128,384]{1,0:T(8,128)S(1)} %collective-permute-done.3.refs_8_), channel_id=1, source_target_pairs={{0,16},{16,0},{1,17},{17,1},{2,18},{18,2},{3,19},{19,3},{4,20},{20... | collective-permute-start | bytes 589832 | tf_op jit(solution)/shard_map/ppermute | solution.py:45
  47.9 0.6 collective-permute-done.13.refs_12_
  48.5 1.9 %collective-permute-done.14.refs_13_ = f32[128,256]{1,0:T(8,128)} collective-permute-done((f32[128,256]{1,0:T(8,128)}, f32[128,256]{1,0:T(8,128)}, u32[]{:S(2)}, u32[]{:S(2)}) %collective-permute-start.14) | collective-permute-done | bytes 131104 | tf_op jit(solution)/shard_map/ppermute | solution.py:45
  50.4 10.5 %shard_map.105 = (f32[512,384]{1,0:T(8,128)S(1)}, f32[1024,384]{1,0:T(8,128)S(1)}) custom-call(s32[3]{0:T(128)S(1)} %copy-done.5, s32[4,2]{1,0:T(4,128)S(1)} %copy.11.neighbours, f32[512,1024]{1,0:T(8,128)S(1)} %shard_map.103.refs_0_.x, f32[256,256]{1,0:T(8,128)S(1)} %copy-done.1, f32[256,256]{1,0:T(8,128)S(1)} %copy-done.2, f32[256,256]{1,0:T(8,128)S(1)} %copy-done.3, ...), custom_call_target="tpu_custom_call" | custom-call | flops 6442450944 | bytes 25165824 | tf_op jit(solution)/shard_map/pallas_call | solution.py:29
  61.0 0.0 collective-permute-done.16.refs_7_
  61.0 0.0 collective-permute-done.17.refs_9_
  61.0 2.6 %shard_map.108 = f32[512,384]{1,0:T(8,128)S(1)} custom-call(s32[3]{0:T(128)S(1)} %copy-done.5, f32[512,1024]{1,0:T(8,128)S(1)} %shard_map.103.refs_0_.x, f32[512,384]{1,0:T(8,128)S(1)} %get-tuple-element.46.stacked.refs_0_), custom_call_target="tpu_custom_call" | custom-call | tf_op jit(solution)/shard_map/pallas_call | solution.py:29
  63.6 1.3 collective-permute-start.18
  64.9 2.4 %shard_map.107.keep = f32[512,384]{1,0:T(8,128)S(1)} custom-call(s32[3]{0:T(128)S(1)} %copy-done.5, f32[512,1024]{1,0:T(8,128)S(1)} %shard_map.103.refs_0_.x, f32[512,384]{1,0:T(8,128)S(1)} %get-tuple-element.46.stacked.refs_0_), custom_call_target="tpu_custom_call" | custom-call | tf_op jit(solution)/shard_map/pallas_call | solution.py:29
  67.4 10.4 %shard_map.106 = (f32[512,384]{1,0:T(8,128)S(1)}, f32[1024,384]{1,0:T(8,128)S(1)}) custom-call(s32[3]{0:T(128)S(1)} %copy-done.5, s32[4,2]{1,0:T(4,128)S(1)} %copy.11.neighbours, f32[512,1024]{1,0:T(8,128)S(1)} %shard_map.103.refs_0_.x, f32[256,256]{1,0:T(8,128)S(1)} %copy-done.1, f32[256,256]{1,0:T(8,128)S(1)} %copy-done.2, f32[256,256]{1,0:T(8,128)S(1)} %copy-done.3, ...), custom_call_target="tpu_custom_call" | custom-call | flops 6442450944 | bytes 25165824 | tf_op jit(solution)/shard_map/pallas_call | solution.py:29
  77.7 2.7 %shard_map.110 = f32[512,384]{1,0:T(8,128)S(1)} custom-call(s32[3]{0:T(128)S(1)} %copy-done.5, f32[512,1024]{1,0:T(8,128)S(1)} %shard_map.103.refs_0_.x, f32[512,384]{1,0:T(8,128)S(1)} %get-tuple-element.48.stacked.refs_1_), custom_call_target="tpu_custom_call" | custom-call | tf_op jit(solution)/shard_map/pallas_call | solution.py:29
  80.4 3.2 %collective-permute-done.18.got = f32[512,384]{1,0:T(8,128)S(1)} collective-permute-done((f32[512,384]{1,0:T(8,128)S(1)}, f32[512,384]{1,0:T(8,128)S(1)}, u32[]{:S(2)}, u32[]{:S(2)}) %collective-permute-start.18) | collective-permute-done | bytes 786464 | tf_op jit(solution)/shard_map/ppermute | solution.py:45
  83.6 0.1 shard_map.109
  83.7 3.5 %shard_map.112 = f32[256,1024]{1,0:T(8,128)S(1)} custom-call(f32[512,384]{1,0:T(8,128)S(1)} %get-tuple-element.46.stacked.refs_0_, f32[512,384]{1,0:T(8,128)S(1)} %get-tuple-element.48.stacked.refs_1_, f32[1024,384]{1,0:T(8,128)S(1)} %get-tuple-element.52.refs_2_, f32[1024,384]{1,0:T(8,128)S(1)} %get-tuple-element.54.refs_3_), custom_call_target="tpu_custom_call" | custom-call | tf_op jit(solution)/shard_map/pallas_call | solution.py:29
  87.3 0.1 collective-permute-start.19
  87.3 1.3 collective-permute-start.22
  88.6 1.1 collective-permute-start.21
  89.7 3.5 %shard_map.111.keep = f32[256,1024]{1,0:T(8,128)S(1)} custom-call(f32[512,384]{1,0:T(8,128)S(1)} %get-tuple-element.46.stacked.refs_0_, f32[512,384]{1,0:T(8,128)S(1)} %get-tuple-element.48.stacked.refs_1_, f32[1024,384]{1,0:T(8,128)S(1)} %get-tuple-element.52.refs_2_, f32[1024,384]{1,0:T(8,128)S(1)} %get-tuple-element.54.refs_3_), custom_call_target="tpu_custom_call" | custom-call | tf_op jit(solution)/shard_map/pallas_call | solution.py:29
  93.2 0.0 collective-permute-done.19.got
  93.3 0.1 shard_map.113
  93.4 1.1 collective-permute-start.20
  94.5 2.4 %shard_map.114.keep = f32[512,384]{1,0:T(8,128)S(1)} custom-call(s32[3]{0:T(128)S(1)} %copy-done.5, f32[512,1024]{1,0:T(8,128)S(1)} %shard_map.103.refs_0_.x, f32[512,384]{1,0:T(8,128)S(1)} %get-tuple-element.48.stacked.refs_1_), custom_call_target="tpu_custom_call" | custom-call | tf_op jit(solution)/shard_map/pallas_call | solution.py:29
  96.9 18.8 %collective-permute-done.22.got = f32[512,384]{1,0:T(8,128)S(1)} collective-permute-done((f32[512,384]{1,0:T(8,128)S(1)}, f32[512,384]{1,0:T(8,128)S(1)}, u32[]{:S(2)}, u32[]{:S(2)}) %collective-permute-start.22) | collective-permute-done | bytes 786464 | tf_op jit(solution)/shard_map/ppermute | solution.py:45
  115.7 0.0 collective-permute-done.21.refs_1_
  115.7 0.1 shard_map.115
  115.8 2.2 %collective-permute-start.23 = (f32[256,384]{1,0:T(8,128)S(1)}, f32[256,384]{1,0:T(8,128)S(1)}, u32[]{:S(2)}, u32[]{:S(2)}) collective-permute-start(f32[256,384]{1,0:T(8,128)S(1)} %get-tuple-element.60), channel_id=1, source_target_pairs={{0,8},{4,12},{8,0},{12,4},{1,9},{5,13},{9,1},{13,5},{2,10},{6,14},... | collective-permute-start | bytes 1179656 | tf_op jit(solution)/shard_map/ppermute | solution.py:45
  118.0 17.9 %collective-permute-done.23.refs_3_ = f32[256,384]{1,0:T(8,128)S(1)} collective-permute-done((f32[256,384]{1,0:T(8,128)S(1)}, f32[256,384]{1,0:T(8,128)S(1)}, u32[]{:S(2)}, u32[]{:S(2)}) %collective-permute-start.23) | collective-permute-done | bytes 393248 | tf_op jit(solution)/shard_map/ppermute | solution.py:45
  135.9 1.0 shard_map.116
  136.8 0.0 collective-permute-done.20
  136.8 0.9 add_bitcast_fusion
  (24 shorter events, 0.1 us)
Async XLA Ops:
  0.6 43.2 %copy-start = (f32[1,128,1024]{2,1,0:T(8,128)S(1)}, f32[1,128,1024]{2,1,0:T(8,128)}, u32[]{:S(2)}) copy-start(f32[1,128,1024]{2,1,0:T(8,128)} %param.7) | copy-start | bytes 1572868
  0.6 43.1 %copy-start.10 = (s32[4,2]{0,1:T(2,128)S(1)}, s32[4,2]{0,1:T(2,128)}, u32[]{:S(2)}) copy-start(s32[4,2]{0,1:T(2,128)} %param.10) | copy-start | bytes 100
  0.7 16.8 %collective-permute-start.5 = (f32[128,1024]{1,0:T(8,128)}, f32[128,1024]{1,0:T(8,128)S(1)}, u32[]{:S(2)}, u32[]{:S(2)}) collective-permute-start(f32[128,1024]{1,0:T(8,128)} %bitcast.8), channel_id=1, source_target_pairs={{0,2},{1,3},{2,0},{3,1},{4,6},{5,7},{6,4},{7,5},{8,10},{9,11},{10,... | collective-permute-start | bytes 1572872 | tf_op jit(solution)/shard_map/ppermute | solution.py:45
  6.8 10.7 %collective-permute-start.6 = (f32[128,384]{1,0:T(8,128)}, f32[128,384]{1,0:T(8,128)S(1)}, u32[]{:S(2)}, u32[]{:S(2)}) collective-permute-start(f32[128,384]{1,0:T(8,128)} %get-tuple-element.35), channel_id=1, source_target_pairs={{0,4},{4,0},{8,12},{12,8},{1,5},{5,1},{9,13},{13,9},{2,6},{6,2},{1... | collective-permute-start | bytes 589832 | tf_op jit(solution)/shard_map/ppermute | solution.py:45
  8.3 11.5 %collective-permute-start = (f32[128,384]{1,0:T(8,128)}, f32[128,384]{1,0:T(8,128)S(1)}, u32[]{:S(2)}, u32[]{:S(2)}) collective-permute-start(f32[128,384]{1,0:T(8,128)} %get-tuple-element.35), channel_id=1, source_target_pairs={{0,8},{4,12},{8,0},{12,4},{1,9},{5,13},{9,1},{13,5},{2,10},{6,14},... | collective-permute-start | bytes 589832 | tf_op jit(solution)/shard_map/ppermute | solution.py:45
  10.9 30.9 %collective-permute-start.4 = (f32[128,1024]{1,0:T(8,128)}, f32[128,1024]{1,0:T(8,128)S(1)}, u32[]{:S(2)}, u32[]{:S(2)}) collective-permute-start(f32[128,1024]{1,0:T(8,128)} %bitcast.9), channel_id=1, source_target_pairs={{0,1},{1,0},{2,3},{3,2},{4,5},{5,4},{6,7},{7,6},{8,9},{9,8},{10,11... | collective-permute-start | bytes 1572872 | tf_op jit(solution)/shard_map/ppermute | solution.py:45
  17.4 25.2 %collective-permute-start.7 = (f32[128,1024]{1,0:T(8,128)S(1)}, f32[128,1024]{1,0:T(8,128)S(1)}, u32[]{:S(2)}, u32[]{:S(2)}) collective-permute-start(f32[128,1024]{1,0:T(8,128)S(1)} %collective-permute-done.5.refs_2_), channel_id=1, source_target_pairs={{0,1},{1,0},{2,3},{3,2},{4,5},{5,4},{6,7},{7,6},{8,9},{9,8},{10,11... | collective-permute-start | bytes 1572872 | tf_op jit(solution)/shard_map/ppermute | solution.py:45
  17.4 7.3 %collective-permute-start.8 = (f32[128,384]{1,0:T(8,128)S(1)}, f32[128,384]{1,0:T(8,128)S(1)}, u32[]{:S(2)}, u32[]{:S(2)}) collective-permute-start(f32[128,384]{1,0:T(8,128)S(1)} %collective-permute-done.6.refs_4_), channel_id=1, source_target_pairs={{0,16},{16,0},{1,17},{17,1},{2,18},{18,2},{3,19},{19,3},{4,20},{20... | collective-permute-start | bytes 589832 | tf_op jit(solution)/shard_map/ppermute | solution.py:45
  19.8 11.5 %collective-permute-start.2 = (f32[128,384]{1,0:T(8,128)}, f32[128,384]{1,0:T(8,128)S(1)}, u32[]{:S(2)}, u32[]{:S(2)}) collective-permute-start(f32[128,384]{1,0:T(8,128)} %get-tuple-element.36), channel_id=1, source_target_pairs={{0,8},{4,12},{8,0},{12,4},{1,9},{5,13},{9,1},{13,5},{2,10},{6,14},... | collective-permute-start | bytes 589832 | tf_op jit(solution)/shard_map/ppermute | solution.py:45
  20.2 12.3 %collective-permute-start.1 = (f32[128,384]{1,0:T(8,128)}, f32[128,384]{1,0:T(8,128)S(1)}, u32[]{:S(2)}, u32[]{:S(2)}) collective-permute-start(f32[128,384]{1,0:T(8,128)} %get-tuple-element.36), channel_id=1, source_target_pairs={{0,4},{4,0},{8,12},{12,8},{1,5},{5,1},{9,13},{13,9},{2,6},{6,2},{1... | collective-permute-start | bytes 589832 | tf_op jit(solution)/shard_map/ppermute | solution.py:45
  24.7 12.0 %collective-permute-start.10 = (f32[128,384]{1,0:T(8,128)S(1)}, f32[128,384]{1,0:T(8,128)S(1)}, u32[]{:S(2)}, u32[]{:S(2)}) collective-permute-start(f32[128,384]{1,0:T(8,128)S(1)} %collective-permute-done.refs_6_), channel_id=1, source_target_pairs={{0,4},{4,0},{8,12},{12,8},{1,5},{5,1},{9,13},{13,9},{2,6},{6,2},{1... | collective-permute-start | bytes 589832 | tf_op jit(solution)/shard_map/ppermute | solution.py:45
  31.3 10.6 %collective-permute-start.3 = (f32[128,384]{1,0:T(8,128)S(1)}, f32[128,384]{1,0:T(8,128)S(1)}, u32[]{:S(2)}, u32[]{:S(2)}) collective-permute-start(f32[128,384]{1,0:T(8,128)S(1)} %collective-permute-done.2.refs_6_), channel_id=1, source_target_pairs={{0,4},{4,0},{8,12},{12,8},{1,5},{5,1},{9,13},{13,9},{2,6},{6,2},{1... | collective-permute-start | bytes 589832 | tf_op jit(solution)/shard_map/ppermute | solution.py:45
  32.5 11.5 %collective-permute-start.9 = (f32[128,384]{1,0:T(8,128)S(1)}, f32[128,384]{1,0:T(8,128)}, u32[]{:S(2)}, u32[]{:S(2)}) collective-permute-start(f32[128,384]{1,0:T(8,128)S(1)} %collective-permute-done.refs_6_), channel_id=1, source_target_pairs={{0,16},{16,0},{1,17},{17,1},{2,18},{18,2},{3,19},{19,3},{4,20},{20... | collective-permute-start | bytes 589832 | tf_op jit(solution)/shard_map/ppermute | solution.py:45
  36.7 9.1 %collective-permute-start.11 = (f32[128,384]{1,0:T(8,128)S(1)}, f32[128,384]{1,0:T(8,128)}, u32[]{:S(2)}, u32[]{:S(2)}) collective-permute-start(f32[128,384]{1,0:T(8,128)S(1)} %collective-permute-done.10.refs_8_), channel_id=1, source_target_pairs={{0,16},{16,0},{1,17},{17,1},{2,18},{18,2},{3,19},{19,3},{4,20},{20... | collective-permute-start | bytes 589832 | tf_op jit(solution)/shard_map/ppermute | solution.py:45
  36.9 0.7 copy-start.4
  37.6 1.0 copy-start.6
  38.6 0.7 copy-start.7
  41.2 0.7 copy-start.8
  41.8 4.3 %collective-permute-start.12 = (f32[128,256]{1,0:T(8,128)}, f32[128,256]{1,0:T(8,128)}, u32[]{:S(2)}, u32[]{:S(2)}) collective-permute-start(f32[128,256]{1,0:T(8,128)} %get-tuple-element.41), channel_id=1, source_target_pairs={{0,1},{1,0},{2,3},{3,2},{4,5},{5,4},{6,7},{7,6},{8,9},{9,8},{10,11... | collective-permute-start | bytes 393224 | tf_op jit(solution)/shard_map/ppermute | solution.py:45
  41.8 6.7 %collective-permute-start.13 = (f32[128,256]{1,0:T(8,128)}, f32[128,256]{1,0:T(8,128)}, u32[]{:S(2)}, u32[]{:S(2)}) collective-permute-start(f32[128,256]{1,0:T(8,128)} %get-tuple-element.43), channel_id=1, source_target_pairs={{0,2},{1,3},{2,0},{3,1},{4,6},{5,7},{6,4},{7,5},{8,10},{9,11},{10,... | collective-permute-start | bytes 393224 | tf_op jit(solution)/shard_map/ppermute | solution.py:45
  42.7 7.7 %collective-permute-start.14 = (f32[128,256]{1,0:T(8,128)}, f32[128,256]{1,0:T(8,128)}, u32[]{:S(2)}, u32[]{:S(2)}) collective-permute-start(f32[128,256]{1,0:T(8,128)} %get-tuple-element.45), channel_id=1, source_target_pairs={{0,3},{1,2},{2,1},{3,0},{4,7},{5,6},{6,5},{7,4},{8,11},{9,10},{10,... | collective-permute-start | bytes 393224 | tf_op jit(solution)/shard_map/ppermute | solution.py:45
  43.8 6.6 %copy-start.1 = (f32[256,256]{1,0:T(8,128)S(1)}, f32[256,256]{1,0:T(8,128)}, u32[]{:S(2)}) copy-start(f32[256,256]{1,0:T(8,128)} %refs_1_.5) | copy-start | bytes 786436
  43.8 6.6 %copy-start.2 = (f32[256,256]{1,0:T(8,128)S(1)}, f32[256,256]{1,0:T(8,128)}, u32[]{:S(2)}) copy-start(f32[256,256]{1,0:T(8,128)} %refs_2_.5) | copy-start | bytes 786436
  43.8 6.6 %copy-start.3 = (f32[256,256]{1,0:T(8,128)S(1)}, f32[256,256]{1,0:T(8,128)}, u32[]{:S(2)}) copy-start(f32[256,256]{1,0:T(8,128)} %refs_3_.3) | copy-start | bytes 786436
  43.8 6.6 %copy-start.5 = (s32[3]{0:T(128)S(1)}, s32[3]{0:T(128)}, u32[]{:S(2)}) copy-start(s32[3]{0:T(128)} %pad_add_fusion.info) | copy-start | bytes 40
  43.8 6.6 %copy-start.9 = (f32[128,256]{1,0:T(8,128)S(1)}, f32[128,256]{1,0:T(8,128)}, u32[]{:S(2)}) copy-start(f32[128,256]{1,0:T(8,128)} %copy-done.8) | copy-start | bytes 393220
  44.0 17.0 %collective-permute-start.16 = (f32[128,384]{1,0:T(8,128)S(1)}, f32[128,384]{1,0:T(8,128)S(1)}, u32[]{:S(2)}, u32[]{:S(2)}) collective-permute-start(f32[128,384]{1,0:T(8,128)S(1)} %collective-permute-done.2.refs_6_), channel_id=1, source_target_pairs={{0,16},{16,0},{1,17},{17,1},{2,18},{18,2},{3,19},{19,3},{4,20},{20... | collective-permute-start | bytes 589832 | tf_op jit(solution)/shard_map/ppermute | solution.py:45
  45.9 15.1 %collective-permute-start.15 = (f32[128,384]{1,0:T(8,128)S(1)}, f32[128,384]{1,0:T(8,128)S(1)}, u32[]{:S(2)}, u32[]{:S(2)}) collective-permute-start(f32[128,384]{1,0:T(8,128)S(1)} %collective-permute-done.1.refs_4_), channel_id=1, source_target_pairs={{0,16},{16,0},{1,17},{17,1},{2,18},{18,2},{3,19},{19,3},{4,20},{20... | collective-permute-start | bytes 589832 | tf_op jit(solution)/shard_map/ppermute | solution.py:45
  46.1 14.9 %collective-permute-start.17 = (f32[128,384]{1,0:T(8,128)S(1)}, f32[128,384]{1,0:T(8,128)S(1)}, u32[]{:S(2)}, u32[]{:S(2)}) collective-permute-start(f32[128,384]{1,0:T(8,128)S(1)} %collective-permute-done.3.refs_8_), channel_id=1, source_target_pairs={{0,16},{16,0},{1,17},{17,1},{2,18},{18,2},{3,19},{19,3},{4,20},{20... | collective-permute-start | bytes 589832 | tf_op jit(solution)/shard_map/ppermute | solution.py:45
  63.6 20.0 %collective-permute-start.18 = (f32[512,384]{1,0:T(8,128)S(1)}, f32[512,384]{1,0:T(8,128)S(1)}, u32[]{:S(2)}, u32[]{:S(2)}) collective-permute-start(f32[512,384]{1,0:T(8,128)S(1)} %shard_map.108), channel_id=1, source_target_pairs={{0,4},{4,0},{8,12},{12,8},{1,5},{5,1},{9,13},{13,9},{2,6},{6,2},{1... | collective-permute-start | bytes 2359304 | tf_op jit(solution)/shard_map/ppermute | solution.py:45
  87.3 6.0 %collective-permute-start.19 = (f32[256,1024]{1,0:T(8,128)S(1)}, f32[256,1024]{1,0:T(8,128)S(1)}, u32[]{:S(2)}, u32[]{:S(2)}) collective-permute-start(f32[256,1024]{1,0:T(8,128)S(1)} %shard_map.112), channel_id=1, source_target_pairs={{0,1},{1,0},{2,3},{3,2},{4,5},{5,4},{6,7},{7,6},{8,9},{9,8},{10,11... | collective-permute-start | bytes 3145736 | tf_op jit(solution)/shard_map/ppermute | solution.py:45
  87.3 28.4 %collective-permute-start.22 = (f32[512,384]{1,0:T(8,128)S(1)}, f32[512,384]{1,0:T(8,128)S(1)}, u32[]{:S(2)}, u32[]{:S(2)}) collective-permute-start(f32[512,384]{1,0:T(8,128)S(1)} %shard_map.110), channel_id=1, source_target_pairs={{0,4},{4,0},{8,12},{12,8},{1,5},{5,1},{9,13},{13,9},{2,6},{6,2},{1... | collective-permute-start | bytes 2359304 | tf_op jit(solution)/shard_map/ppermute | solution.py:45
  88.6 27.1 %collective-permute-start.21 = (f32[256,384]{1,0:T(8,128)S(1)}, f32[256,384]{1,0:T(8,128)S(1)}, u32[]{:S(2)}, u32[]{:S(2)}) collective-permute-start(f32[256,384]{1,0:T(8,128)S(1)} %get-tuple-element.57), channel_id=1, source_target_pairs={{0,8},{4,12},{8,0},{12,4},{1,9},{5,13},{9,1},{13,5},{2,10},{6,14},... | collective-permute-start | bytes 1179656 | tf_op jit(solution)/shard_map/ppermute | solution.py:45
  93.4 43.5 %collective-permute-start.20 = (f32[128,1024]{1,0:T(8,128)S(1)}, f32[128,1024]{1,0:T(8,128)S(1)}, u32[]{:S(2)}, u32[]{:S(2)}) collective-permute-start(f32[128,1024]{1,0:T(8,128)S(1)} %get-tuple-element.56), channel_id=1, source_target_pairs={{0,2},{1,3},{2,0},{3,1},{4,6},{5,7},{6,4},{7,5},{8,10},{9,11},{10,... | collective-permute-start | bytes 1572872 | tf_op jit(solution)/shard_map/ppermute | solution.py:45
  115.8 20.1 %collective-permute-start.23 = (f32[256,384]{1,0:T(8,128)S(1)}, f32[256,384]{1,0:T(8,128)S(1)}, u32[]{:S(2)}, u32[]{:S(2)}) collective-permute-start(f32[256,384]{1,0:T(8,128)S(1)} %get-tuple-element.60), channel_id=1, source_target_pairs={{0,8},{4,12},{8,0},{12,4},{1,9},{5,13},{9,1},{13,5},{2,10},{6,14},... | collective-permute-start | bytes 1179656 | tf_op jit(solution)/shard_map/ppermute | solution.py:45

commit v2 on v1

--- a/solution.py
+++ b/solution.py
@@ -49,32 +49,11 @@
     return lax.optimization_barrier((value, *others))[0]
 
 
-def halves_body(chunks, wq, wk, wv, *outs):
-    for c in range(chunks):
-        cols = slice(c * LANES, (c + 1) * LANES)
-        outs[c][:, 0:LANES] = wq[:, cols]
-        outs[c][:, LANES : 2 * LANES] = wk[:, cols]
-        outs[c][:, 2 * LANES : 3 * LANES] = wv[:, cols]
-
-
-def weight_halves(info, w_query, w_key, w_value, rows, chunks):
-    columns = w_query.shape[1]
-    spec = pl.BlockSpec((rows, columns), lambda i, info: (info[1], 0))
-    out = pl.BlockSpec((rows, 3 * LANES), lambda i, info: (0, 0))
-    return pl.pallas_call(
-        functools.partial(halves_body_prefetch, chunks),
-        out_shape=[shaped(rows, 3 * LANES)] * chunks,
-        grid_spec=pltpu.PrefetchScalarGridSpec(
-            num_scalar_prefetch=1, grid=(1,), in_specs=[spec] * 3, out_specs=[out] * chunks
-        ),
-    )(info, w_query, w_key, w_value)
-
-
-def halves_body_prefetch(chunks, info, *refs):
-    halves_body(chunks, *refs)
-
-
-def adjoint_body(parts, info, ids, sensors, *refs):
+def entry_body(parts, info, ids, sensors, wq, wk, wv, packed, *refs):
+    if packed is not None:
+        packed[:, 0:LANES] = wq[...]
+        packed[:, LANES : 2 * LANES] = wk[...]
+        packed[:, 2 * LANES :] = wv[...]
     outs, rows = refs[:parts], refs[parts]
     count = sensors.shape[0]
     columns = outs[0].shape[1]
@@ -86,29 +65,70 @@
         outs[r][...] = rows[:, pl.ds(start, columns)]
 
 
+def entry(info, ids, sensors, weights, parts, direct):
+    rows, columns = weights[0].shape
+    count, width = sensors.shape
+
+    def whole(*shape):
+        return pl.BlockSpec(shape, lambda i, info: (0, 0))
+
+    spec = pl.BlockSpec((rows, LANES), lambda i, info: (0, info[1]))
+    body = entry_body if direct else adjoint_body
+    outs = ([(rows, 3 * LANES)] if direct else []) + [(count, columns)] * parts
+    return pl.pallas_call(
+        functools.partial(body, parts),
+        out_shape=[shaped(*o) for o in outs],
+        grid_spec=pltpu.PrefetchScalarGridSpec(
+            num_scalar_prefetch=1,
+            grid=(1,),
+            in_specs=[whole(1, count), whole(count, width)] + ([spec] * 3 if direct else []),
+            out_specs=[whole(*o) for o in outs],
+            scratch_shapes=[pltpu.VMEM((count, width), F32)],
+        ),
+        compiler_params=pltpu.CompilerParams(vmem_limit_bytes=60 << 20),
+    )(info, ids, sensors, *(weights if direct else ()))
+
+
+def columns_of(turn, info):
+    return pl.ds(pl.multiple_of((info[1] ^ turn) * LANES, LANES), LANES)
+
+
+def spread(held, axis, size):
+    held, step = dict(held), size
+    while step > 1:
+        step //= 2
+        if step not in held:
+            held.update({r | step: swap(v, axis, size, step) for r, v in list(held.items())})
+    return held
+
+
+def adjoint_body(parts, info, ids, sensors, *refs):
+    entry_body(parts, info, ids, sensors, None, None, None, None, *refs)
+
+
 def stack_body(parts, *refs):
     rows = refs[0].shape[0]
     for r in range(parts):
         refs[parts][r * rows : (r + 1) * rows, :] = refs[r][...]
 
 
-def attention_body(chunk, blocks, pieces, info, neighbours, *refs):
+def attention_body(turn, blocks, wa, info, neighbours, *refs):
     x, wq, wk, wv = refs[:4]
-    halves = refs[4 : 4 + len(pieces)]
-    adjoints = refs[4 + len(pieces) : 4 + len(pieces) + blocks]
-    out, panel, proj = refs[4 + len(pieces) + blocks :]
-    z, y, t = info[0], info[1], info[2]
-    cols = slice(chunk * LANES, (chunk + 1) * LANES)
-    own = wq.shape[0]
-    rows = pl.ds(pl.multiple_of(z * own, 8), own)
-    panel[rows, 0:LANES] = wq[:, cols]
-    panel[rows, LANES : 2 * LANES] = wk[:, cols]
-    panel[rows, 2 * LANES : 3 * LANES] = wv[:, cols]
-    for (r, g), half in zip(pieces, halves):
-        count = half.shape[0]
-        start = (z ^ r) * own + (y ^ g) * count
-        panel[pl.ds(pl.multiple_of(start, 8), count), :] = half[...]
-    attention_core(cols, blocks, t, neighbours, x, panel, adjoints, out, proj)
+    pieces = refs[4 : 3 + wa]
+    adjoints = refs[3 + wa : 3 + wa + blocks]
+    out, panel, proj = refs[3 + wa + blocks :]
+    cols = columns_of(turn, info)
+    count = wq.shape[0]
+
+    def rows(r):
+        return pl.ds(pl.multiple_of((info[0] ^ r) * count, 8), count)
+
+    panel[rows(0), 0:LANES] = wq[:, cols]
+    panel[rows(0), LANES : 2 * LANES] = wk[:, cols]
+    panel[rows(0), 2 * LANES : 3 * LANES] = wv[:, cols]
+    for r in range(1, wa):
+        panel[rows(r), :] = pieces[r - 1][...]
+    attention_core(cols, blocks, info[2], neighbours, x, panel, adjoints, out, proj)
 
 
 def attention_panel_body(chunk, blocks, info, neighbours, x, panel, *refs):
@@ -198,12 +218,12 @@
         first = keep if first is None else first
 
 
-def join_body(chunks, *refs):
-    for c in range(chunks):
+def join_body(turns, info, *refs):
+    for turn in range(turns):
         for i in range(3):
             part = slice(i * LANES, (i + 1) * LANES)
-            term = refs[2 * c][:, part] + refs[2 * c + 1][:, part]
-            refs[2 * chunks + i][:, c * LANES : (c + 1) * LANES] = term
+            term = refs[2 * turn][:, part] + refs[2 * turn + 1][:, part]
+            refs[2 * turns + i][:, columns_of(turn, info)] = term
 
 
 def per_device(sizes, node_features, sensor_adjoint, sensor_node, neighbours, *weights):
@@ -216,73 +236,51 @@
     nodes = nodes_here * ta
     z, y, t = lax.axis_index("wa"), lax.axis_index("grp"), lax.axis_index("ta")
     info = jnp.stack([z, y, t]).astype(jnp.int32)
-    direct = rows_here % LANES == 0 and rows_here % (8 * grp) == 0 and wa > 1
-
-    first = []
+    direct = rows_here % LANES == 0 and chunks == grp == 2 and wa > 1
+
+    blocks_out = entry(info, sensor_node.reshape(1, -1), sensor_adjoint[0], weights, ta, direct)
+    held = {0: hour_rows}
     if direct:
-        half = rows_here // grp
-        halves = weight_halves(info, *weights, half, chunks)
-        gathered, crossed, last = [], [], None
-        for c in range(chunks):
-            mine = {0: halves[c] if last is None else after(halves[c], last)}
-            step = wa
-            while step > 1:
-                step //= 2
-                mine.update({r | step: swap(v, "wa", wa, step) for r, v in list(mine.items())})
-            last = mine[wa // 2]
-            gathered.append(mine)
-            crossed.append(
-                {(r, g): swap(mine[r], "grp", grp, g) for g in range(1, grp) for r in range(1, wa)}
-            )
-
-        first = [gathered[0][1]]
-
-    held = {0: hour_rows}
-    step = ta
-    while step > 1:
-        step //= 2
-        held.update(
-            {
-                r | step: swap(after(v, *first) if r else v, "ta", ta, step)
-                for r, v in list(held.items())
-            }
-        )
+        first, *blocks_out = blocks_out
+        held[0] = after(hour_rows, first)
+        gathered = [spread({0: first}, "wa", wa)]
+        gathered.append({r: swap(gathered[0][r], "grp", grp, 1) for r in range(1, wa)})
+        held[ta // 2] = after(swap(held[0], "ta", ta, ta // 2), gathered[0][1])
+    held = spread(held, "ta", ta)
+    adjoints = [blocks_out[0]] + [
+        swap(after(blocks_out[r], held[ta // 2]), "ta", ta, r) for r in range(1, ta)
+    ]
     inputs = local_call(
         functools.partial(stack_body, ta), [shaped(nodes, width)], [held[r] for r in range(ta)]
     )[0]
 
-    blocks_out = local_call(
-        functools.partial(adjoint_body, ta),
-        [shaped(nodes_here, columns)] * ta,
-        [sensor_node.reshape(1, -1), sensor_adjoint[0]],
-        scalars=[info],
-        scratch=[pltpu.VMEM((nodes_here, width), F32)],
-        flops=12 * nodes_here * nodes_here * width,
-    )
-    adjoints = [blocks_out[0]] + [
-        swap(after(blocks_out[r], held[ta // 2]), "ta", ta, r) for r in range(1, ta)
-    ]
-
     stacked, panels, owned, firsts = [], [], [], []
     for c in range(chunks):
-        turn = after(info, stacked[-1]) if stacked else info
-        more = direct and c + 1 < chunks
-        if more:
-            turn = after(turn, *[gathered[c + 1][r] for r in range(1, wa)])
         proj_flops = 12 * nodes * width * 3 * LANES + 60 * 2 * nodes * 4 * BLOCK * LANES
         scratch = [pltpu.VMEM((nodes, 3 * LANES), F32)]
+        turn = after(info, stacked[-1]) if stacked else info
         if direct:
-            pieces = {(r, 0): gathered[c][r] for r in range(1, wa)}
-            pieces.update(crossed[c])
-            names = sorted(pieces)
             dqkv, panel = local_call(
-                functools.partial(attention_body, c, blocks, names),
+                functools.partial(attention_body, c, blocks, wa),
                 [shaped(nodes, 3 * LANES), shaped(width, 3 * LANES)],
-                [inputs, *weights, *[pieces[n] for n in names], *adjoints],
+                [inputs, *weights, *[gathered[c][r] for r in range(1, wa)], *adjoints],
                 scalars=[turn, neighbours],
                 scratch=scratch,
                 flops=proj_flops,
             )
+            later = info if c else after(info, dqkv, *[gathered[1][r] for r in range(1, wa - 1)])
+            sends = [
+                local_call(
+                    functools.partial(weight_grad_body, range(odd, wa, 2), rows_here),
+                    [shaped(rows_here * wa // 2, 3 * LANES)],
+                    [inputs, dqkv],
+                    scalars=[later],
+                )[0]
+                for odd in (1, 0)
+            ]
+            kept, got, early = scatter_halving(*sends, "wa", wa, rows_here, owned[-1:])
+            owned += [kept, got]
+            firsts += [sends[0]] if c else [early]
         else:
             cols = slice(c * LANES, (c + 1) * LANES)
             local = jnp.concatenate([w[:, cols] for w in weights], axis=1)
@@ -295,30 +293,10 @@
                 scratch=scratch,
                 flops=proj_flops,
             )[0]
+            full = local_call(whole_grad_body, [shaped(width, 3 * LANES)], [inputs, dqkv])[0]
+            owned.append(lax.psum_scatter(full, "wa", scatter_dimension=0, tiled=True))
         stacked.append(dqkv)
         panels.append(panel)
-        if direct:
-            later = after(info, dqkv, *crossed[c + 1].values()) if more else info
-            sends = [
-                local_call(
-                    functools.partial(weight_grad_body, range(odd, wa, 2), rows_here),
-                    [shaped(rows_here * wa // 2, 3 * LANES)],
-                    [inputs, dqkv],
-                    scalars=[later],
-                )[0]
-                for odd in (1, 0)
-            ]
-            kept, got, early = scatter_halving(*sends, "wa", wa, rows_here, owned[-1:])
-            owned += [kept, got]
-            firsts = (firsts or [early]) if more else [*firsts, sends[0]]
-        else:
-            full = local_call(
-                whole_grad_body,
-                [shaped(width, 3 * LANES)],
-                [inputs, dqkv],
-                flops=12 * nodes * width * 3 * LANES,
-            )[0]
-            owned.append(lax.psum_scatter(full, "wa", scatter_dimension=0, tiled=True))
 
     backs = [
         local_call(
@@ -329,16 +307,21 @@
         for odd in (1, 0)
     ]
     kept, got, _ = scatter_halving(*backs, "ta", ta, nodes_here)
+    back = (kept + got)[None]
     if direct:
+        owned[-1] = after(owned[-1], back)
         grads = local_call(
-            functools.partial(join_body, chunks), [shaped(rows_here, columns)] * 3, owned
+            functools.partial(join_body, chunks),
+            [shaped(rows_here, columns)] * 3,
+            owned,
+            scalars=[info],
         )
     else:
         grads = [
             jnp.concatenate([o[:, i * LANES : (i + 1) * LANES] for o in owned], axis=1)
             for i in range(3)
         ]
-    return ((kept + got)[None], *grads)
+    return (back, *grads)
 
 
 def solution(mesh):

time: 138 us -> 127 us (0.920)
  starting transfers between devices: 25.1 us -> 20.9 us
  waiting for transfers between devices: 63.3 us -> 60.3 us
  local copies, waits for them, and re-layouts: 3.14 us -> 0.79 us
    ppermute x24 -> x18, starting transfers between devices: 25.1 us -> 20.9 us  [swap(): return lax.ppermute(value, axis, [(i, i ^ step) for i in range(size)])]
    ppermute x24 -> x18, waiting for transfers between devices: 63.3 us -> 60.3 us  [swap(): return lax.ppermute(value, axis, [(i, i ^ step) for i in range(size)])]
    unnamed x23 -> x13, local copies, waits for them, and re-layouts: 3.14 us -> 0.79 us
    pallas_call x14 -> x13, Pallas kernels: 41.3 us -> 39.6 us  [local_call(): pl.pallas_call(body, out_shape=outs, in_specs=[smem] * len(scalars) + [vm...]
  transfers between devices with their start and end apart: 24 -> 18, of which waited for: 11 -> 8; matrix products, arithmetic and copies ran while one was open for 1% -> 1% of each run, Pallas kernels for 27% -> 27%
where the time goes in v2:
time: 127 us
  waiting for transfers between devices  60.3 us (47%)
  Pallas kernels  42.8 us (34%)
  starting transfers between devices  20.9 us (16%)
  other arithmetic  1.42 us (1%)
    ppermute x18, waiting for transfers between devices, swap(): return lax.ppermute(value, axis, [(i, i ^ step) for i in range(size)])  60.3 us
    pallas_call x13, Pallas kernels, local_call(): pl.pallas_call(body, out_shape=outs, in_specs=[smem] * len(scalars) + [vm...  39.6 us
    ppermute x18, starting transfers between devices, swap(): return lax.ppermute(value, axis, [(i, i ^ step) for i in range(size)])  20.9 us
    pallas_call x1, Pallas kernels, entry(): pl.pallas_call(functools.partial(body, parts), out_shape=[shaped(*o) for...  3.18 us
  transfers between devices with their start and end apart: 18, of which 8 were waited for; matrix products, arithmetic and copies ran while one was open for 1% of the time, Pallas kernels for 27%

profile of v2, /device:TPU:0, one launch (start us, length us, event | category | flops | bytes accessed | tf_op | source)
XLA Modules:
  0.0 127.1 jit_solution(5515089637831368931)
XLA Ops:
  0.6 0.0 copy-start
  0.6 0.6 pad_add_fusion.info
  1.2 3.2 %shard_map.102 = (f32[256,384]{1,0:T(8,128)}, f32[128,256]{1,0:T(8,128)}, f32[128,256]{1,0:T(8,128)}, f32[128,256]{1,0:T(8,128)}, f32[128,256]{1,0:T(8,128)}) custom-call(s32[3]{0:T(128)} %pad_add_fusion.info, s32[1,128]{1,0:T(1,128)} %bitcast.12, f32[128,1024]{1,0:T(8,128)} %bitcast.11, f32[256,256]{1,0:T(8,128)} %refs_1_.3, f32[256,256]{1,0:T(8,128)} %refs_2_.3, ...), custom_call_target="tpu_custom_call" | custom-call | tf_op jit(solution)/shard_map/pallas_call | solution.py:78
  4.4 2.9 %collective-permute-start.1 = (f32[128,1024]{1,0:T(8,128)}, f32[128,1024]{1,0:T(8,128)S(1)}, u32[]{:S(2)}, u32[]{:S(2)}) collective-permute-start(f32[128,1024]{1,0:T(8,128)} %bitcast.8), channel_id=1, source_target_pairs={{0,2},{1,3},{2,0},{3,1},{4,6},{5,7},{6,4},{7,5},{8,10},{9,11},{10,... | collective-permute-start | bytes 1572872 | tf_op jit(solution)/shard_map/ppermute | solution.py:45
  7.3 1.6 %collective-permute-start.2 = (f32[256,384]{1,0:T(8,128)}, f32[256,384]{1,0:T(8,128)S(1)}, u32[]{:S(2)}, u32[]{:S(2)}) collective-permute-start(f32[256,384]{1,0:T(8,128)} %get-tuple-element.33), channel_id=1, source_target_pairs={{0,4},{4,0},{8,12},{12,8},{1,5},{5,1},{9,13},{13,9},{2,6},{6,2},{1... | collective-permute-start | bytes 1179656 | tf_op jit(solution)/shard_map/ppermute | solution.py:45
  8.9 2.6 %collective-permute-start.4 = (f32[256,384]{1,0:T(8,128)}, f32[256,384]{1,0:T(8,128)S(1)}, u32[]{:S(2)}, u32[]{:S(2)}) collective-permute-start(f32[256,384]{1,0:T(8,128)} %get-tuple-element.33), channel_id=1, source_target_pairs={{0,8},{4,12},{8,0},{12,4},{1,9},{5,13},{9,1},{13,5},{2,10},{6,14},... | collective-permute-start | bytes 1179656 | tf_op jit(solution)/shard_map/ppermute | solution.py:45
  11.5 0.0 collective-permute-start
  11.5 14.9 %collective-permute-done.2.refs_4_ = f32[256,384]{1,0:T(8,128)S(1)} collective-permute-done((f32[256,384]{1,0:T(8,128)}, f32[256,384]{1,0:T(8,128)S(1)}, u32[]{:S(2)}, u32[]{:S(2)}) %collective-permute-start.2) | collective-permute-done | bytes 393248 | tf_op jit(solution)/shard_map/ppermute | solution.py:45
  26.4 0.0 collective-permute-done.1.refs_2_
  26.4 0.0 collective-permute-start.3
  26.4 2.4 %collective-permute-done.4.refs_5_ = f32[256,384]{1,0:T(8,128)S(1)} collective-permute-done((f32[256,384]{1,0:T(8,128)}, f32[256,384]{1,0:T(8,128)S(1)}, u32[]{:S(2)}, u32[]{:S(2)}) %collective-permute-start.4) | collective-permute-done | bytes 393248 | tf_op jit(solution)/shard_map/ppermute | solution.py:45
  28.8 0.4 collective-permute-start.5
  29.2 0.0 collective-permute-start.6
  29.2 0.5 collective-permute-start.7
  29.8 0.0 collective-permute-done.refs_1_
  29.8 1.3 %collective-permute-start.8 = (f32[128,256]{1,0:T(8,128)}, f32[128,256]{1,0:T(8,128)}, u32[]{:S(2)}, u32[]{:S(2)}) collective-permute-start(f32[128,256]{1,0:T(8,128)} %get-tuple-element.42), channel_id=1, source_target_pairs={{0,3},{1,2},{2,1},{3,0},{4,7},{5,6},{6,5},{7,4},{8,11},{9,10},{10,... | collective-permute-start | bytes 393224 | tf_op jit(solution)/shard_map/ppermute | solution.py:45
  31.1 0.8 copy.11.neighbours
  31.9 0.0 copy-start.1
  31.9 0.0 copy-start.2
  31.9 0.0 copy-start.3
  31.9 0.0 copy-start.5
  31.9 0.0 collective-permute-done.3.refs_3_
  31.9 1.6 %collective-permute-start.10 = (f32[256,384]{1,0:T(8,128)S(1)}, f32[256,384]{1,0:T(8,128)S(1)}, u32[]{:S(2)}, u32[]{:S(2)}) collective-permute-start(f32[256,384]{1,0:T(8,128)S(1)} %collective-permute-done.4.refs_5_), channel_id=1, source_target_pairs={{0,16},{16,0},{1,17},{17,1},{2,18},{18,2},{3,19},{19,3},{4,20},{20... | collective-permute-start | bytes 1179656 | tf_op jit(solution)/shard_map/ppermute | solution.py:45
  33.5 0.0 copy-done
  33.5 0.1 shard_map.103.refs_0_.x
  33.6 0.0 collective-permute-done.6.refs_8_
  33.6 0.6 collective-permute-start.9
  34.2 3.7 %collective-permute-done.5.refs_6_ = f32[256,384]{1,0:T(8,128)S(1)} collective-permute-done((f32[256,384]{1,0:T(8,128)S(1)}, f32[256,384]{1,0:T(8,128)S(1)}, u32[]{:S(2)}, u32[]{:S(2)}) %collective-permute-start.5) | collective-permute-done | bytes 393248 | tf_op jit(solution)/shard_map/ppermute | solution.py:45
  38.0 1.5 %collective-permute-start.11 = (f32[256,384]{1,0:T(8,128)S(1)}, f32[256,384]{1,0:T(8,128)S(1)}, u32[]{:S(2)}, u32[]{:S(2)}) collective-permute-start(f32[256,384]{1,0:T(8,128)S(1)} %collective-permute-done.5.refs_6_), channel_id=1, source_target_pairs={{0,16},{16,0},{1,17},{17,1},{2,18},{18,2},{3,19},{19,3},{4,20},{20... | collective-permute-start | bytes 1179656 | tf_op jit(solution)/shard_map/ppermute | solution.py:45
  39.5 0.0 collective-permute-done.7.refs_9_
  39.5 0.0 collective-permute-done.8.refs_10_
  39.5 0.0 copy-done.1
  39.5 0.0 copy-done.2
  39.5 0.0 copy-done.3
  39.5 0.0 copy-done.4
  39.5 0.0 copy-done.5
  39.5 10.2 %shard_map.104 = (f32[512,384]{1,0:T(8,128)S(1)}, f32[1024,384]{1,0:T(8,128)S(1)}) custom-call(s32[3]{0:T(128)S(1)} %copy-done.4, s32[4,2]{1,0:T(4,128)S(1)} %copy.11.neighbours, f32[512,1024]{1,0:T(8,128)S(1)} %shard_map.103.refs_0_.x, f32[256,256]{1,0:T(8,128)S(1)} %copy-done.1, f32[256,256]{1,0:T(8,128)S(1)} %copy-done.2, f32[256,256]{1,0:T(8,128)S(1)} %copy-done.3, ...), custom_call_target="tpu_custom_call" | custom-call | flops 6442450944 | bytes 25165824 | tf_op jit(solution)/shard_map/pallas_call | solution.py:29
  49.8 0.0 collective-permute-done.10.refs_5_
  49.8 2.6 %collective-permute-done.9.refs_4_ = f32[256,384]{1,0:T(8,128)S(1)} collective-permute-done((f32[256,384]{1,0:T(8,128)S(1)}, f32[256,384]{1,0:T(8,128)S(1)}, u32[]{:S(2)}, u32[]{:S(2)}) %collective-permute-start.9) | collective-permute-done | bytes 393248 | tf_op jit(solution)/shard_map/ppermute | solution.py:45
  52.3 2.6 %shard_map.107 = f32[512,384]{1,0:T(8,128)S(1)} custom-call(s32[3]{0:T(128)S(1)} %copy-done.4, f32[512,1024]{1,0:T(8,128)S(1)} %shard_map.103.refs_0_.x, f32[512,384]{1,0:T(8,128)S(1)} %get-tuple-element.43.stacked.refs_0_), custom_call_target="tpu_custom_call" | custom-call | tf_op jit(solution)/shard_map/pallas_call | solution.py:29
  55.0 1.7 %collective-permute-start.12 = (f32[512,384]{1,0:T(8,128)S(1)}, f32[512,384]{1,0:T(8,128)S(1)}, u32[]{:S(2)}, u32[]{:S(2)}) collective-permute-start(f32[512,384]{1,0:T(8,128)S(1)} %shard_map.107), channel_id=1, source_target_pairs={{0,4},{4,0},{8,12},{12,8},{1,5},{5,1},{9,13},{13,9},{2,6},{6,2},{1... | collective-permute-start | bytes 2359304 | tf_op jit(solution)/shard_map/ppermute | solution.py:45
  56.6 2.4 %shard_map.106.keep = f32[512,384]{1,0:T(8,128)S(1)} custom-call(s32[3]{0:T(128)S(1)} %copy-done.4, f32[512,1024]{1,0:T(8,128)S(1)} %shard_map.103.refs_0_.x, f32[512,384]{1,0:T(8,128)S(1)} %get-tuple-element.43.stacked.refs_0_), custom_call_target="tpu_custom_call" | custom-call | tf_op jit(solution)/shard_map/pallas_call | solution.py:29
  59.1 1.0 collective-permute-done.11.refs_6_
  60.1 10.2 %shard_map.105 = (f32[512,384]{1,0:T(8,128)S(1)}, f32[1024,384]{1,0:T(8,128)S(1)}) custom-call(s32[3]{0:T(128)S(1)} %copy-done.4, s32[4,2]{1,0:T(4,128)S(1)} %copy.11.neighbours, f32[512,1024]{1,0:T(8,128)S(1)} %shard_map.103.refs_0_.x, f32[256,256]{1,0:T(8,128)S(1)} %copy-done.1, f32[256,256]{1,0:T(8,128)S(1)} %copy-done.2, f32[256,256]{1,0:T(8,128)S(1)} %copy-done.3, ...), custom_call_target="tpu_custom_call" | custom-call | flops 6442450944 | bytes 25165824 | tf_op jit(solution)/shard_map/pallas_call | solution.py:29
  70.4 2.7 %shard_map.109 = f32[512,384]{1,0:T(8,128)S(1)} custom-call(s32[3]{0:T(128)S(1)} %copy-done.4, f32[512,1024]{1,0:T(8,128)S(1)} %shard_map.103.refs_0_.x, f32[512,384]{1,0:T(8,128)S(1)} %get-tuple-element.45.stacked.refs_1_), custom_call_target="tpu_custom_call" | custom-call | tf_op jit(solution)/shard_map/pallas_call | solution.py:29
  73.0 0.3 collective-permute-done.12.got
  73.3 0.1 shard_map.108
  73.4 3.5 %shard_map.111 = f32[256,1024]{1,0:T(8,128)S(1)} custom-call(f32[512,384]{1,0:T(8,128)S(1)} %get-tuple-element.43.stacked.refs_0_, f32[512,384]{1,0:T(8,128)S(1)} %get-tuple-element.45.stacked.refs_1_, f32[1024,384]{1,0:T(8,128)S(1)} %get-tuple-element.49.refs_2_, f32[1024,384]{1,0:T(8,128)S(1)} %get-tuple-element.51.refs_3_), custom_call_target="tpu_custom_call" | custom-call | tf_op jit(solution)/shard_map/pallas_call | solution.py:29
  76.9 0.1 collective-permute-start.13
  77.0 1.7 %collective-permute-start.16 = (f32[512,384]{1,0:T(8,128)S(1)}, f32[512,384]{1,0:T(8,128)S(1)}, u32[]{:S(2)}, u32[]{:S(2)}) collective-permute-start(f32[512,384]{1,0:T(8,128)S(1)} %shard_map.109), channel_id=1, source_target_pairs={{0,4},{4,0},{8,12},{12,8},{1,5},{5,1},{9,13},{13,9},{2,6},{6,2},{1... | collective-permute-start | bytes 2359304 | tf_op jit(solution)/shard_map/ppermute | solution.py:45
  78.7 3.5 %shard_map.110.keep = f32[256,1024]{1,0:T(8,128)S(1)} custom-call(f32[512,384]{1,0:T(8,128)S(1)} %get-tuple-element.43.stacked.refs_0_, f32[512,384]{1,0:T(8,128)S(1)} %get-tuple-element.45.stacked.refs_1_, f32[1024,384]{1,0:T(8,128)S(1)} %get-tuple-element.49.refs_2_, f32[1024,384]{1,0:T(8,128)S(1)} %get-tuple-element.51.refs_3_), custom_call_target="tpu_custom_call" | custom-call | tf_op jit(solution)/shard_map/pallas_call | solution.py:29
  82.2 0.0 collective-permute-done.13.got
  82.2 0.1 shard_map.112
  82.3 0.6 collective-permute-start.14
  82.9 1.3 %collective-permute-start.15 = (f32[256,384]{1,0:T(8,128)S(1)}, f32[256,384]{1,0:T(8,128)S(1)}, u32[]{:S(2)}, u32[]{:S(2)}) collective-permute-start(f32[256,384]{1,0:T(8,128)S(1)} %get-tuple-element.54), channel_id=1, source_target_pairs={{0,8},{4,12},{8,0},{12,4},{1,9},{5,13},{9,1},{13,5},{2,10},{6,14},... | collective-permute-start | bytes 1179656 | tf_op jit(solution)/shard_map/ppermute | solution.py:45
  84.2 2.4 %shard_map.113.keep = f32[512,384]{1,0:T(8,128)S(1)} custom-call(s32[3]{0:T(128)S(1)} %copy-done.4, f32[512,1024]{1,0:T(8,128)S(1)} %shard_map.103.refs_0_.x, f32[512,384]{1,0:T(8,128)S(1)} %get-tuple-element.45.stacked.refs_1_), custom_call_target="tpu_custom_call" | custom-call | tf_op jit(solution)/shard_map/pallas_call | solution.py:29
  86.6 18.8 %collective-permute-done.16.got = f32[512,384]{1,0:T(8,128)S(1)} collective-permute-done((f32[512,384]{1,0:T(8,128)S(1)}, f32[512,384]{1,0:T(8,128)S(1)}, u32[]{:S(2)}, u32[]{:S(2)}) %collective-permute-start.16) | collective-permute-done | bytes 786464 | tf_op jit(solution)/shard_map/ppermute | solution.py:45
  105.4 0.0 collective-permute-done.15.refs_1_
  105.4 0.1 shard_map.114
  105.5 2.6 %collective-permute-start.17 = (f32[256,384]{1,0:T(8,128)S(1)}, f32[256,384]{1,0:T(8,128)S(1)}, u32[]{:S(2)}, u32[]{:S(2)}) collective-permute-start(f32[256,384]{1,0:T(8,128)S(1)} %get-tuple-element.57), channel_id=1, source_target_pairs={{0,8},{4,12},{8,0},{12,4},{1,9},{5,13},{9,1},{13,5},{2,10},{6,14},... | collective-permute-start | bytes 1179656 | tf_op jit(solution)/shard_map/ppermute | solution.py:45
  108.1 0.0 collective-permute-done.14
  108.1 0.9 add_bitcast_fusion
  108.9 16.6 %collective-permute-done.17.refs_3_ = f32[256,384]{1,0:T(8,128)S(1)} collective-permute-done((f32[256,384]{1,0:T(8,128)S(1)}, f32[256,384]{1,0:T(8,128)S(1)}, u32[]{:S(2)}, u32[]{:S(2)}) %collective-permute-start.17) | collective-permute-done | bytes 393248 | tf_op jit(solution)/shard_map/ppermute | solution.py:45
  125.6 1.5 %shard_map.115 = (f32[256,256]{1,0:T(8,128)}, f32[256,256]{1,0:T(8,128)}, f32[256,256]{1,0:T(8,128)}) custom-call(s32[3]{0:T(128)S(1)} %copy-done.4, f32[256,384]{1,0:T(8,128)S(1)} %get-tuple-element.48.refs_0_, f32[256,384]{1,0:T(8,128)S(1)} %collective-permute-done.15.refs_1_, f32[256,384]{1,0:T(8,128)S(1)} %get-tuple-element.56.refs_2_, ...), custom_call_target="tpu_custom_call" | custom-call | tf_op jit(solution)/shard_map/pallas_call | solution.py:29
  (1 shorter events, 0.0 us)
Async XLA Ops:
  0.6 32.9 %copy-start = (f32[1,128,1024]{2,1,0:T(8,128)S(1)}, f32[1,128,1024]{2,1,0:T(8,128)}, u32[]{:S(2)}) copy-start(f32[1,128,1024]{2,1,0:T(8,128)} %param.7) | copy-start | bytes 1572868
  4.4 22.0 %collective-permute-start.1 = (f32[128,1024]{1,0:T(8,128)}, f32[128,1024]{1,0:T(8,128)S(1)}, u32[]{:S(2)}, u32[]{:S(2)}) collective-permute-start(f32[128,1024]{1,0:T(8,128)} %bitcast.8), channel_id=1, source_target_pairs={{0,2},{1,3},{2,0},{3,1},{4,6},{5,7},{6,4},{7,5},{8,10},{9,11},{10,... | collective-permute-start | bytes 1572872 | tf_op jit(solution)/shard_map/ppermute | solution.py:45
  7.3 19.1 %collective-permute-start.2 = (f32[256,384]{1,0:T(8,128)}, f32[256,384]{1,0:T(8,128)S(1)}, u32[]{:S(2)}, u32[]{:S(2)}) collective-permute-start(f32[256,384]{1,0:T(8,128)} %get-tuple-element.33), channel_id=1, source_target_pairs={{0,4},{4,0},{8,12},{12,8},{1,5},{5,1},{9,13},{13,9},{2,6},{6,2},{1... | collective-permute-start | bytes 1179656 | tf_op jit(solution)/shard_map/ppermute | solution.py:45
  8.9 19.9 %collective-permute-start.4 = (f32[256,384]{1,0:T(8,128)}, f32[256,384]{1,0:T(8,128)S(1)}, u32[]{:S(2)}, u32[]{:S(2)}) collective-permute-start(f32[256,384]{1,0:T(8,128)} %get-tuple-element.33), channel_id=1, source_target_pairs={{0,8},{4,12},{8,0},{12,4},{1,9},{5,13},{9,1},{13,5},{2,10},{6,14},... | collective-permute-start | bytes 1179656 | tf_op jit(solution)/shard_map/ppermute | solution.py:45
  11.5 18.3 %collective-permute-start = (f32[128,1024]{1,0:T(8,128)}, f32[128,1024]{1,0:T(8,128)S(1)}, u32[]{:S(2)}, u32[]{:S(2)}) collective-permute-start(f32[128,1024]{1,0:T(8,128)} %bitcast.9), channel_id=1, source_target_pairs={{0,1},{1,0},{2,3},{3,2},{4,5},{5,4},{6,7},{7,6},{8,9},{9,8},{10,11... | collective-permute-start | bytes 1572872 | tf_op jit(solution)/shard_map/ppermute | solution.py:45
  26.4 5.5 %collective-permute-start.3 = (f32[128,1024]{1,0:T(8,128)S(1)}, f32[128,1024]{1,0:T(8,128)S(1)}, u32[]{:S(2)}, u32[]{:S(2)}) collective-permute-start(f32[128,1024]{1,0:T(8,128)S(1)} %collective-permute-done.1.refs_2_), channel_id=1, source_target_pairs={{0,1},{1,0},{2,3},{3,2},{4,5},{5,4},{6,7},{7,6},{8,9},{9,8},{10,11... | collective-permute-start | bytes 1572872 | tf_op jit(solution)/shard_map/ppermute | solution.py:45
  28.8 9.1 %collective-permute-start.5 = (f32[256,384]{1,0:T(8,128)S(1)}, f32[256,384]{1,0:T(8,128)S(1)}, u32[]{:S(2)}, u32[]{:S(2)}) collective-permute-start(f32[256,384]{1,0:T(8,128)S(1)} %collective-permute-done.4.refs_5_), channel_id=1, source_target_pairs={{0,4},{4,0},{8,12},{12,8},{1,5},{5,1},{9,13},{13,9},{2,6},{6,2},{1... | collective-permute-start | bytes 1179656 | tf_op jit(solution)/shard_map/ppermute | solution.py:45
  29.2 4.4 %collective-permute-start.6 = (f32[128,256]{1,0:T(8,128)}, f32[128,256]{1,0:T(8,128)S(1)}, u32[]{:S(2)}, u32[]{:S(2)}) collective-permute-start(f32[128,256]{1,0:T(8,128)} %get-tuple-element.38), channel_id=1, source_target_pairs={{0,1},{1,0},{2,3},{3,2},{4,5},{5,4},{6,7},{7,6},{8,9},{9,8},{10,11... | collective-permute-start | bytes 393224 | tf_op jit(solution)/shard_map/ppermute | solution.py:45
  29.2 10.2 %collective-permute-start.7 = (f32[128,256]{1,0:T(8,128)}, f32[128,256]{1,0:T(8,128)S(1)}, u32[]{:S(2)}, u32[]{:S(2)}) collective-permute-start(f32[128,256]{1,0:T(8,128)} %get-tuple-element.40), channel_id=1, source_target_pairs={{0,2},{1,3},{2,0},{3,1},{4,6},{5,7},{6,4},{7,5},{8,10},{9,11},{10,... | collective-permute-start | bytes 393224 | tf_op jit(solution)/shard_map/ppermute | solution.py:45
  29.8 9.7 %collective-permute-start.8 = (f32[128,256]{1,0:T(8,128)}, f32[128,256]{1,0:T(8,128)}, u32[]{:S(2)}, u32[]{:S(2)}) collective-permute-start(f32[128,256]{1,0:T(8,128)} %get-tuple-element.42), channel_id=1, source_target_pairs={{0,3},{1,2},{2,1},{3,0},{4,7},{5,6},{6,5},{7,4},{8,11},{9,10},{10,... | collective-permute-start | bytes 393224 | tf_op jit(solution)/shard_map/ppermute | solution.py:45
  31.9 7.6 %copy-start.1 = (f32[256,256]{1,0:T(8,128)S(1)}, f32[256,256]{1,0:T(8,128)}, u32[]{:S(2)}) copy-start(f32[256,256]{1,0:T(8,128)} %refs_1_.3) | copy-start | bytes 786436
  31.9 7.6 %copy-start.2 = (f32[256,256]{1,0:T(8,128)S(1)}, f32[256,256]{1,0:T(8,128)}, u32[]{:S(2)}) copy-start(f32[256,256]{1,0:T(8,128)} %refs_2_.3) | copy-start | bytes 786436
  31.9 7.6 %copy-start.3 = (f32[256,256]{1,0:T(8,128)S(1)}, f32[256,256]{1,0:T(8,128)}, u32[]{:S(2)}) copy-start(f32[256,256]{1,0:T(8,128)} %refs_3_.3) | copy-start | bytes 786436
  31.9 7.6 %copy-start.4 = (s32[3]{0:T(128)S(1)}, s32[3]{0:T(128)}, u32[]{:S(2)}) copy-start(s32[3]{0:T(128)} %pad_add_fusion.info) | copy-start | bytes 40
  31.9 7.6 %copy-start.5 = (f32[128,256]{1,0:T(8,128)S(1)}, f32[128,256]{1,0:T(8,128)}, u32[]{:S(2)}) copy-start(f32[128,256]{1,0:T(8,128)} %get-tuple-element.36.refs_7_) | copy-start | bytes 393220
  31.9 17.9 %collective-permute-start.10 = (f32[256,384]{1,0:T(8,128)S(1)}, f32[256,384]{1,0:T(8,128)S(1)}, u32[]{:S(2)}, u32[]{:S(2)}) collective-permute-start(f32[256,384]{1,0:T(8,128)S(1)} %collective-permute-done.4.refs_5_), channel_id=1, source_target_pairs={{0,16},{16,0},{1,17},{17,1},{2,18},{18,2},{3,19},{19,3},{4,20},{20... | collective-permute-start | bytes 1179656 | tf_op jit(solution)/shard_map/ppermute | solution.py:45
  33.6 18.7 %collective-permute-start.9 = (f32[256,384]{1,0:T(8,128)S(1)}, f32[256,384]{1,0:T(8,128)S(1)}, u32[]{:S(2)}, u32[]{:S(2)}) collective-permute-start(f32[256,384]{1,0:T(8,128)S(1)} %collective-permute-done.2.refs_4_), channel_id=1, source_target_pairs={{0,16},{16,0},{1,17},{17,1},{2,18},{18,2},{3,19},{19,3},{4,20},{20... | collective-permute-start | bytes 1179656 | tf_op jit(solution)/shard_map/ppermute | solution.py:45
  38.0 22.2 %collective-permute-start.11 = (f32[256,384]{1,0:T(8,128)S(1)}, f32[256,384]{1,0:T(8,128)S(1)}, u32[]{:S(2)}, u32[]{:S(2)}) collective-permute-start(f32[256,384]{1,0:T(8,128)S(1)} %collective-permute-done.5.refs_6_), channel_id=1, source_target_pairs={{0,16},{16,0},{1,17},{17,1},{2,18},{18,2},{3,19},{19,3},{4,20},{20... | collective-permute-start | bytes 1179656 | tf_op jit(solution)/shard_map/ppermute | solution.py:45
  55.0 18.3 %collective-permute-start.12 = (f32[512,384]{1,0:T(8,128)S(1)}, f32[512,384]{1,0:T(8,128)S(1)}, u32[]{:S(2)}, u32[]{:S(2)}) collective-permute-start(f32[512,384]{1,0:T(8,128)S(1)} %shard_map.107), channel_id=1, source_target_pairs={{0,4},{4,0},{8,12},{12,8},{1,5},{5,1},{9,13},{13,9},{2,6},{6,2},{1... | collective-permute-start | bytes 2359304 | tf_op jit(solution)/shard_map/ppermute | solution.py:45
  76.9 5.3 %collective-permute-start.13 = (f32[256,1024]{1,0:T(8,128)S(1)}, f32[256,1024]{1,0:T(8,128)S(1)}, u32[]{:S(2)}, u32[]{:S(2)}) collective-permute-start(f32[256,1024]{1,0:T(8,128)S(1)} %shard_map.111), channel_id=1, source_target_pairs={{0,1},{1,0},{2,3},{3,2},{4,5},{5,4},{6,7},{7,6},{8,9},{9,8},{10,11... | collective-permute-start | bytes 3145736 | tf_op jit(solution)/shard_map/ppermute | solution.py:45
  77.0 28.4 %collective-permute-start.16 = (f32[512,384]{1,0:T(8,128)S(1)}, f32[512,384]{1,0:T(8,128)S(1)}, u32[]{:S(2)}, u32[]{:S(2)}) collective-permute-start(f32[512,384]{1,0:T(8,128)S(1)} %shard_map.109), channel_id=1, source_target_pairs={{0,4},{4,0},{8,12},{12,8},{1,5},{5,1},{9,13},{13,9},{2,6},{6,2},{1... | collective-permute-start | bytes 2359304 | tf_op jit(solution)/shard_map/ppermute | solution.py:45
  82.3 25.7 %collective-permute-start.14 = (f32[128,1024]{1,0:T(8,128)S(1)}, f32[128,1024]{1,0:T(8,128)S(1)}, u32[]{:S(2)}, u32[]{:S(2)}) collective-permute-start(f32[128,1024]{1,0:T(8,128)S(1)} %get-tuple-element.53), channel_id=1, source_target_pairs={{0,2},{1,3},{2,0},{3,1},{4,6},{5,7},{6,4},{7,5},{8,10},{9,11},{10,... | collective-permute-start | bytes 1572872 | tf_op jit(solution)/shard_map/ppermute | solution.py:45
  82.9 22.5 %collective-permute-start.15 = (f32[256,384]{1,0:T(8,128)S(1)}, f32[256,384]{1,0:T(8,128)S(1)}, u32[]{:S(2)}, u32[]{:S(2)}) collective-permute-start(f32[256,384]{1,0:T(8,128)S(1)} %get-tuple-element.54), channel_id=1, source_target_pairs={{0,8},{4,12},{8,0},{12,4},{1,9},{5,13},{9,1},{13,5},{2,10},{6,14},... | collective-permute-start | bytes 1179656 | tf_op jit(solution)/shard_map/ppermute | solution.py:45
  105.5 20.1 %collective-permute-start.17 = (f32[256,384]{1,0:T(8,128)S(1)}, f32[256,384]{1,0:T(8,128)S(1)}, u32[]{:S(2)}, u32[]{:S(2)}) collective-permute-start(f32[256,384]{1,0:T(8,128)S(1)} %get-tuple-element.57), channel_id=1, source_target_pairs={{0,8},{4,12},{8,0},{12,4},{1,9},{5,13},{9,1},{13,5},{2,10},{6,14},... | collective-permute-start | bytes 1179656 | tf_op jit(solution)/shard_map/ppermute | solution.py:45

commit v3 on v2

--- a/solution.py
+++ b/solution.py
@@ -10,6 +10,7 @@
 DH = 64
 BLOCK = 128
 KB = 2
+GATE = (1,)
 LANES = 128
 F32 = jnp.float32
 NN = ((1,), (0,))
@@ -21,6 +22,21 @@
     return lax.dot_general(
         left, right, (dims, ((), ())), precision=lax.Precision.HIGHEST, preferred_element_type=F32
     )
+
+
+def grads_of(shares, info, inputs, stacked, rows):
+    return local_call(
+        functools.partial(weight_grad_body, shares, rows),
+        [shaped(rows * len(shares), stacked.shape[1])],
+        [inputs, stacked],
+        scalars=[info],
+    )[0]
+
+
+def total_of(kept, got, rows):
+    return local_call(
+        functools.partial(sum_body, rows), [shaped(rows, kept.shape[1])], [kept, got]
+    )[0]
 
 
 def local_call(body, outs, args, scalars=(), scratch=(), flops=0, vmem_mib=24):
@@ -205,25 +221,32 @@
         out[place, :] = keep[here, :] + got[here, :]
 
 
-def scatter_halving(send, keep, axis, size, rows, wait=()):
+def scatter_halving(send, keep, axis, size, rows):
     step, first = 1, None
     while True:
         got = swap(send, axis, size, step)
         step *= 2
         if step == size:
             return keep, got, first
-        got = after(got, *wait) if wait else got
         shape = shaped(keep.shape[0] // 2, keep.shape[1])
         send, keep = local_call(functools.partial(halve_body, rows), [shape] * 2, [keep, got])
         first = keep if first is None else first
 
 
+def sum_body(rows, kept, got, out):
+    out[...] = kept[-rows:, :] + got[-rows:, :]
+
+
 def join_body(turns, info, *refs):
+    count = (len(refs) - 3) // turns
     for turn in range(turns):
         for i in range(3):
             part = slice(i * LANES, (i + 1) * LANES)
-            term = refs[2 * turn][:, part] + refs[2 * turn + 1][:, part]
-            refs[2 * turns + i][:, columns_of(turn, info)] = term
+            rows = refs[-1].shape[0]
+            total = refs[turn * count][:rows, part]
+            for term in refs[turn * count + 1 : (turn + 1) * count]:
+                total += term[:rows, part]
+            refs[turns * count + i][:, columns_of(turn, info)] = total
 
 
 def per_device(sizes, node_features, sensor_adjoint, sensor_node, neighbours, *weights):
@@ -236,7 +259,7 @@
     nodes = nodes_here * ta
     z, y, t = lax.axis_index("wa"), lax.axis_index("grp"), lax.axis_index("ta")
     info = jnp.stack([z, y, t]).astype(jnp.int32)
-    direct = rows_here % LANES == 0 and chunks == grp == 2 and wa > 1
+    direct = rows_here % LANES == 0 and chunks == grp == 2 and wa == 4
 
     blocks_out = entry(info, sensor_node.reshape(1, -1), sensor_adjoint[0], weights, ta, direct)
     held = {0: hour_rows}
@@ -254,11 +277,11 @@
         functools.partial(stack_body, ta), [shaped(nodes, width)], [held[r] for r in range(ta)]
     )[0]
 
-    stacked, panels, owned, firsts = [], [], [], []
+    stacked, panels, owned, sent, ready = [], [], [], [], []
     for c in range(chunks):
         proj_flops = 12 * nodes * width * 3 * LANES + 60 * 2 * nodes * 4 * BLOCK * LANES
         scratch = [pltpu.VMEM((nodes, 3 * LANES), F32)]
-        turn = after(info, stacked[-1]) if stacked else info
+        turn = after(info, stacked[-1], *sent) if stacked else info
         if direct:
             dqkv, panel = local_call(
                 functools.partial(attention_body, c, blocks, wa),
@@ -268,19 +291,19 @@
                 scratch=scratch,
                 flops=proj_flops,
             )
-            later = info if c else after(info, dqkv, *[gathered[1][r] for r in range(1, wa - 1)])
-            sends = [
-                local_call(
-                    functools.partial(weight_grad_body, range(odd, wa, 2), rows_here),
-                    [shaped(rows_here * wa // 2, 3 * LANES)],
-                    [inputs, dqkv],
-                    scalars=[later],
-                )[0]
-                for odd in (1, 0)
-            ]
-            kept, got, early = scatter_halving(*sends, "wa", wa, rows_here, owned[-1:])
-            owned += [kept, got]
-            firsts += [sends[0]] if c else [early]
+            if not c:
+                later = after(info, dqkv, *[gathered[1][r] for r in GATE])
+                odd = grads_of((1, 3), later, inputs, dqkv, rows_here)
+                even = grads_of((0, 2), after(info, odd), inputs, dqkv, rows_here)
+                got = swap(odd, "wa", wa, 1)
+                passed = total_of(even, got, rows_here)
+                owned = [even, got, swap(passed, "wa", wa, 2)]
+                sent = [odd]
+            else:
+                shares = {}
+                for r in (3, 1, 2, 0):
+                    shares[r] = grads_of((r,), after(info, *shares.values()), inputs, dqkv, rows_here)
+                ready.append(shares)
         else:
             cols = slice(c * LANES, (c + 1) * LANES)
             local = jnp.concatenate([w[:, cols] for w in weights], axis=1)
@@ -298,18 +321,27 @@
         stacked.append(dqkv)
         panels.append(panel)
 
+    if direct:
+        (shares,) = ready
+        message = swap(after(shares[3], owned[1]), "wa", wa, 1)
+        sent = [shares[3]]
     backs = [
         local_call(
             functools.partial(back_body, range(odd, ta, 2), chunks),
             [shaped(nodes // 2, width)],
-            [*stacked, *[after(p, *firsts) for p in panels]],
+            [*stacked, *[after(p, *sent) for p in panels]],
         )[0]
         for odd in (1, 0)
     ]
-    kept, got, _ = scatter_halving(*backs, "ta", ta, nodes_here)
+    backs[0] = after(backs[0], backs[1], shares[1], shares[2], message, owned[2]) if direct else backs[0]
+    kept, got, early = scatter_halving(*backs, "ta", ta, nodes_here)
+    if direct:
+        wait = [owned[2]] + []
+        passed = total_of(shares[2], after(message, *wait), rows_here)
+        direct_got = swap(after(shares[1], message, *wait), "wa", wa, 1)
+        owned += [shares[0], direct_got, swap(passed, "wa", wa, 2)]
     back = (kept + got)[None]
     if direct:
-        owned[-1] = after(owned[-1], back)
         grads = local_call(
             functools.partial(join_body, chunks),
             [shaped(rows_here, columns)] * 3,

time: 127 us -> 119 us (0.937)
  waiting for transfers between devices: 60.3 us -> 50.2 us
    ppermute x18 -> x19, waiting for transfers between devices: 60.3 us -> 50.2 us  [swap(): return lax.ppermute(value, axis, [(i, i ^ step) for i in range(size)])]
    pallas_call x13 -> x15, Pallas kernels: 39.6 us -> 40.8 us  [local_call(): pl.pallas_call(body, out_shape=outs, in_specs=[smem] * len(scalars) + [vm...]
    ppermute x18 -> x19, starting transfers between devices: 20.9 us -> 21 us  [swap(): return lax.ppermute(value, axis, [(i, i ^ step) for i in range(size)])]
  transfers between devices with their start and end apart: 18 -> 19, of which waited for: 8 -> 10; matrix products, arithmetic and copies ran while one was open for 1% -> 1% of each run, Pallas kernels for 27% -> 34%
where the time goes in v3:
time: 119 us; the launch traced here: 118 us
  waiting for transfers between devices  50.2 us (42%)
  Pallas kernels  44 us (37%)
  starting transfers between devices  21 us (18%)
  other arithmetic  1.51 us (1%)
    ppermute x19, waiting for transfers between devices, swap(): return lax.ppermute(value, axis, [(i, i ^ step) for i in range(size)])  50.2 us
    pallas_call x15, Pallas kernels, local_call(): pl.pallas_call(body, out_shape=outs, in_specs=[smem] * len(scalars) + [vm...  40.8 us
    ppermute x19, starting transfers between devices, swap(): return lax.ppermute(value, axis, [(i, i ^ step) for i in range(size)])  21 us
    pallas_call x1, Pallas kernels, entry(): pl.pallas_call(functools.partial(body, parts), out_shape=[shaped(*o) for...  3.18 us
  transfers between devices with their start and end apart: 19, of which 10 were waited for; matrix products, arithmetic and copies ran while one was open for 1% of the time, Pallas kernels for 34%

profile of v3, /device:TPU:0, one launch (start us, length us, event | category | flops | bytes accessed | tf_op | source)
XLA Modules:
  0.0 118.3 jit_solution(12653227987839471946)
XLA Ops:
  0.6 0.0 copy-start
  0.6 0.7 pad_add_fusion.info
  1.3 3.2 %shard_map.102 = (f32[256,384]{1,0:T(8,128)}, f32[128,256]{1,0:T(8,128)}, f32[128,256]{1,0:T(8,128)}, f32[128,256]{1,0:T(8,128)}, f32[128,256]{1,0:T(8,128)}) custom-call(s32[3]{0:T(128)} %pad_add_fusion.info, s32[1,128]{1,0:T(1,128)} %bitcast.12, f32[128,1024]{1,0:T(8,128)} %bitcast.11, f32[256,256]{1,0:T(8,128)} %refs_1_.3, f32[256,256]{1,0:T(8,128)} %refs_2_.3, ...), custom_call_target="tpu_custom_call" | custom-call | tf_op jit(solution)/shard_map/pallas_call | solution.py:94
  4.5 2.9 %collective-permute-start.1 = (f32[128,1024]{1,0:T(8,128)}, f32[128,1024]{1,0:T(8,128)S(1)}, u32[]{:S(2)}, u32[]{:S(2)}) collective-permute-start(f32[128,1024]{1,0:T(8,128)} %bitcast.8), channel_id=1, source_target_pairs={{0,2},{1,3},{2,0},{3,1},{4,6},{5,7},{6,4},{7,5},{8,10},{9,11},{10,... | collective-permute-start | bytes 1572872 | tf_op jit(solution)/shard_map/ppermute | solution.py:61
  7.4 1.6 %collective-permute-start.2 = (f32[256,384]{1,0:T(8,128)}, f32[256,384]{1,0:T(8,128)S(1)}, u32[]{:S(2)}, u32[]{:S(2)}) collective-permute-start(f32[256,384]{1,0:T(8,128)} %get-tuple-element.35), channel_id=1, source_target_pairs={{0,4},{4,0},{8,12},{12,8},{1,5},{5,1},{9,13},{13,9},{2,6},{6,2},{1... | collective-permute-start | bytes 1179656 | tf_op jit(solution)/shard_map/ppermute | solution.py:61
  9.0 2.6 %collective-permute-start.4 = (f32[256,384]{1,0:T(8,128)}, f32[256,384]{1,0:T(8,128)S(1)}, u32[]{:S(2)}, u32[]{:S(2)}) collective-permute-start(f32[256,384]{1,0:T(8,128)} %get-tuple-element.35), channel_id=1, source_target_pairs={{0,8},{4,12},{8,0},{12,4},{1,9},{5,13},{9,1},{13,5},{2,10},{6,14},... | collective-permute-start | bytes 1179656 | tf_op jit(solution)/shard_map/ppermute | solution.py:61
  11.6 0.0 collective-permute-start
  11.6 14.9 %collective-permute-done.2.refs_4_ = f32[256,384]{1,0:T(8,128)S(1)} collective-permute-done((f32[256,384]{1,0:T(8,128)}, f32[256,384]{1,0:T(8,128)S(1)}, u32[]{:S(2)}, u32[]{:S(2)}) %collective-permute-start.2) | collective-permute-done | bytes 393248 | tf_op jit(solution)/shard_map/ppermute | solution.py:61
  26.5 0.0 collective-permute-done.1.refs_2_
  26.5 0.0 collective-permute-start.3
  26.5 2.4 %collective-permute-done.4.refs_5_ = f32[256,384]{1,0:T(8,128)S(1)} collective-permute-done((f32[256,384]{1,0:T(8,128)}, f32[256,384]{1,0:T(8,128)S(1)}, u32[]{:S(2)}, u32[]{:S(2)}) %collective-permute-start.4) | collective-permute-done | bytes 393248 | tf_op jit(solution)/shard_map/ppermute | solution.py:61
  28.9 0.4 collective-permute-start.5
  29.3 0.0 collective-permute-start.6
  29.3 0.5 collective-permute-start.7
  29.9 0.0 collective-permute-done.refs_1_
  29.9 1.3 %collective-permute-start.8 = (f32[128,256]{1,0:T(8,128)}, f32[128,256]{1,0:T(8,128)}, u32[]{:S(2)}, u32[]{:S(2)}) collective-permute-start(f32[128,256]{1,0:T(8,128)} %get-tuple-element.44), channel_id=1, source_target_pairs={{0,3},{1,2},{2,1},{3,0},{4,7},{5,6},{6,5},{7,4},{8,11},{9,10},{10,... | collective-permute-start | bytes 393224 | tf_op jit(solution)/shard_map/ppermute | solution.py:61
  31.2 0.8 copy.11.neighbours
  32.0 0.0 copy-start.5
  32.0 0.0 collective-permute-done.3.refs_3_
  32.0 1.6 %collective-permute-start.10 = (f32[256,384]{1,0:T(8,128)S(1)}, f32[256,384]{1,0:T(8,128)S(1)}, u32[]{:S(2)}, u32[]{:S(2)}) collective-permute-start(f32[256,384]{1,0:T(8,128)S(1)} %collective-permute-done.4.refs_5_), channel_id=1, source_target_pairs={{0,16},{16,0},{1,17},{17,1},{2,18},{18,2},{3,19},{19,3},{4,20},{20... | collective-permute-start | bytes 1179656 | tf_op jit(solution)/shard_map/ppermute | solution.py:61
  33.6 0.0 copy-done
  33.6 0.1 shard_map.103.refs_0_.x
  33.7 0.0 collective-permute-done.6.refs_8_
  33.7 0.6 collective-permute-start.9
  34.3 3.7 %collective-permute-done.5.refs_6_ = f32[256,384]{1,0:T(8,128)S(1)} collective-permute-done((f32[256,384]{1,0:T(8,128)S(1)}, f32[256,384]{1,0:T(8,128)S(1)}, u32[]{:S(2)}, u32[]{:S(2)}) %collective-permute-start.5) | collective-permute-done | bytes 393248 | tf_op jit(solution)/shard_map/ppermute | solution.py:61
  38.0 1.5 %collective-permute-start.11 = (f32[256,384]{1,0:T(8,128)S(1)}, f32[256,384]{1,0:T(8,128)S(1)}, u32[]{:S(2)}, u32[]{:S(2)}) collective-permute-start(f32[256,384]{1,0:T(8,128)S(1)} %collective-permute-done.5.refs_6_), channel_id=1, source_target_pairs={{0,16},{16,0},{1,17},{17,1},{2,18},{18,2},{3,19},{19,3},{4,20},{20... | collective-permute-start | bytes 1179656 | tf_op jit(solution)/shard_map/ppermute | solution.py:61
  39.6 0.0 collective-permute-done.7.refs_9_
  39.6 0.0 collective-permute-done.8.refs_10_
  39.6 0.0 copy-done.1
  39.6 0.0 copy-done.2
  39.6 0.0 copy-done.3
  39.6 0.0 copy-done.4
  39.6 0.0 copy-done.5
  39.6 10.2 %shard_map.104 = (f32[512,384]{1,0:T(8,128)S(1)}, f32[1024,384]{1,0:T(8,128)S(1)}) custom-call(s32[3]{0:T(128)S(1)} %copy-done.4, s32[4,2]{1,0:T(4,128)S(1)} %copy.11.neighbours, f32[512,1024]{1,0:T(8,128)S(1)} %shard_map.103.refs_0_.x, f32[256,256]{1,0:T(8,128)S(1)} %copy-done.1, f32[256,256]{1,0:T(8,128)S(1)} %copy-done.2, f32[256,256]{1,0:T(8,128)S(1)} %copy-done.3, ...), custom_call_target="tpu_custom_call" | custom-call | flops 6442450944 | bytes 25165824 | tf_op jit(solution)/shard_map/pallas_call | solution.py:45
  49.9 2.6 %collective-permute-done.9.refs_4_ = f32[256,384]{1,0:T(8,128)S(1)} collective-permute-done((f32[256,384]{1,0:T(8,128)S(1)}, f32[256,384]{1,0:T(8,128)S(1)}, u32[]{:S(2)}, u32[]{:S(2)}) %collective-permute-start.9) | collective-permute-done | bytes 393248 | tf_op jit(solution)/shard_map/ppermute | solution.py:61
  52.4 2.6 %shard_map.105 = f32[512,384]{1,0:T(8,128)S(1)} custom-call(s32[3]{0:T(128)S(1)} %copy-done.4, f32[512,1024]{1,0:T(8,128)S(1)} %shard_map.103.refs_0_.x, f32[512,384]{1,0:T(8,128)S(1)} %get-tuple-element.45.stacked.refs_0_), custom_call_target="tpu_custom_call" | custom-call | tf_op jit(solution)/shard_map/pallas_call | solution.py:45
  55.1 1.7 %collective-permute-start.12 = (f32[512,384]{1,0:T(8,128)S(1)}, f32[512,384]{1,0:T(8,128)S(1)}, u32[]{:S(2)}, u32[]{:S(2)}) collective-permute-start(f32[512,384]{1,0:T(8,128)S(1)} %shard_map.105), channel_id=1, source_target_pairs={{0,4},{4,0},{8,12},{12,8},{1,5},{5,1},{9,13},{13,9},{2,6},{6,2},{1... | collective-permute-start | bytes 2359304 | tf_op jit(solution)/shard_map/ppermute | solution.py:61
  56.7 2.4 %shard_map.112.kept.refs_0_ = f32[512,384]{1,0:T(8,128)S(1)} custom-call(s32[3]{0:T(128)S(1)} %copy-done.4, f32[512,1024]{1,0:T(8,128)S(1)} %shard_map.103.refs_0_.x, f32[512,384]{1,0:T(8,128)S(1)} %get-tuple-element.45.stacked.refs_0_), custom_call_target="tpu_custom_call" | custom-call | tf_op jit(solution)/shard_map/pallas_call | solution.py:45
  59.2 0.0 collective-permute-done.10.refs_5_
  59.2 1.0 collective-permute-done.11.refs_6_
  60.2 10.2 %shard_map.106 = (f32[512,384]{1,0:T(8,128)S(1)}, f32[1024,384]{1,0:T(8,128)S(1)}) custom-call(s32[3]{0:T(128)S(1)} %copy-done.4, s32[4,2]{1,0:T(4,128)S(1)} %copy.11.neighbours, f32[512,1024]{1,0:T(8,128)S(1)} %shard_map.103.refs_0_.x, f32[256,256]{1,0:T(8,128)S(1)} %copy-done.1, f32[256,256]{1,0:T(8,128)S(1)} %copy-done.2, f32[256,256]{1,0:T(8,128)S(1)} %copy-done.3, ...), custom_call_target="tpu_custom_call" | custom-call | flops 6442450944 | bytes 25165824 | tf_op jit(solution)/shard_map/pallas_call | solution.py:45
  70.5 1.6 %shard_map.107 = f32[256,384]{1,0:T(8,128)S(1)} custom-call(s32[3]{0:T(128)S(1)} %copy-done.4, f32[512,1024]{1,0:T(8,128)S(1)} %shard_map.103.refs_0_.x, f32[512,384]{1,0:T(8,128)S(1)} %get-tuple-element.48.stacked.refs_1_), custom_call_target="tpu_custom_call" | custom-call | tf_op jit(solution)/shard_map/pallas_call | solution.py:45
  72.1 1.3 %collective-permute-done.12.got.refs_1_ = f32[512,384]{1,0:T(8,128)S(1)} collective-permute-done((f32[512,384]{1,0:T(8,128)S(1)}, f32[512,384]{1,0:T(8,128)S(1)}, u32[]{:S(2)}, u32[]{:S(2)}) %collective-permute-start.12) | collective-permute-done | bytes 786464 | tf_op jit(solution)/shard_map/ppermute | solution.py:61
  73.4 0.1 shard_map.113
  73.4 2.7 %collective-permute-start.14 = (f32[256,384]{1,0:T(8,128)S(1)}, f32[256,384]{1,0:T(8,128)S(1)}, u32[]{:S(2)}, u32[]{:S(2)}) collective-permute-start(f32[256,384]{1,0:T(8,128)S(1)} %shard_map.113), channel_id=1, source_target_pairs={{0,8},{4,12},{8,0},{12,4},{1,9},{5,13},{9,1},{13,5},{2,10},{6,14},... | collective-permute-start | bytes 1179656 | tf_op jit(solution)/shard_map/ppermute | solution.py:61
  76.1 0.3 collective-permute-start.13
  76.4 3.5 %shard_map.108.keep = f32[256,1024]{1,0:T(8,128)S(1)} custom-call(f32[512,384]{1,0:T(8,128)S(1)} %get-tuple-element.45.stacked.refs_0_, f32[512,384]{1,0:T(8,128)S(1)} %get-tuple-element.48.stacked.refs_1_, f32[1024,384]{1,0:T(8,128)S(1)} %get-tuple-element.50.refs_2_, f32[1024,384]{1,0:T(8,128)S(1)} %get-tuple-element.52.refs_3_), custom_call_target="tpu_custom_call" | custom-call | tf_op jit(solution)/shard_map/pallas_call | solution.py:45
  79.9 3.5 %shard_map.109 = f32[256,1024]{1,0:T(8,128)S(1)} custom-call(f32[512,384]{1,0:T(8,128)S(1)} %get-tuple-element.45.stacked.refs_0_, f32[512,384]{1,0:T(8,128)S(1)} %get-tuple-element.48.stacked.refs_1_, f32[1024,384]{1,0:T(8,128)S(1)} %get-tuple-element.50.refs_2_, f32[1024,384]{1,0:T(8,128)S(1)} %get-tuple-element.52.refs_3_), custom_call_target="tpu_custom_call" | custom-call | tf_op jit(solution)/shard_map/pallas_call | solution.py:45
  83.5 1.6 %shard_map.110 = f32[256,384]{1,0:T(8,128)S(1)} custom-call(s32[3]{0:T(128)S(1)} %copy-done.4, f32[512,1024]{1,0:T(8,128)S(1)} %shard_map.103.refs_0_.x, f32[512,384]{1,0:T(8,128)S(1)} %get-tuple-element.48.stacked.refs_1_), custom_call_target="tpu_custom_call" | custom-call | tf_op jit(solution)/shard_map/pallas_call | solution.py:45
  85.0 1.6 %shard_map.111.kept = f32[256,384]{1,0:T(8,128)S(1)} custom-call(s32[3]{0:T(128)S(1)} %copy-done.4, f32[512,1024]{1,0:T(8,128)S(1)} %shard_map.103.refs_0_.x, f32[512,384]{1,0:T(8,128)S(1)} %get-tuple-element.48.stacked.refs_1_), custom_call_target="tpu_custom_call" | custom-call | tf_op jit(solution)/shard_map/pallas_call | solution.py:45
  86.6 5.5 %collective-permute-done.14.refs_2_ = f32[256,384]{1,0:T(8,128)S(1)} collective-permute-done((f32[256,384]{1,0:T(8,128)S(1)}, f32[256,384]{1,0:T(8,128)S(1)}, u32[]{:S(2)}, u32[]{:S(2)}) %collective-permute-start.14) | collective-permute-done | bytes 393248 | tf_op jit(solution)/shard_map/ppermute | solution.py:61
  92.1 0.2 collective-permute-done.13.got
  92.3 0.0 collective-permute-start.15
  92.3 2.7 %collective-permute-done.15.got = f32[256,1024]{1,0:T(8,128)S(1)} collective-permute-done((f32[256,1024]{1,0:T(8,128)S(1)}, f32[256,1024]{1,0:T(8,128)S(1)}, u32[]{:S(2)}, u32[]{:S(2)}) %collective-permute-start.15) | collective-permute-done | bytes 1048608 | tf_op jit(solution)/shard_map/ppermute | solution.py:61
  94.9 0.1 shard_map.114
  95.0 0.6 collective-permute-start.16
  95.7 1.4 %collective-permute-start.18 = (f32[256,384]{1,0:T(8,128)S(1)}, f32[256,384]{1,0:T(8,128)S(1)}, u32[]{:S(2)}, u32[]{:S(2)}) collective-permute-start(f32[256,384]{1,0:T(8,128)S(1)} %shard_map.116), channel_id=1, source_target_pairs={{0,8},{4,12},{8,0},{12,4},{1,9},{5,13},{9,1},{13,5},{2,10},{6,14},... | collective-permute-start | bytes 1179656 | tf_op jit(solution)/shard_map/ppermute | solution.py:61
  97.1 1.3 %collective-permute-start.17 = (f32[256,384]{1,0:T(8,128)S(1)}, f32[256,384]{1,0:T(8,128)S(1)}, u32[]{:S(2)}, u32[]{:S(2)}) collective-permute-start(f32[256,384]{1,0:T(8,128)S(1)} %shard_map.110), channel_id=1, source_target_pairs={{0,4},{4,0},{8,12},{12,8},{1,5},{5,1},{9,13},{13,9},{2,6},{6,2},{1... | collective-permute-start | bytes 1179656 | tf_op jit(solution)/shard_map/ppermute | solution.py:61
  98.4 1.6 %shard_map.115.refs_3_ = f32[256,384]{1,0:T(8,128)S(1)} custom-call(s32[3]{0:T(128)S(1)} %copy-done.4, f32[512,1024]{1,0:T(8,128)S(1)} %shard_map.103.refs_0_.x, f32[512,384]{1,0:T(8,128)S(1)} %get-tuple-element.48.stacked.refs_1_), custom_call_target="tpu_custom_call" | custom-call | tf_op jit(solution)/shard_map/pallas_call | solution.py:45
  100.0 16.0 %collective-permute-done.18.refs_5_ = f32[256,384]{1,0:T(8,128)S(1)} collective-permute-done((f32[256,384]{1,0:T(8,128)S(1)}, f32[256,384]{1,0:T(8,128)S(1)}, u32[]{:S(2)}, u32[]{:S(2)}) %collective-permute-start.18) | collective-permute-done | bytes 393248 | tf_op jit(solution)/shard_map/ppermute | solution.py:61
  115.9 0.0 collective-permute-done.17.refs_4_
  115.9 1.5 %shard_map.117 = (f32[256,256]{1,0:T(8,128)}, f32[256,256]{1,0:T(8,128)}, f32[256,256]{1,0:T(8,128)}) custom-call(s32[3]{0:T(128)S(1)} %copy-done.4, f32[512,384]{1,0:T(8,128)S(1)} %shard_map.112.kept.refs_0_, f32[512,384]{1,0:T(8,128)S(1)} %collective-permute-done.12.got.refs_1_, f32[256,384]{1,0:T(8,128)S(1)} %collective-permute-done.14.refs_2_, ...), custom_call_target="tpu_custom_call" | custom-call | tf_op jit(solution)/shard_map/pallas_call | solution.py:45
  117.5 0.0 collective-permute-done.16
  117.5 0.9 add_bitcast_fusion
  (5 shorter events, 0.0 us)
Async XLA Ops:
  0.6 33.0 %copy-start = (f32[1,128,1024]{2,1,0:T(8,128)S(1)}, f32[1,128,1024]{2,1,0:T(8,128)}, u32[]{:S(2)}) copy-start(f32[1,128,1024]{2,1,0:T(8,128)} %param.7) | copy-start | bytes 1572868
  4.5 22.0 %collective-permute-start.1 = (f32[128,1024]{1,0:T(8,128)}, f32[128,1024]{1,0:T(8,128)S(1)}, u32[]{:S(2)}, u32[]{:S(2)}) collective-permute-start(f32[128,1024]{1,0:T(8,128)} %bitcast.8), channel_id=1, source_target_pairs={{0,2},{1,3},{2,0},{3,1},{4,6},{5,7},{6,4},{7,5},{8,10},{9,11},{10,... | collective-permute-start | bytes 1572872 | tf_op jit(solution)/shard_map/ppermute | solution.py:61
  7.4 19.1 %collective-permute-start.2 = (f32[256,384]{1,0:T(8,128)}, f32[256,384]{1,0:T(8,128)S(1)}, u32[]{:S(2)}, u32[]{:S(2)}) collective-permute-start(f32[256,384]{1,0:T(8,128)} %get-tuple-element.35), channel_id=1, source_target_pairs={{0,4},{4,0},{8,12},{12,8},{1,5},{5,1},{9,13},{13,9},{2,6},{6,2},{1... | collective-permute-start | bytes 1179656 | tf_op jit(solution)/shard_map/ppermute | solution.py:61
  9.0 19.9 %collective-permute-start.4 = (f32[256,384]{1,0:T(8,128)}, f32[256,384]{1,0:T(8,128)S(1)}, u32[]{:S(2)}, u32[]{:S(2)}) collective-permute-start(f32[256,384]{1,0:T(8,128)} %get-tuple-element.35), channel_id=1, source_target_pairs={{0,8},{4,12},{8,0},{12,4},{1,9},{5,13},{9,1},{13,5},{2,10},{6,14},... | collective-permute-start | bytes 1179656 | tf_op jit(solution)/shard_map/ppermute | solution.py:61
  11.6 18.3 %collective-permute-start = (f32[128,1024]{1,0:T(8,128)}, f32[128,1024]{1,0:T(8,128)S(1)}, u32[]{:S(2)}, u32[]{:S(2)}) collective-permute-start(f32[128,1024]{1,0:T(8,128)} %bitcast.9), channel_id=1, source_target_pairs={{0,1},{1,0},{2,3},{3,2},{4,5},{5,4},{6,7},{7,6},{8,9},{9,8},{10,11... | collective-permute-start | bytes 1572872 | tf_op jit(solution)/shard_map/ppermute | solution.py:61
  26.5 5.5 %collective-permute-start.3 = (f32[128,1024]{1,0:T(8,128)S(1)}, f32[128,1024]{1,0:T(8,128)S(1)}, u32[]{:S(2)}, u32[]{:S(2)}) collective-permute-start(f32[128,1024]{1,0:T(8,128)S(1)} %collective-permute-done.1.refs_2_), channel_id=1, source_target_pairs={{0,1},{1,0},{2,3},{3,2},{4,5},{5,4},{6,7},{7,6},{8,9},{9,8},{10,11... | collective-permute-start | bytes 1572872 | tf_op jit(solution)/shard_map/ppermute | solution.py:61
  28.9 9.1 %collective-permute-start.5 = (f32[256,384]{1,0:T(8,128)S(1)}, f32[256,384]{1,0:T(8,128)S(1)}, u32[]{:S(2)}, u32[]{:S(2)}) collective-permute-start(f32[256,384]{1,0:T(8,128)S(1)} %collective-permute-done.4.refs_5_), channel_id=1, source_target_pairs={{0,4},{4,0},{8,12},{12,8},{1,5},{5,1},{9,13},{13,9},{2,6},{6,2},{1... | collective-permute-start | bytes 1179656 | tf_op jit(solution)/shard_map/ppermute | solution.py:61
  29.3 4.4 %collective-permute-start.6 = (f32[128,256]{1,0:T(8,128)}, f32[128,256]{1,0:T(8,128)S(1)}, u32[]{:S(2)}, u32[]{:S(2)}) collective-permute-start(f32[128,256]{1,0:T(8,128)} %get-tuple-element.40), channel_id=1, source_target_pairs={{0,1},{1,0},{2,3},{3,2},{4,5},{5,4},{6,7},{7,6},{8,9},{9,8},{10,11... | collective-permute-start | bytes 393224 | tf_op jit(solution)/shard_map/ppermute | solution.py:61
  29.3 10.2 %collective-permute-start.7 = (f32[128,256]{1,0:T(8,128)}, f32[128,256]{1,0:T(8,128)S(1)}, u32[]{:S(2)}, u32[]{:S(2)}) collective-permute-start(f32[128,256]{1,0:T(8,128)} %get-tuple-element.42), channel_id=1, source_target_pairs={{0,2},{1,3},{2,0},{3,1},{4,6},{5,7},{6,4},{7,5},{8,10},{9,11},{10,... | collective-permute-start | bytes 393224 | tf_op jit(solution)/shard_map/ppermute | solution.py:61
  29.9 9.7 %collective-permute-start.8 = (f32[128,256]{1,0:T(8,128)}, f32[128,256]{1,0:T(8,128)}, u32[]{:S(2)}, u32[]{:S(2)}) collective-permute-start(f32[128,256]{1,0:T(8,128)} %get-tuple-element.44), channel_id=1, source_target_pairs={{0,3},{1,2},{2,1},{3,0},{4,7},{5,6},{6,5},{7,4},{8,11},{9,10},{10,... | collective-permute-start | bytes 393224 | tf_op jit(solution)/shard_map/ppermute | solution.py:61
  32.0 7.6 %copy-start.1 = (f32[256,256]{1,0:T(8,128)S(1)}, f32[256,256]{1,0:T(8,128)}, u32[]{:S(2)}) copy-start(f32[256,256]{1,0:T(8,128)} %refs_1_.3) | copy-start | bytes 786436
  32.0 7.6 %copy-start.2 = (f32[256,256]{1,0:T(8,128)S(1)}, f32[256,256]{1,0:T(8,128)}, u32[]{:S(2)}) copy-start(f32[256,256]{1,0:T(8,128)} %refs_2_.3) | copy-start | bytes 786436
  32.0 7.6 %copy-start.3 = (f32[256,256]{1,0:T(8,128)S(1)}, f32[256,256]{1,0:T(8,128)}, u32[]{:S(2)}) copy-start(f32[256,256]{1,0:T(8,128)} %refs_3_.3) | copy-start | bytes 786436
  32.0 7.6 %copy-start.4 = (s32[3]{0:T(128)S(1)}, s32[3]{0:T(128)}, u32[]{:S(2)}) copy-start(s32[3]{0:T(128)} %pad_add_fusion.info) | copy-start | bytes 40
  32.0 7.6 %copy-start.5 = (f32[128,256]{1,0:T(8,128)S(1)}, f32[128,256]{1,0:T(8,128)}, u32[]{:S(2)}) copy-start(f32[128,256]{1,0:T(8,128)} %get-tuple-element.38.refs_7_) | copy-start | bytes 393220
  32.0 27.2 %collective-permute-start.10 = (f32[256,384]{1,0:T(8,128)S(1)}, f32[256,384]{1,0:T(8,128)S(1)}, u32[]{:S(2)}, u32[]{:S(2)}) collective-permute-start(f32[256,384]{1,0:T(8,128)S(1)} %collective-permute-done.4.refs_5_), channel_id=1, source_target_pairs={{0,16},{16,0},{1,17},{17,1},{2,18},{18,2},{3,19},{19,3},{4,20},{20... | collective-permute-start | bytes 1179656 | tf_op jit(solution)/shard_map/ppermute | solution.py:61
  33.7 18.7 %collective-permute-start.9 = (f32[256,384]{1,0:T(8,128)S(1)}, f32[256,384]{1,0:T(8,128)S(1)}, u32[]{:S(2)}, u32[]{:S(2)}) collective-permute-start(f32[256,384]{1,0:T(8,128)S(1)} %collective-permute-done.2.refs_4_), channel_id=1, source_target_pairs={{0,16},{16,0},{1,17},{17,1},{2,18},{18,2},{3,19},{19,3},{4,20},{20... | collective-permute-start | bytes 1179656 | tf_op jit(solution)/shard_map/ppermute | solution.py:61
  38.0 22.2 %collective-permute-start.11 = (f32[256,384]{1,0:T(8,128)S(1)}, f32[256,384]{1,0:T(8,128)S(1)}, u32[]{:S(2)}, u32[]{:S(2)}) collective-permute-start(f32[256,384]{1,0:T(8,128)S(1)} %collective-permute-done.5.refs_6_), channel_id=1, source_target_pairs={{0,16},{16,0},{1,17},{17,1},{2,18},{18,2},{3,19},{19,3},{4,20},{20... | collective-permute-start | bytes 1179656 | tf_op jit(solution)/shard_map/ppermute | solution.py:61
  55.1 18.3 %collective-permute-start.12 = (f32[512,384]{1,0:T(8,128)S(1)}, f32[512,384]{1,0:T(8,128)S(1)}, u32[]{:S(2)}, u32[]{:S(2)}) collective-permute-start(f32[512,384]{1,0:T(8,128)S(1)} %shard_map.105), channel_id=1, source_target_pairs={{0,4},{4,0},{8,12},{12,8},{1,5},{5,1},{9,13},{13,9},{2,6},{6,2},{1... | collective-permute-start | bytes 2359304 | tf_op jit(solution)/shard_map/ppermute | solution.py:61
  73.4 18.7 %collective-permute-start.14 = (f32[256,384]{1,0:T(8,128)S(1)}, f32[256,384]{1,0:T(8,128)S(1)}, u32[]{:S(2)}, u32[]{:S(2)}) collective-permute-start(f32[256,384]{1,0:T(8,128)S(1)} %shard_map.113), channel_id=1, source_target_pairs={{0,8},{4,12},{8,0},{12,4},{1,9},{5,13},{9,1},{13,5},{2,10},{6,14},... | collective-permute-start | bytes 1179656 | tf_op jit(solution)/shard_map/ppermute | solution.py:61
  76.1 16.2 %collective-permute-start.13 = (f32[256,384]{1,0:T(8,128)S(1)}, f32[256,384]{1,0:T(8,128)S(1)}, u32[]{:S(2)}, u32[]{:S(2)}) collective-permute-start(f32[256,384]{1,0:T(8,128)S(1)} %shard_map.107), channel_id=1, source_target_pairs={{0,4},{4,0},{8,12},{12,8},{1,5},{5,1},{9,13},{13,9},{2,6},{6,2},{1... | collective-permute-start | bytes 1179656 | tf_op jit(solution)/shard_map/ppermute | solution.py:61
  92.3 2.7 %collective-permute-start.15 = (f32[256,1024]{1,0:T(8,128)S(1)}, f32[256,1024]{1,0:T(8,128)S(1)}, u32[]{:S(2)}, u32[]{:S(2)}) collective-permute-start(f32[256,1024]{1,0:T(8,128)S(1)} %shard_map.109), channel_id=1, source_target_pairs={{0,1},{1,0},{2,3},{3,2},{4,5},{5,4},{6,7},{7,6},{8,9},{9,8},{10,11... | collective-permute-start | bytes 3145736 | tf_op jit(solution)/shard_map/ppermute | solution.py:61
  95.0 22.4 %collective-permute-start.16 = (f32[128,1024]{1,0:T(8,128)S(1)}, f32[128,1024]{1,0:T(8,128)S(1)}, u32[]{:S(2)}, u32[]{:S(2)}) collective-permute-start(f32[128,1024]{1,0:T(8,128)S(1)} %get-tuple-element.59), channel_id=1, source_target_pairs={{0,2},{1,3},{2,0},{3,1},{4,6},{5,7},{6,4},{7,5},{8,10},{9,11},{10,... | collective-permute-start | bytes 1572872 | tf_op jit(solution)/shard_map/ppermute | solution.py:61
  95.7 20.3 %collective-permute-start.18 = (f32[256,384]{1,0:T(8,128)S(1)}, f32[256,384]{1,0:T(8,128)S(1)}, u32[]{:S(2)}, u32[]{:S(2)}) collective-permute-start(f32[256,384]{1,0:T(8,128)S(1)} %shard_map.116), channel_id=1, source_target_pairs={{0,8},{4,12},{8,0},{12,4},{1,9},{5,13},{9,1},{13,5},{2,10},{6,14},... | collective-permute-start | bytes 1179656 | tf_op jit(solution)/shard_map/ppermute | solution.py:61
  97.1 18.8 %collective-permute-start.17 = (f32[256,384]{1,0:T(8,128)S(1)}, f32[256,384]{1,0:T(8,128)S(1)}, u32[]{:S(2)}, u32[]{:S(2)}) collective-permute-start(f32[256,384]{1,0:T(8,128)S(1)} %shard_map.110), channel_id=1, source_target_pairs={{0,4},{4,0},{8,12},{12,8},{1,5},{5,1},{9,13},{13,9},{2,6},{6,2},{1... | collective-permute-start | bytes 1179656 | tf_op jit(solution)/shard_map/ppermute | solution.py:61

commit v4 on v3

--- a/solution.py
+++ b/solution.py
@@ -10,7 +10,7 @@
 DH = 64
 BLOCK = 128
 KB = 2
-GATE = (1,)
+GATE = ()
 LANES = 128
 F32 = jnp.float32
 NN = ((1,), (0,))
@@ -154,6 +154,23 @@
     )
 
 
+BF16 = jnp.bfloat16
+
+
+def halves_of(value):
+    high = value.astype(BF16)
+    return high, (value - high.astype(F32)).astype(BF16)
+
+
+def dot_halves(left, right, dims):
+    (high, low), (high_right, low_right) = left, right
+
+    def term(one, other):
+        return lax.dot_general(one, other, (dims, ((), ())), preferred_element_type=F32)
+
+    return (term(high, low_right) + term(low, high_right)) + term(high, high_right)
+
+
 def attention_core(cols, blocks, t, neighbours, x, panel, adjoints, out, proj):
     proj[...] = dot(x[...], panel[...], NN)
     out[:, LANES:] = jnp.zeros((out.shape[0], 2 * LANES), F32)
@@ -165,27 +182,35 @@
             [jnp.where(first, value, 0.0), jnp.where(first, 0.0, value)], axis=0
         )
 
-    for r in range(blocks):
-        here = slice(r * BLOCK, (r + 1) * BLOCK)
-        there = [
+    every = range(blocks)
+    here = [slice(r * BLOCK, (r + 1) * BLOCK) for r in every]
+    there = [
+        [
             pl.ds(pl.multiple_of((neighbours[t ^ r, j] ^ t) * BLOCK, BLOCK), BLOCK)
             for j in range(KB)
         ]
-        query = by_head(proj[here, 0:LANES])
-        adjoint = by_head(adjoints[r][:, cols])
-        key = jnp.concatenate([proj[w, LANES : 2 * LANES] for w in there], axis=0)
-        value = jnp.concatenate([proj[w, 2 * LANES :] for w in there], axis=0)
-        scores = dot(query, key, NT) * scale
-        raised = jnp.exp(scores - jnp.max(scores, axis=1, keepdims=True))
-        attention = raised / jnp.sum(raised, axis=1, keepdims=True)
-        weight_adjoint = dot(adjoint, value, NT)
-        row_dots = jnp.sum(attention * weight_adjoint, axis=1, keepdims=True)
-        score_adjoint = attention * (weight_adjoint - row_dots) * scale
-        both = dot(score_adjoint, key, NN)
-        out[here, 0:LANES] = jnp.where(first, both[:BLOCK], both[BLOCK:])
-        dkey = dot(score_adjoint, query, TN)
-        dvalue = dot(attention, adjoint, TN)
-        for j, w in enumerate(there):
+        for r in every
+    ]
+    query = [by_head(proj[here[r], 0:LANES]) for r in every]
+    adjoint = [by_head(adjoints[r][:, cols]) for r in every]
+    key = [jnp.concatenate([proj[w, LANES : 2 * LANES] for w in there[r]], axis=0) for r in every]
+    value = [jnp.concatenate([proj[w, 2 * LANES :] for w in there[r]], axis=0) for r in every]
+    scores = [dot(query[r], key[r], NT) * scale for r in every]
+    weight_adjoint = [dot(adjoint[r], value[r], NT) for r in every]
+    raised = [jnp.exp(s - jnp.max(s, axis=1, keepdims=True)) for s in scores]
+    attention = [v / jnp.sum(v, axis=1, keepdims=True) for v in raised]
+    row_dots = [
+        jnp.sum(attention[r] * weight_adjoint[r], axis=1, keepdims=True) for r in every
+    ]
+    score_adjoint = [
+        halves_of(attention[r] * (weight_adjoint[r] - row_dots[r]) * scale) for r in every
+    ]
+    for r in every:
+        dvalue = dot_halves(halves_of(attention[r]), halves_of(adjoint[r]), TN)
+        both = dot_halves(score_adjoint[r], halves_of(key[r]), NN)
+        out[here[r], 0:LANES] = jnp.where(first, both[:BLOCK], both[BLOCK:])
+        dkey = dot_halves(score_adjoint[r], halves_of(query[r]), TN)
+        for j, w in enumerate(there[r]):
             part = slice(j * BLOCK, (j + 1) * BLOCK)
             out[w, LANES : 2 * LANES] += dkey[part]
             out[w, 2 * LANES :] += dvalue[part]
@@ -271,7 +296,7 @@
         held[ta // 2] = after(swap(held[0], "ta", ta, ta // 2), gathered[0][1])
     held = spread(held, "ta", ta)
     adjoints = [blocks_out[0]] + [
-        swap(after(blocks_out[r], held[ta // 2]), "ta", ta, r) for r in range(1, ta)
+        swap(after(blocks_out[r], *[held[q] for q in range(1, ta)]), "ta", ta, r) for r in range(1, ta)
     ]
     inputs = local_call(
         functools.partial(stack_body, ta), [shaped(nodes, width)], [held[r] for r in range(ta)]
@@ -282,6 +307,8 @@
         proj_flops = 12 * nodes * width * 3 * LANES + 60 * 2 * nodes * 4 * BLOCK * LANES
         scratch = [pltpu.VMEM((nodes, 3 * LANES), F32)]
         turn = after(info, stacked[-1], *sent) if stacked else info
+        if direct and not c:
+            turn = after(turn, gathered[1][1])
         if direct:
             dqkv, panel = local_call(
                 functools.partial(attention_body, c, blocks, wa),
@@ -298,7 +325,7 @@
                 got = swap(odd, "wa", wa, 1)
                 passed = total_of(even, got, rows_here)
                 owned = [even, got, swap(passed, "wa", wa, 2)]
-                sent = [odd]
+                sent = [odd, even]
             else:
                 shares = {}
                 for r in (3, 1, 2, 0):
@@ -323,7 +350,7 @@
 
     if direct:
         (shares,) = ready
-        message = swap(after(shares[3], owned[1]), "wa", wa, 1)
+        message = swap(shares[3], "wa", wa, 1)
         sent = [shares[3]]
     backs = [
         local_call(
@@ -333,12 +360,11 @@
         )[0]
         for odd in (1, 0)
     ]
-    backs[0] = after(backs[0], backs[1], shares[1], shares[2], message, owned[2]) if direct else backs[0]
     kept, got, early = scatter_halving(*backs, "ta", ta, nodes_here)
     if direct:
-        wait = [owned[2]] + []
+        wait = [owned[2]] + ([early] if early is not None else [])
         passed = total_of(shares[2], after(message, *wait), rows_here)
-        direct_got = swap(after(shares[1], message, *wait), "wa", wa, 1)
+        direct_got = swap(after(shares[1], message), "wa", wa, 1)
         owned += [shares[0], direct_got, swap(passed, "wa", wa, 2)]
     back = (kept + got)[None]
     if direct:

time: 119 us -> 113 us (0.950)
  Pallas kernels: 44 us -> 39.5 us
  starting transfers between devices: 21 us -> 17.9 us
  waiting for transfers between devices: 50.2 us -> 52.2 us
    pallas_call x15, Pallas kernels: 40.8 us -> 36.3 us  [local_call(): pl.pallas_call(body, out_shape=outs, in_specs=[smem] * len(scalars) + [vm...]
    ppermute x19, starting transfers between devices: 21 us -> 17.9 us  [swap(): return lax.ppermute(value, axis, [(i, i ^ step) for i in range(size)])]
    ppermute x19, waiting for transfers between devices: 50.2 us -> 52.2 us  [swap(): return lax.ppermute(value, axis, [(i, i ^ step) for i in range(size)])]
  transfers between devices with their start and end apart: 19 -> 19, of which waited for: 10 -> 8; matrix products, arithmetic and copies ran while one was open for 1% -> 1% of each run, Pallas kernels for 34% -> 32%
where the time goes in v4:
time: 113 us
  waiting for transfers between devices  52.2 us (46%)
  Pallas kernels  39.5 us (35%)
  starting transfers between devices  17.9 us (16%)
  other arithmetic  1.52 us (1%)
    ppermute x19, waiting for transfers between devices, swap(): return lax.ppermute(value, axis, [(i, i ^ step) for i in range(size)])  52.2 us
    pallas_call x15, Pallas kernels, local_call(): pl.pallas_call(body, out_shape=outs, in_specs=[smem] * len(scalars) + [vm...  36.3 us
    ppermute x19, starting transfers between devices, swap(): return lax.ppermute(value, axis, [(i, i ^ step) for i in range(size)])  17.9 us
    pallas_call x1, Pallas kernels, entry(): pl.pallas_call(functools.partial(body, parts), out_shape=[shaped(*o) for...  3.2 us
  transfers between devices with their start and end apart: 19, of which 8 were waited for; matrix products, arithmetic and copies ran while one was open for 1% of the time, Pallas kernels for 32%

profile of v4, /device:TPU:0, one launch (start us, length us, event | category | flops | bytes accessed | tf_op | source)
XLA Modules:
  0.0 112.8 jit_solution(2294097542002219701)
XLA Ops:
  0.6 0.0 copy-start
  0.6 0.6 pad_add_fusion.info
  1.3 3.2 %shard_map.102 = (f32[256,384]{1,0:T(8,128)}, f32[128,256]{1,0:T(8,128)}, f32[128,256]{1,0:T(8,128)}, f32[128,256]{1,0:T(8,128)}, f32[128,256]{1,0:T(8,128)}) custom-call(s32[3]{0:T(128)} %pad_add_fusion.info, s32[1,128]{1,0:T(1,128)} %bitcast.12, f32[128,1024]{1,0:T(8,128)} %bitcast.11, f32[256,256]{1,0:T(8,128)} %refs_1_.3, f32[256,256]{1,0:T(8,128)} %refs_2_.3, ...), custom_call_target="tpu_custom_call" | custom-call | tf_op jit(solution)/shard_map/pallas_call | solution.py:94
  4.5 2.9 %collective-permute-start.3 = (f32[128,1024]{1,0:T(8,128)}, f32[128,1024]{1,0:T(8,128)S(1)}, u32[]{:S(2)}, u32[]{:S(2)}) collective-permute-start(f32[128,1024]{1,0:T(8,128)} %bitcast.8), channel_id=1, source_target_pairs={{0,2},{1,3},{2,0},{3,1},{4,6},{5,7},{6,4},{7,5},{8,10},{9,11},{10,... | collective-permute-start | bytes 1572872 | tf_op jit(solution)/shard_map/ppermute | solution.py:61
  7.4 1.6 %collective-permute-start = (f32[256,384]{1,0:T(8,128)}, f32[256,384]{1,0:T(8,128)S(1)}, u32[]{:S(2)}, u32[]{:S(2)}) collective-permute-start(f32[256,384]{1,0:T(8,128)} %get-tuple-element.34), channel_id=1, source_target_pairs={{0,4},{4,0},{8,12},{12,8},{1,5},{5,1},{9,13},{13,9},{2,6},{6,2},{1... | collective-permute-start | bytes 1179656 | tf_op jit(solution)/shard_map/ppermute | solution.py:61
  9.0 2.6 %collective-permute-start.5 = (f32[256,384]{1,0:T(8,128)}, f32[256,384]{1,0:T(8,128)S(1)}, u32[]{:S(2)}, u32[]{:S(2)}) collective-permute-start(f32[256,384]{1,0:T(8,128)} %get-tuple-element.34), channel_id=1, source_target_pairs={{0,8},{4,12},{8,0},{12,4},{1,9},{5,13},{9,1},{13,5},{2,10},{6,14},... | collective-permute-start | bytes 1179656 | tf_op jit(solution)/shard_map/ppermute | solution.py:61
  11.6 0.0 collective-permute-start.2
  11.6 14.9 %collective-permute-done.refs_4_ = f32[256,384]{1,0:T(8,128)S(1)} collective-permute-done((f32[256,384]{1,0:T(8,128)}, f32[256,384]{1,0:T(8,128)S(1)}, u32[]{:S(2)}, u32[]{:S(2)}) %collective-permute-start) | collective-permute-done | bytes 393248 | tf_op jit(solution)/shard_map/ppermute | solution.py:61
  26.5 0.0 collective-permute-done.3.refs_2_
  26.5 0.0 collective-permute-start.4
  26.5 1.5 %collective-permute-start.1 = (f32[256,384]{1,0:T(8,128)S(1)}, f32[256,384]{1,0:T(8,128)S(1)}, u32[]{:S(2)}, u32[]{:S(2)}) collective-permute-start(f32[256,384]{1,0:T(8,128)S(1)} %collective-permute-done.refs_4_), channel_id=1, source_target_pairs={{0,16},{16,0},{1,17},{17,1},{2,18},{18,2},{3,19},{19,3},{4,20},{20... | collective-permute-start | bytes 1179656 | tf_op jit(solution)/shard_map/ppermute | solution.py:61
  28.0 0.9 collective-permute-done.5.refs_5_
  28.9 0.4 collective-permute-start.6
  29.3 0.0 collective-permute-done.2.refs_1_
  29.3 0.0 collective-permute-done.4.refs_3_
  29.3 0.0 collective-permute-start.7
  29.4 0.6 collective-permute-start.8
  29.9 1.3 %collective-permute-start.9 = (f32[128,256]{1,0:T(8,128)}, f32[128,256]{1,0:T(8,128)}, u32[]{:S(2)}, u32[]{:S(2)}) collective-permute-start(f32[128,256]{1,0:T(8,128)} %get-tuple-element.44), channel_id=1, source_target_pairs={{0,3},{1,2},{2,1},{3,0},{4,7},{5,6},{6,5},{7,4},{8,11},{9,10},{10,... | collective-permute-start | bytes 393224 | tf_op jit(solution)/shard_map/ppermute | solution.py:61
  31.2 0.8 copy.11.neighbours
  32.0 0.0 copy-start.5
  32.0 6.1 %collective-permute-done.1.refs_4_ = f32[256,384]{1,0:T(8,128)S(1)} collective-permute-done((f32[256,384]{1,0:T(8,128)S(1)}, f32[256,384]{1,0:T(8,128)S(1)}, u32[]{:S(2)}, u32[]{:S(2)}) %collective-permute-start.1) | collective-permute-done | bytes 393248 | tf_op jit(solution)/shard_map/ppermute | solution.py:61
  38.1 1.5 %collective-permute-start.10 = (f32[256,384]{1,0:T(8,128)S(1)}, f32[256,384]{1,0:T(8,128)S(1)}, u32[]{:S(2)}, u32[]{:S(2)}) collective-permute-start(f32[256,384]{1,0:T(8,128)S(1)} %collective-permute-done.5.refs_5_), channel_id=1, source_target_pairs={{0,16},{16,0},{1,17},{17,1},{2,18},{18,2},{3,19},{19,3},{4,20},{20... | collective-permute-start | bytes 1179656 | tf_op jit(solution)/shard_map/ppermute | solution.py:61
  39.6 0.0 collective-permute-done.6.refs_6_
  39.6 0.5 collective-permute-start.11
  40.1 0.0 copy-done
  40.1 0.1 shard_map.103.refs_0_.x
  40.2 0.0 collective-permute-done.7.refs_8_
  40.2 0.0 collective-permute-done.8.refs_9_
  40.2 0.0 collective-permute-done.9.refs_10_
  40.3 0.0 copy-done.1
  40.3 0.0 copy-done.2
  40.3 0.0 copy-done.3
  40.3 0.0 copy-done.4
  40.3 0.0 copy-done.5
  40.3 8.0 %shard_map.104 = (f32[512,384]{1,0:T(8,128)S(1)}, f32[1024,384]{1,0:T(8,128)S(1)}) custom-call(s32[3]{0:T(128)S(1)} %copy-done.4, s32[4,2]{1,0:T(4,128)S(1)} %copy.11.neighbours, f32[512,1024]{1,0:T(8,128)S(1)} %shard_map.103.refs_0_.x, f32[256,256]{1,0:T(8,128)S(1)} %copy-done.1, f32[256,256]{1,0:T(8,128)S(1)} %copy-done.2, f32[256,256]{1,0:T(8,128)S(1)} %copy-done.3, ...), custom_call_target="tpu_custom_call" | custom-call | flops 6442450944 | bytes 25165824 | tf_op jit(solution)/shard_map/pallas_call | solution.py:45
  48.3 2.4 %shard_map.105 = f32[512,384]{1,0:T(8,128)S(1)} custom-call(s32[3]{0:T(128)S(1)} %copy-done.4, f32[512,1024]{1,0:T(8,128)S(1)} %shard_map.103.refs_0_.x, f32[512,384]{1,0:T(8,128)S(1)} %get-tuple-element.45.stacked.refs_0_), custom_call_target="tpu_custom_call" | custom-call | tf_op jit(solution)/shard_map/pallas_call | solution.py:45
  50.7 0.6 collective-permute-start.14
  51.3 2.4 %shard_map.106.kept.refs_0_ = f32[512,384]{1,0:T(8,128)S(1)} custom-call(s32[3]{0:T(128)S(1)} %copy-done.4, f32[512,1024]{1,0:T(8,128)S(1)} %shard_map.103.refs_0_.x, f32[512,384]{1,0:T(8,128)S(1)} %get-tuple-element.45.stacked.refs_0_), custom_call_target="tpu_custom_call" | custom-call | tf_op jit(solution)/shard_map/pallas_call | solution.py:45
  53.7 0.0 collective-permute-done.10.refs_5_
  53.7 3.6 %collective-permute-done.11.refs_6_ = f32[256,384]{1,0:T(8,128)S(1)} collective-permute-done((f32[256,384]{1,0:T(8,128)}, f32[256,384]{1,0:T(8,128)S(1)}, u32[]{:S(2)}, u32[]{:S(2)}) %collective-permute-start.11) | collective-permute-done | bytes 393248 | tf_op jit(solution)/shard_map/ppermute | solution.py:61
  57.3 8.0 %shard_map.107 = (f32[512,384]{1,0:T(8,128)S(1)}, f32[1024,384]{1,0:T(8,128)S(1)}) custom-call(s32[3]{0:T(128)S(1)} %copy-done.4, s32[4,2]{1,0:T(4,128)S(1)} %copy.11.neighbours, f32[512,1024]{1,0:T(8,128)S(1)} %shard_map.103.refs_0_.x, f32[256,256]{1,0:T(8,128)S(1)} %copy-done.1, f32[256,256]{1,0:T(8,128)S(1)} %copy-done.2, f32[256,256]{1,0:T(8,128)S(1)} %copy-done.3, ...), custom_call_target="tpu_custom_call" | custom-call | flops 6442450944 | bytes 25165824 | tf_op jit(solution)/shard_map/pallas_call | solution.py:45
  65.4 1.6 %shard_map.108 = f32[256,384]{1,0:T(8,128)S(1)} custom-call(s32[3]{0:T(128)S(1)} %copy-done.4, f32[512,1024]{1,0:T(8,128)S(1)} %shard_map.103.refs_0_.x, f32[512,384]{1,0:T(8,128)S(1)} %get-tuple-element.49.stacked.refs_1_), custom_call_target="tpu_custom_call" | custom-call | tf_op jit(solution)/shard_map/pallas_call | solution.py:45
  67.0 3.5 %shard_map.110 = f32[256,1024]{1,0:T(8,128)S(1)} custom-call(f32[512,384]{1,0:T(8,128)S(1)} %get-tuple-element.45.stacked.refs_0_, f32[512,384]{1,0:T(8,128)S(1)} %get-tuple-element.49.stacked.refs_1_, f32[1024,384]{1,0:T(8,128)S(1)} %get-tuple-element.51.refs_2_, f32[1024,384]{1,0:T(8,128)S(1)} %get-tuple-element.53.refs_3_), custom_call_target="tpu_custom_call" | custom-call | tf_op jit(solution)/shard_map/pallas_call | solution.py:45
  70.5 0.1 collective-permute-start.12
  70.6 0.1 collective-permute-start.16
  70.7 0.0 collective-permute-done.14.got.refs_1_
  70.7 0.1 shard_map.112
  70.7 3.1 %collective-permute-start.15 = (f32[256,384]{1,0:T(8,128)S(1)}, f32[256,384]{1,0:T(8,128)S(1)}, u32[]{:S(2)}, u32[]{:S(2)}) collective-permute-start(f32[256,384]{1,0:T(8,128)S(1)} %shard_map.112), channel_id=1, source_target_pairs={{0,8},{4,12},{8,0},{12,4},{1,9},{5,13},{9,1},{13,5},{2,10},{6,14},... | collective-permute-start | bytes 1179656 | tf_op jit(solution)/shard_map/ppermute | solution.py:61
  73.8 3.8 %shard_map.109.keep = f32[256,1024]{1,0:T(8,128)S(1)} custom-call(f32[512,384]{1,0:T(8,128)S(1)} %get-tuple-element.45.stacked.refs_0_, f32[512,384]{1,0:T(8,128)S(1)} %get-tuple-element.49.stacked.refs_1_, f32[1024,384]{1,0:T(8,128)S(1)} %get-tuple-element.51.refs_2_, f32[1024,384]{1,0:T(8,128)S(1)} %get-tuple-element.53.refs_3_), custom_call_target="tpu_custom_call" | custom-call | tf_op jit(solution)/shard_map/pallas_call | solution.py:45
  77.6 0.0 collective-permute-done.12.got
  77.6 0.1 shard_map.111
  77.7 0.6 collective-permute-start.13
  78.3 1.6 %shard_map.113 = f32[256,384]{1,0:T(8,128)S(1)} custom-call(s32[3]{0:T(128)S(1)} %copy-done.4, f32[512,1024]{1,0:T(8,128)S(1)} %shard_map.103.refs_0_.x, f32[512,384]{1,0:T(8,128)S(1)} %get-tuple-element.49.stacked.refs_1_), custom_call_target="tpu_custom_call" | custom-call | tf_op jit(solution)/shard_map/pallas_call | solution.py:45
  79.9 1.6 %shard_map.114.kept = f32[256,384]{1,0:T(8,128)S(1)} custom-call(s32[3]{0:T(128)S(1)} %copy-done.4, f32[512,1024]{1,0:T(8,128)S(1)} %shard_map.103.refs_0_.x, f32[512,384]{1,0:T(8,128)S(1)} %get-tuple-element.49.stacked.refs_1_), custom_call_target="tpu_custom_call" | custom-call | tf_op jit(solution)/shard_map/pallas_call | solution.py:45
  81.5 8.7 %collective-permute-done.16.got = f32[256,384]{1,0:T(8,128)S(1)} collective-permute-done((f32[256,384]{1,0:T(8,128)S(1)}, f32[256,384]{1,0:T(8,128)S(1)}, u32[]{:S(2)}, u32[]{:S(2)}) %collective-permute-start.16) | collective-permute-done | bytes 393248 | tf_op jit(solution)/shard_map/ppermute | solution.py:61
  90.2 0.0 collective-permute-start.17
  90.2 1.6 %collective-permute-done.15.refs_2_ = f32[256,384]{1,0:T(8,128)S(1)} collective-permute-done((f32[256,384]{1,0:T(8,128)S(1)}, f32[256,384]{1,0:T(8,128)S(1)}, u32[]{:S(2)}, u32[]{:S(2)}) %collective-permute-start.15) | collective-permute-done | bytes 393248 | tf_op jit(solution)/shard_map/ppermute | solution.py:61
  91.8 0.5 collective-permute-start.18
  92.3 1.6 %shard_map.115.refs_3_ = f32[256,384]{1,0:T(8,128)S(1)} custom-call(s32[3]{0:T(128)S(1)} %copy-done.4, f32[512,1024]{1,0:T(8,128)S(1)} %shard_map.103.refs_0_.x, f32[512,384]{1,0:T(8,128)S(1)} %get-tuple-element.49.stacked.refs_1_), custom_call_target="tpu_custom_call" | custom-call | tf_op jit(solution)/shard_map/pallas_call | solution.py:45
  93.9 14.1 %collective-permute-done.17.refs_4_ = f32[256,384]{1,0:T(8,128)S(1)} collective-permute-done((f32[256,384]{1,0:T(8,128)S(1)}, f32[256,384]{1,0:T(8,128)S(1)}, u32[]{:S(2)}, u32[]{:S(2)}) %collective-permute-start.17) | collective-permute-done | bytes 393248 | tf_op jit(solution)/shard_map/ppermute | solution.py:61
  108.0 2.3 %collective-permute-done.18.refs_5_ = f32[256,384]{1,0:T(8,128)S(1)} collective-permute-done((f32[256,384]{1,0:T(8,128)S(1)}, f32[256,384]{1,0:T(8,128)S(1)}, u32[]{:S(2)}, u32[]{:S(2)}) %collective-permute-start.18) | collective-permute-done | bytes 393248 | tf_op jit(solution)/shard_map/ppermute | solution.py:61
  110.3 1.5 %shard_map.117 = (f32[256,256]{1,0:T(8,128)}, f32[256,256]{1,0:T(8,128)}, f32[256,256]{1,0:T(8,128)}) custom-call(s32[3]{0:T(128)S(1)} %copy-done.4, f32[512,384]{1,0:T(8,128)S(1)} %shard_map.106.kept.refs_0_, f32[512,384]{1,0:T(8,128)S(1)} %collective-permute-done.14.got.refs_1_, f32[256,384]{1,0:T(8,128)S(1)} %collective-permute-done.15.refs_2_, ...), custom_call_target="tpu_custom_call" | custom-call | tf_op jit(solution)/shard_map/pallas_call | solution.py:45
  111.9 0.0 collective-permute-done.13
  111.9 0.9 add_bitcast_fusion
  (5 shorter events, 0.0 us)
Async XLA Ops:
  0.6 39.5 %copy-start = (f32[1,128,1024]{2,1,0:T(8,128)S(1)}, f32[1,128,1024]{2,1,0:T(8,128)}, u32[]{:S(2)}) copy-start(f32[1,128,1024]{2,1,0:T(8,128)} %param.7) | copy-start | bytes 1572868
  4.5 22.0 %collective-permute-start.3 = (f32[128,1024]{1,0:T(8,128)}, f32[128,1024]{1,0:T(8,128)S(1)}, u32[]{:S(2)}, u32[]{:S(2)}) collective-permute-start(f32[128,1024]{1,0:T(8,128)} %bitcast.8), channel_id=1, source_target_pairs={{0,2},{1,3},{2,0},{3,1},{4,6},{5,7},{6,4},{7,5},{8,10},{9,11},{10,... | collective-permute-start | bytes 1572872 | tf_op jit(solution)/shard_map/ppermute | solution.py:61
  7.4 19.1 %collective-permute-start = (f32[256,384]{1,0:T(8,128)}, f32[256,384]{1,0:T(8,128)S(1)}, u32[]{:S(2)}, u32[]{:S(2)}) collective-permute-start(f32[256,384]{1,0:T(8,128)} %get-tuple-element.34), channel_id=1, source_target_pairs={{0,4},{4,0},{8,12},{12,8},{1,5},{5,1},{9,13},{13,9},{2,6},{6,2},{1... | collective-permute-start | bytes 1179656 | tf_op jit(solution)/shard_map/ppermute | solution.py:61
  9.0 19.9 %collective-permute-start.5 = (f32[256,384]{1,0:T(8,128)}, f32[256,384]{1,0:T(8,128)S(1)}, u32[]{:S(2)}, u32[]{:S(2)}) collective-permute-start(f32[256,384]{1,0:T(8,128)} %get-tuple-element.34), channel_id=1, source_target_pairs={{0,8},{4,12},{8,0},{12,4},{1,9},{5,13},{9,1},{13,5},{2,10},{6,14},... | collective-permute-start | bytes 1179656 | tf_op jit(solution)/shard_map/ppermute | solution.py:61
  11.6 17.7 %collective-permute-start.2 = (f32[128,1024]{1,0:T(8,128)}, f32[128,1024]{1,0:T(8,128)S(1)}, u32[]{:S(2)}, u32[]{:S(2)}) collective-permute-start(f32[128,1024]{1,0:T(8,128)} %bitcast.9), channel_id=1, source_target_pairs={{0,1},{1,0},{2,3},{3,2},{4,5},{5,4},{6,7},{7,6},{8,9},{9,8},{10,11... | collective-permute-start | bytes 1572872 | tf_op jit(solution)/shard_map/ppermute | solution.py:61
  26.5 2.8 %collective-permute-start.4 = (f32[128,1024]{1,0:T(8,128)S(1)}, f32[128,1024]{1,0:T(8,128)S(1)}, u32[]{:S(2)}, u32[]{:S(2)}) collective-permute-start(f32[128,1024]{1,0:T(8,128)S(1)} %collective-permute-done.3.refs_2_), channel_id=1, source_target_pairs={{0,1},{1,0},{2,3},{3,2},{4,5},{5,4},{6,7},{7,6},{8,9},{9,8},{10,11... | collective-permute-start | bytes 1572872 | tf_op jit(solution)/shard_map/ppermute | solution.py:61
  26.5 11.5 %collective-permute-start.1 = (f32[256,384]{1,0:T(8,128)S(1)}, f32[256,384]{1,0:T(8,128)S(1)}, u32[]{:S(2)}, u32[]{:S(2)}) collective-permute-start(f32[256,384]{1,0:T(8,128)S(1)} %collective-permute-done.refs_4_), channel_id=1, source_target_pairs={{0,16},{16,0},{1,17},{17,1},{2,18},{18,2},{3,19},{19,3},{4,20},{20... | collective-permute-start | bytes 1179656 | tf_op jit(solution)/shard_map/ppermute | solution.py:61
  28.9 10.7 %collective-permute-start.6 = (f32[256,384]{1,0:T(8,128)S(1)}, f32[256,384]{1,0:T(8,128)}, u32[]{:S(2)}, u32[]{:S(2)}) collective-permute-start(f32[256,384]{1,0:T(8,128)S(1)} %collective-permute-done.5.refs_5_), channel_id=1, source_target_pairs={{0,4},{4,0},{8,12},{12,8},{1,5},{5,1},{9,13},{13,9},{2,6},{6,2},{1... | collective-permute-start | bytes 1179656 | tf_op jit(solution)/shard_map/ppermute | solution.py:61
  29.3 10.9 %collective-permute-start.7 = (f32[128,256]{1,0:T(8,128)}, f32[128,256]{1,0:T(8,128)S(1)}, u32[]{:S(2)}, u32[]{:S(2)}) collective-permute-start(f32[128,256]{1,0:T(8,128)} %get-tuple-element.40), channel_id=1, source_target_pairs={{0,1},{1,0},{2,3},{3,2},{4,5},{5,4},{6,7},{7,6},{8,9},{9,8},{10,11... | collective-permute-start | bytes 393224 | tf_op jit(solution)/shard_map/ppermute | solution.py:61
  29.4 10.9 %collective-permute-start.8 = (f32[128,256]{1,0:T(8,128)}, f32[128,256]{1,0:T(8,128)S(1)}, u32[]{:S(2)}, u32[]{:S(2)}) collective-permute-start(f32[128,256]{1,0:T(8,128)} %get-tuple-element.42), channel_id=1, source_target_pairs={{0,2},{1,3},{2,0},{3,1},{4,6},{5,7},{6,4},{7,5},{8,10},{9,11},{10,... | collective-permute-start | bytes 393224 | tf_op jit(solution)/shard_map/ppermute | solution.py:61
  29.9 10.3 %collective-permute-start.9 = (f32[128,256]{1,0:T(8,128)}, f32[128,256]{1,0:T(8,128)}, u32[]{:S(2)}, u32[]{:S(2)}) collective-permute-start(f32[128,256]{1,0:T(8,128)} %get-tuple-element.44), channel_id=1, source_target_pairs={{0,3},{1,2},{2,1},{3,0},{4,7},{5,6},{6,5},{7,4},{8,11},{9,10},{10,... | collective-permute-start | bytes 393224 | tf_op jit(solution)/shard_map/ppermute | solution.py:61
  32.0 8.3 %copy-start.1 = (f32[256,256]{1,0:T(8,128)S(1)}, f32[256,256]{1,0:T(8,128)}, u32[]{:S(2)}) copy-start(f32[256,256]{1,0:T(8,128)} %refs_1_.3) | copy-start | bytes 786436
  32.0 8.3 %copy-start.2 = (f32[256,256]{1,0:T(8,128)S(1)}, f32[256,256]{1,0:T(8,128)}, u32[]{:S(2)}) copy-start(f32[256,256]{1,0:T(8,128)} %refs_2_.3) | copy-start | bytes 786436
  32.0 8.3 %copy-start.3 = (f32[256,256]{1,0:T(8,128)S(1)}, f32[256,256]{1,0:T(8,128)}, u32[]{:S(2)}) copy-start(f32[256,256]{1,0:T(8,128)} %refs_3_.3) | copy-start | bytes 786436
  32.0 8.3 %copy-start.4 = (s32[3]{0:T(128)S(1)}, s32[3]{0:T(128)}, u32[]{:S(2)}) copy-start(s32[3]{0:T(128)} %pad_add_fusion.info) | copy-start | bytes 40
  32.0 8.3 %copy-start.5 = (f32[128,256]{1,0:T(8,128)S(1)}, f32[128,256]{1,0:T(8,128)}, u32[]{:S(2)}) copy-start(f32[128,256]{1,0:T(8,128)} %get-tuple-element.38.refs_7_) | copy-start | bytes 393220
  38.1 15.7 %collective-permute-start.10 = (f32[256,384]{1,0:T(8,128)S(1)}, f32[256,384]{1,0:T(8,128)S(1)}, u32[]{:S(2)}, u32[]{:S(2)}) collective-permute-start(f32[256,384]{1,0:T(8,128)S(1)} %collective-permute-done.5.refs_5_), channel_id=1, source_target_pairs={{0,16},{16,0},{1,17},{17,1},{2,18},{18,2},{3,19},{19,3},{4,20},{20... | collective-permute-start | bytes 1179656 | tf_op jit(solution)/shard_map/ppermute | solution.py:61
  39.6 17.8 %collective-permute-start.11 = (f32[256,384]{1,0:T(8,128)}, f32[256,384]{1,0:T(8,128)S(1)}, u32[]{:S(2)}, u32[]{:S(2)}) collective-permute-start(f32[256,384]{1,0:T(8,128)} %collective-permute-done.6.refs_6_), channel_id=1, source_target_pairs={{0,16},{16,0},{1,17},{17,1},{2,18},{18,2},{3,19},{19,3},{4,20},{20... | collective-permute-start | bytes 1179656 | tf_op jit(solution)/shard_map/ppermute | solution.py:61
  50.7 20.0 %collective-permute-start.14 = (f32[512,384]{1,0:T(8,128)S(1)}, f32[512,384]{1,0:T(8,128)S(1)}, u32[]{:S(2)}, u32[]{:S(2)}) collective-permute-start(f32[512,384]{1,0:T(8,128)S(1)} %shard_map.105), channel_id=1, source_target_pairs={{0,4},{4,0},{8,12},{12,8},{1,5},{5,1},{9,13},{13,9},{2,6},{6,2},{1... | collective-permute-start | bytes 2359304 | tf_op jit(solution)/shard_map/ppermute | solution.py:61
  70.5 7.1 %collective-permute-start.12 = (f32[256,1024]{1,0:T(8,128)S(1)}, f32[256,1024]{1,0:T(8,128)S(1)}, u32[]{:S(2)}, u32[]{:S(2)}) collective-permute-start(f32[256,1024]{1,0:T(8,128)S(1)} %shard_map.110), channel_id=1, source_target_pairs={{0,1},{1,0},{2,3},{3,2},{4,5},{5,4},{6,7},{7,6},{8,9},{9,8},{10,11... | collective-permute-start | bytes 3145736 | tf_op jit(solution)/shard_map/ppermute | solution.py:61
  70.6 19.6 %collective-permute-start.16 = (f32[256,384]{1,0:T(8,128)S(1)}, f32[256,384]{1,0:T(8,128)S(1)}, u32[]{:S(2)}, u32[]{:S(2)}) collective-permute-start(f32[256,384]{1,0:T(8,128)S(1)} %shard_map.108), channel_id=1, source_target_pairs={{0,4},{4,0},{8,12},{12,8},{1,5},{5,1},{9,13},{13,9},{2,6},{6,2},{1... | collective-permute-start | bytes 1179656 | tf_op jit(solution)/shard_map/ppermute | solution.py:61
  70.7 21.0 %collective-permute-start.15 = (f32[256,384]{1,0:T(8,128)S(1)}, f32[256,384]{1,0:T(8,128)S(1)}, u32[]{:S(2)}, u32[]{:S(2)}) collective-permute-start(f32[256,384]{1,0:T(8,128)S(1)} %shard_map.112), channel_id=1, source_target_pairs={{0,8},{4,12},{8,0},{12,4},{1,9},{5,13},{9,1},{13,5},{2,10},{6,14},... | collective-permute-start | bytes 1179656 | tf_op jit(solution)/shard_map/ppermute | solution.py:61
  77.7 34.2 %collective-permute-start.13 = (f32[128,1024]{1,0:T(8,128)S(1)}, f32[128,1024]{1,0:T(8,128)S(1)}, u32[]{:S(2)}, u32[]{:S(2)}) collective-permute-start(f32[128,1024]{1,0:T(8,128)S(1)} %get-tuple-element.55), channel_id=1, source_target_pairs={{0,2},{1,3},{2,0},{3,1},{4,6},{5,7},{6,4},{7,5},{8,10},{9,11},{10,... | collective-permute-start | bytes 1572872 | tf_op jit(solution)/shard_map/ppermute | solution.py:61
  90.2 17.9 %collective-permute-start.17 = (f32[256,384]{1,0:T(8,128)S(1)}, f32[256,384]{1,0:T(8,128)S(1)}, u32[]{:S(2)}, u32[]{:S(2)}) collective-permute-start(f32[256,384]{1,0:T(8,128)S(1)} %shard_map.113), channel_id=1, source_target_pairs={{0,4},{4,0},{8,12},{12,8},{1,5},{5,1},{9,13},{13,9},{2,6},{6,2},{1... | collective-permute-start | bytes 1179656 | tf_op jit(solution)/shard_map/ppermute | solution.py:61
  91.8 18.6 %collective-permute-start.18 = (f32[256,384]{1,0:T(8,128)S(1)}, f32[256,384]{1,0:T(8,128)S(1)}, u32[]{:S(2)}, u32[]{:S(2)}) collective-permute-start(f32[256,384]{1,0:T(8,128)S(1)} %shard_map.116), channel_id=1, source_target_pairs={{0,8},{4,12},{8,0},{12,4},{1,9},{5,13},{9,1},{13,5},{2,10},{6,14},... | collective-permute-start | bytes 1179656 | tf_op jit(solution)/shard_map/ppermute | solution.py:61

commit v5 on v4

--- a/solution.py
+++ b/solution.py
@@ -129,29 +129,47 @@
 
 
 def attention_body(turn, blocks, wa, info, neighbours, *refs):
-    x, wq, wk, wv = refs[:4]
-    pieces = refs[4 : 3 + wa]
-    adjoints = refs[3 + wa : 3 + wa + blocks]
-    out, panel, proj = refs[3 + wa + blocks :]
+    own = 1 if turn == 0 else 3
+    x, *weights = refs[: 1 + own]
+    pieces = refs[1 + own : own + wa]
+    adjoints = refs[own + wa : own + wa + blocks]
+    *parts, out, panel, proj = refs[own + wa + blocks :]
     cols = columns_of(turn, info)
-    count = wq.shape[0]
+    count = weights[0].shape[0]
 
     def rows(r):
         return pl.ds(pl.multiple_of((info[0] ^ r) * count, 8), count)
 
-    panel[rows(0), 0:LANES] = wq[:, cols]
-    panel[rows(0), LANES : 2 * LANES] = wk[:, cols]
-    panel[rows(0), 2 * LANES : 3 * LANES] = wv[:, cols]
+    if turn == 0:
+        panel[rows(0), :] = weights[0][...]
+    else:
+        for i, weight in enumerate(weights):
+            panel[rows(0), i * LANES : (i + 1) * LANES] = weight[:, cols]
     for r in range(1, wa):
         panel[rows(r), :] = pieces[r - 1][...]
-    attention_core(cols, blocks, info[2], neighbours, x, panel, adjoints, out, proj)
+    if parts:
+        last = pl.ds(pl.multiple_of((info[0] ^ (wa - 1)) * count, LANES), count)
+        proj[...] = parts[0][...] + dot(x[:, last], pieces[-1][...], NN)
+    else:
+        proj[...] = dot(x[...], panel[...], NN)
+    attention_core(cols, blocks, info[2], neighbours, adjoints, out, proj)
+
+
+def partial_body(info, x, *refs):
+    *pieces, out = refs
+    total = None
+    for r, piece in enumerate(pieces):
+        count = piece.shape[0]
+        here = pl.ds(pl.multiple_of((info[0] ^ r) * count, LANES), count)
+        term = dot(x[:, here], piece[...], NN)
+        total = term if total is None else total + term
+    out[...] = total
 
 
 def attention_panel_body(chunk, blocks, info, neighbours, x, panel, *refs):
     cols = slice(chunk * LANES, (chunk + 1) * LANES)
-    attention_core(
-        cols, blocks, info[2], neighbours, x, panel, refs[:blocks], refs[blocks], refs[blocks + 1]
-    )
+    refs[blocks + 1][...] = dot(x[...], panel[...], NN)
+    attention_core(cols, blocks, info[2], neighbours, refs[:blocks], *refs[blocks:])
 
 
 BF16 = jnp.bfloat16
@@ -171,8 +189,7 @@
     return (term(high, low_right) + term(low, high_right)) + term(high, high_right)
 
 
-def attention_core(cols, blocks, t, neighbours, x, panel, adjoints, out, proj):
-    proj[...] = dot(x[...], panel[...], NN)
+def attention_core(cols, blocks, t, neighbours, adjoints, out, proj):
     out[:, LANES:] = jnp.zeros((out.shape[0], 2 * LANES), F32)
     first = lax.broadcasted_iota(jnp.int32, (BLOCK, LANES), 1) < DH
     scale = DH ** (-0.5)
@@ -263,15 +280,18 @@
 
 
 def join_body(turns, info, *refs):
-    count = (len(refs) - 3) // turns
+    *refs, back = refs
+    count = (len(refs) - 5) // turns
+    back[...] = refs[turns * count][...] + refs[turns * count + 1][...]
+    outs = refs[turns * count + 2 :]
     for turn in range(turns):
         for i in range(3):
             part = slice(i * LANES, (i + 1) * LANES)
-            rows = refs[-1].shape[0]
+            rows = outs[0].shape[0]
             total = refs[turn * count][:rows, part]
             for term in refs[turn * count + 1 : (turn + 1) * count]:
                 total += term[:rows, part]
-            refs[turns * count + i][:, columns_of(turn, info)] = total
+            outs[i][:, columns_of(turn, info)] = total
 
 
 def per_device(sizes, node_features, sensor_adjoint, sensor_node, neighbours, *weights):
@@ -292,7 +312,7 @@
         first, *blocks_out = blocks_out
         held[0] = after(hour_rows, first)
         gathered = [spread({0: first}, "wa", wa)]
-        gathered.append({r: swap(gathered[0][r], "grp", grp, 1) for r in range(1, wa)})
+        gathered.append({1: swap(gathered[0][1], "grp", grp, 1)})
         held[ta // 2] = after(swap(held[0], "ta", ta, ta // 2), gathered[0][1])
     held = spread(held, "ta", ta)
     adjoints = [blocks_out[0]] + [
@@ -302,18 +322,33 @@
         functools.partial(stack_body, ta), [shaped(nodes, width)], [held[r] for r in range(ta)]
     )[0]
 
+    parts = []
+    if direct:
+        parts = local_call(
+            partial_body,
+            [shaped(nodes, 3 * LANES)],
+            [inputs, *[gathered[0][r] for r in range(wa - 1)]],
+            scalars=[info],
+        )
+        gathered[1][2] = swap(after(gathered[0][2], *parts, gathered[1][1]), "grp", grp, 1)
+        gathered[1][3] = swap(gathered[0][3], "grp", grp, 1)
+
     stacked, panels, owned, sent, ready = [], [], [], [], []
     for c in range(chunks):
         proj_flops = 12 * nodes * width * 3 * LANES + 60 * 2 * nodes * 4 * BLOCK * LANES
         scratch = [pltpu.VMEM((nodes, 3 * LANES), F32)]
         turn = after(info, stacked[-1], *sent) if stacked else info
-        if direct and not c:
-            turn = after(turn, gathered[1][1])
         if direct:
             dqkv, panel = local_call(
                 functools.partial(attention_body, c, blocks, wa),
                 [shaped(nodes, 3 * LANES), shaped(width, 3 * LANES)],
-                [inputs, *weights, *[gathered[c][r] for r in range(1, wa)], *adjoints],
+                [
+                    inputs,
+                    *(weights if c else [first]),
+                    *[gathered[c][r] for r in range(1, wa)],
+                    *adjoints,
+                    *([] if c else parts),
+                ],
                 scalars=[turn, neighbours],
                 scratch=scratch,
                 flops=proj_flops,
@@ -366,20 +401,20 @@
         passed = total_of(shares[2], after(message, *wait), rows_here)
         direct_got = swap(after(shares[1], message), "wa", wa, 1)
         owned += [shares[0], direct_got, swap(passed, "wa", wa, 2)]
-    back = (kept + got)[None]
     if direct:
-        grads = local_call(
+        *grads, back = local_call(
             functools.partial(join_body, chunks),
-            [shaped(rows_here, columns)] * 3,
-            owned,
+            [shaped(rows_here, columns)] * 3 + [shaped(nodes_here, width)],
+            [*owned, kept, got],
             scalars=[info],
         )
     else:
+        back = kept + got
         grads = [
             jnp.concatenate([o[:, i * LANES : (i + 1) * LANES] for o in owned], axis=1)
             for i in range(3)
         ]
-    return (back, *grads)
+    return (back[None], *grads)
 
 
 def solution(mesh):

time: 113 us -> 111 us (0.982)
  waiting for transfers between devices: 52.2 us -> 49.8 us
    ppermute x19, waiting for transfers between devices: 52.2 us -> 49.8 us  [swap(): return lax.ppermute(value, axis, [(i, i ^ step) for i in range(size)])]
    pallas_call x15 -> x16, Pallas kernels: 36.3 us -> 37.3 us  [local_call(): pl.pallas_call(body, out_shape=outs, in_specs=[smem] * len(scalars) + [vm...]
where the time goes in v5:
time: 111 us; the launch traced here: 110 us
  waiting for transfers between devices  49.8 us (45%)
  Pallas kernels  40.5 us (36%)
  starting transfers between devices  17.8 us (16%)
    ppermute x19, waiting for transfers between devices, swap(): return lax.ppermute(value, axis, [(i, i ^ step) for i in range(size)])  49.8 us
    pallas_call x16, Pallas kernels, local_call(): pl.pallas_call(body, out_shape=outs, in_specs=[smem] * len(scalars) + [vm...  37.3 us
    ppermute x19, starting transfers between devices, swap(): return lax.ppermute(value, axis, [(i, i ^ step) for i in range(size)])  17.8 us
    pallas_call x1, Pallas kernels, entry(): pl.pallas_call(functools.partial(body, parts), out_shape=[shaped(*o) for...  3.19 us
  transfers between devices with their start and end apart: 19, of which 8 were waited for; matrix products, arithmetic and copies ran while one was open for 1% of the time, Pallas kernels for 32%

profile of v5, /device:TPU:0, one launch (start us, length us, event | category | flops | bytes accessed | tf_op | source)
XLA Modules:
  0.0 110.5 jit_solution(8391728337647757856)
XLA Ops:
  0.6 0.0 copy-start
  0.6 0.6 pad_add_fusion.info
  1.3 3.2 %shard_map.102 = (f32[256,384]{1,0:T(8,128)}, f32[128,256]{1,0:T(8,128)}, f32[128,256]{1,0:T(8,128)}, f32[128,256]{1,0:T(8,128)}, f32[128,256]{1,0:T(8,128)}) custom-call(s32[3]{0:T(128)} %pad_add_fusion.info, s32[1,128]{1,0:T(1,128)} %bitcast.11, f32[128,1024]{1,0:T(8,128)} %bitcast.10, f32[256,256]{1,0:T(8,128)} %refs_1_.1, f32[256,256]{1,0:T(8,128)} %refs_2_.1, ...), custom_call_target="tpu_custom_call" | custom-call | tf_op jit(solution)/shard_map/pallas_call | solution.py:94
  4.4 2.9 %collective-permute-start.1 = (f32[128,1024]{1,0:T(8,128)}, f32[128,1024]{1,0:T(8,128)S(1)}, u32[]{:S(2)}, u32[]{:S(2)}) collective-permute-start(f32[128,1024]{1,0:T(8,128)} %bitcast.7), channel_id=1, source_target_pairs={{0,2},{1,3},{2,0},{3,1},{4,6},{5,7},{6,4},{7,5},{8,10},{9,11},{10,... | collective-permute-start | bytes 1572872 | tf_op jit(solution)/shard_map/ppermute | solution.py:61
  7.4 1.6 %collective-permute-start.2 = (f32[256,384]{1,0:T(8,128)}, f32[256,384]{1,0:T(8,128)S(1)}, u32[]{:S(2)}, u32[]{:S(2)}) collective-permute-start(f32[256,384]{1,0:T(8,128)} %get-tuple-element.35.refs_0_.refs_1_), channel_id=1, source_target_pairs={{0,4},{4,0},{8,12},{12,8},{1,5},{5,1},{9,13},{13,9},{2,6},{6,2},{1... | collective-permute-start | bytes 1179656 | tf_op jit(solution)/shard_map/ppermute | solution.py:61
  9.0 2.6 %collective-permute-start.4 = (f32[256,384]{1,0:T(8,128)}, f32[256,384]{1,0:T(8,128)S(1)}, u32[]{:S(2)}, u32[]{:S(2)}) collective-permute-start(f32[256,384]{1,0:T(8,128)} %get-tuple-element.35.refs_0_.refs_1_), channel_id=1, source_target_pairs={{0,8},{4,12},{8,0},{12,4},{1,9},{5,13},{9,1},{13,5},{2,10},{6,14},... | collective-permute-start | bytes 1179656 | tf_op jit(solution)/shard_map/ppermute | solution.py:61
  11.6 0.0 collective-permute-start
  11.6 14.9 %collective-permute-done.2.refs_1_.refs_2_ = f32[256,384]{1,0:T(8,128)S(1)} collective-permute-done((f32[256,384]{1,0:T(8,128)}, f32[256,384]{1,0:T(8,128)S(1)}, u32[]{:S(2)}, u32[]{:S(2)}) %collective-permute-start.2) | collective-permute-done | bytes 393248 | tf_op jit(solution)/shard_map/ppermute | solution.py:61
  26.5 0.0 collective-permute-done.1.refs_2_
  26.5 0.0 collective-permute-start.3
  26.5 2.4 %collective-permute-done.4.refs_2_.refs_3_ = f32[256,384]{1,0:T(8,128)S(1)} collective-permute-done((f32[256,384]{1,0:T(8,128)}, f32[256,384]{1,0:T(8,128)S(1)}, u32[]{:S(2)}, u32[]{:S(2)}) %collective-permute-start.4) | collective-permute-done | bytes 393248 | tf_op jit(solution)/shard_map/ppermute | solution.py:61
  28.9 0.4 collective-permute-start.5
  29.3 1.5 %collective-permute-start.11 = (f32[256,384]{1,0:T(8,128)S(1)}, f32[256,384]{1,0:T(8,128)S(1)}, u32[]{:S(2)}, u32[]{:S(2)}) collective-permute-start(f32[256,384]{1,0:T(8,128)S(1)} %collective-permute-done.2.refs_1_.refs_2_), channel_id=1, source_target_pairs={{0,16},{16,0},{1,17},{17,1},{2,18},{18,2},{3,19},{19,3},{4,20},{20... | collective-permute-start | bytes 1179656 | tf_op jit(solution)/shard_map/ppermute | solution.py:61
  30.8 0.0 collective-permute-done.refs_1_
  30.8 0.0 collective-permute-done.3.refs_3_
  30.8 0.0 collective-permute-start.6
  30.8 0.6 collective-permute-start.7
  31.4 1.3 %collective-permute-start.8 = (f32[128,256]{1,0:T(8,128)}, f32[128,256]{1,0:T(8,128)}, u32[]{:S(2)}, u32[]{:S(2)}) collective-permute-start(f32[128,256]{1,0:T(8,128)} %get-tuple-element.44), channel_id=1, source_target_pairs={{0,3},{1,2},{2,1},{3,0},{4,7},{5,6},{6,5},{7,4},{8,11},{9,10},{10,... | collective-permute-start | bytes 393224 | tf_op jit(solution)/shard_map/ppermute | solution.py:61
  32.7 0.8 copy.11.neighbours
  33.5 4.7 %collective-permute-done.5.refs_4_ = f32[256,384]{1,0:T(8,128)} collective-permute-done((f32[256,384]{1,0:T(8,128)S(1)}, f32[256,384]{1,0:T(8,128)}, u32[]{:S(2)}, u32[]{:S(2)}) %collective-permute-start.5) | collective-permute-done | bytes 393248 | tf_op jit(solution)/shard_map/ppermute | solution.py:61
  38.1 1.5 %collective-permute-start.13 = (f32[256,384]{1,0:T(8,128)}, f32[256,384]{1,0:T(8,128)S(1)}, u32[]{:S(2)}, u32[]{:S(2)}) collective-permute-start(f32[256,384]{1,0:T(8,128)} %collective-permute-done.5.refs_4_), channel_id=1, source_target_pairs={{0,16},{16,0},{1,17},{17,1},{2,18},{18,2},{3,19},{19,3},{4,20},{20... | collective-permute-start | bytes 1179656 | tf_op jit(solution)/shard_map/ppermute | solution.py:61
  39.6 0.0 copy-done
  39.6 0.1 shard_map.103.x.refs_0_
  39.8 0.0 copy-done.1
  39.8 0.0 copy-start.6
  39.8 3.2 %shard_map.104.refs_9_ = f32[512,384]{1,0:T(8,128)S(1)} custom-call(s32[3]{0:T(128)S(1)} %copy-done.5, f32[512,1024]{1,0:T(8,128)S(1)} %shard_map.103.x.refs_0_, f32[256,384]{1,0:T(8,128)S(1)} %copy-done.1, f32[256,384]{1,0:T(8,128)S(1)} %collective-permute-done.2.refs_1_.refs_2_, f32[256,384]{1,0:T(8,128)S(1)} %collective-permute-done.4.refs_2_.refs_3_), custom_call_target="tpu_custom_call" | custom-call | tf_op jit(solution)/shard_map/pallas_call | solution.py:45
  43.0 0.0 collective-permute-done.11.refs_4_
  43.0 0.6 collective-permute-start.12
  43.6 0.0 collective-permute-done.6.refs_6_.refs_8_
  43.6 0.0 collective-permute-done.7.refs_7_.refs_9_
  43.6 0.0 collective-permute-done.8.refs_8_.refs_10_
  43.6 5.5 %shard_map.105 = (f32[512,384]{1,0:T(8,128)S(1)}, f32[1024,384]{1,0:T(8,128)S(1)}) custom-call(s32[3]{0:T(128)S(1)} %copy-done.5, s32[4,2]{1,0:T(4,128)S(1)} %copy.11.neighbours, f32[512,1024]{1,0:T(8,128)S(1)} %shard_map.103.x.refs_0_, f32[256,384]{1,0:T(8,128)S(1)} %copy-done.1, f32[256,384]{1,0:T(8,128)S(1)} %collective-permute-done.2.refs_1_.refs_2_, ...), custom_call_target="tpu_custom_call" | custom-call | flops 6442450944 | bytes 25165824 | tf_op jit(solution)/shard_map/pallas_call | solution.py:45
  49.1 2.4 %shard_map.106 = f32[512,384]{1,0:T(8,128)S(1)} custom-call(s32[3]{0:T(128)S(1)} %copy-done.5, f32[512,1024]{1,0:T(8,128)S(1)} %shard_map.103.x.refs_0_, f32[512,384]{1,0:T(8,128)S(1)} %get-tuple-element.45.stacked.refs_0_), custom_call_target="tpu_custom_call" | custom-call | tf_op jit(solution)/shard_map/pallas_call | solution.py:45
  51.6 0.0 copy-start.2
  51.6 0.0 copy-start.3
  51.6 0.0 copy-start.4
  51.6 1.0 collective-permute-start.9
  52.5 2.4 %shard_map.107.kept.refs_0_ = f32[512,384]{1,0:T(8,128)S(1)} custom-call(s32[3]{0:T(128)S(1)} %copy-done.5, f32[512,1024]{1,0:T(8,128)S(1)} %shard_map.103.x.refs_0_, f32[512,384]{1,0:T(8,128)S(1)} %get-tuple-element.45.stacked.refs_0_), custom_call_target="tpu_custom_call" | custom-call | tf_op jit(solution)/shard_map/pallas_call | solution.py:45
  55.0 0.0 collective-permute-done.13.refs_6_
  55.0 0.5 collective-permute-done.12.refs_5_
  55.5 0.0 copy-done.4
  55.5 8.1 %shard_map.109 = (f32[512,384]{1,0:T(8,128)S(1)}, f32[1024,384]{1,0:T(8,128)S(1)}) custom-call(s32[3]{0:T(128)S(1)} %copy-done.5, s32[4,2]{1,0:T(4,128)S(1)} %copy.11.neighbours, f32[512,1024]{1,0:T(8,128)S(1)} %shard_map.103.x.refs_0_, f32[256,256]{1,0:T(8,128)S(1)} %copy-done.2, f32[256,256]{1,0:T(8,128)S(1)} %copy-done.3, f32[256,256]{1,0:T(8,128)S(1)} %copy-done.4, ...), custom_call_target="tpu_custom_call" | custom-call | flops 6442450944 | bytes 25165824 | tf_op jit(solution)/shard_map/pallas_call | solution.py:45
  63.5 1.6 %shard_map.110 = f32[256,384]{1,0:T(8,128)S(1)} custom-call(s32[3]{0:T(128)S(1)} %copy-done.5, f32[512,1024]{1,0:T(8,128)S(1)} %shard_map.103.x.refs_0_, f32[512,384]{1,0:T(8,128)S(1)} %get-tuple-element.50.stacked.refs_1_), custom_call_target="tpu_custom_call" | custom-call | tf_op jit(solution)/shard_map/pallas_call | solution.py:45
  65.2 3.5 %shard_map.115 = f32[256,1024]{1,0:T(8,128)S(1)} custom-call(f32[512,384]{1,0:T(8,128)S(1)} %get-tuple-element.45.stacked.refs_0_, f32[512,384]{1,0:T(8,128)S(1)} %get-tuple-element.50.stacked.refs_1_, f32[1024,384]{1,0:T(8,128)S(1)} %get-tuple-element.56.refs_2_, f32[1024,384]{1,0:T(8,128)S(1)} %get-tuple-element.58.refs_3_), custom_call_target="tpu_custom_call" | custom-call | tf_op jit(solution)/shard_map/pallas_call | solution.py:45
  68.7 0.1 collective-permute-start.16
  68.7 1.2 %collective-permute-start.14 = (f32[256,384]{1,0:T(8,128)S(1)}, f32[256,384]{1,0:T(8,128)S(1)}, u32[]{:S(2)}, u32[]{:S(2)}) collective-permute-start(f32[256,384]{1,0:T(8,128)S(1)} %shard_map.110), channel_id=1, source_target_pairs={{0,4},{4,0},{8,12},{12,8},{1,5},{5,1},{9,13},{13,9},{2,6},{6,2},{1... | collective-permute-start | bytes 1179656 | tf_op jit(solution)/shard_map/ppermute | solution.py:61
  69.9 0.0 collective-permute-done.9.got.refs_1_
  70.0 1.5 %collective-permute-start.10 = (f32[256,384]{1,0:T(8,128)S(1)}, f32[256,384]{1,0:T(8,128)S(1)}, u32[]{:S(2)}, u32[]{:S(2)}) collective-permute-start(f32[256,384]{1,0:T(8,128)S(1)} %shard_map.108), channel_id=1, source_target_pairs={{0,8},{4,12},{8,0},{12,4},{1,9},{5,13},{9,1},{13,5},{2,10},{6,14},... | collective-permute-start | bytes 1179656 | tf_op jit(solution)/shard_map/ppermute | solution.py:61
  71.5 3.7 %shard_map.114.keep = f32[256,1024]{1,0:T(8,128)S(1)} custom-call(f32[512,384]{1,0:T(8,128)S(1)} %get-tuple-element.45.stacked.refs_0_, f32[512,384]{1,0:T(8,128)S(1)} %get-tuple-element.50.stacked.refs_1_, f32[1024,384]{1,0:T(8,128)S(1)} %get-tuple-element.56.refs_2_, f32[1024,384]{1,0:T(8,128)S(1)} %get-tuple-element.58.refs_3_), custom_call_target="tpu_custom_call" | custom-call | tf_op jit(solution)/shard_map/pallas_call | solution.py:45
  75.3 0.0 collective-permute-done.16.got
  75.3 0.1 shard_map.116
  75.4 0.6 collective-permute-start.18
  76.0 1.6 %shard_map.111 = f32[256,384]{1,0:T(8,128)S(1)} custom-call(s32[3]{0:T(128)S(1)} %copy-done.5, f32[512,1024]{1,0:T(8,128)S(1)} %shard_map.103.x.refs_0_, f32[512,384]{1,0:T(8,128)S(1)} %get-tuple-element.50.stacked.refs_1_), custom_call_target="tpu_custom_call" | custom-call | tf_op jit(solution)/shard_map/pallas_call | solution.py:45
  77.6 1.6 %shard_map.112.kept = f32[256,384]{1,0:T(8,128)S(1)} custom-call(s32[3]{0:T(128)S(1)} %copy-done.5, f32[512,1024]{1,0:T(8,128)S(1)} %shard_map.103.x.refs_0_, f32[512,384]{1,0:T(8,128)S(1)} %get-tuple-element.50.stacked.refs_1_), custom_call_target="tpu_custom_call" | custom-call | tf_op jit(solution)/shard_map/pallas_call | solution.py:45
  79.2 9.3 %collective-permute-done.14.got = f32[256,384]{1,0:T(8,128)S(1)} collective-permute-done((f32[256,384]{1,0:T(8,128)S(1)}, f32[256,384]{1,0:T(8,128)S(1)}, u32[]{:S(2)}, u32[]{:S(2)}) %collective-permute-start.14) | collective-permute-done | bytes 393248 | tf_op jit(solution)/shard_map/ppermute | solution.py:61
  88.5 0.0 collective-permute-start.15
  88.5 1.9 %collective-permute-done.10.refs_2_ = f32[256,384]{1,0:T(8,128)S(1)} collective-permute-done((f32[256,384]{1,0:T(8,128)S(1)}, f32[256,384]{1,0:T(8,128)S(1)}, u32[]{:S(2)}, u32[]{:S(2)}) %collective-permute-start.10) | collective-permute-done | bytes 393248 | tf_op jit(solution)/shard_map/ppermute | solution.py:61
  90.4 0.1 shard_map.117
  90.4 0.5 collective-permute-start.17
  90.9 1.6 %shard_map.113.refs_3_ = f32[256,384]{1,0:T(8,128)S(1)} custom-call(s32[3]{0:T(128)S(1)} %copy-done.5, f32[512,1024]{1,0:T(8,128)S(1)} %shard_map.103.x.refs_0_, f32[512,384]{1,0:T(8,128)S(1)} %get-tuple-element.50.stacked.refs_1_), custom_call_target="tpu_custom_call" | custom-call | tf_op jit(solution)/shard_map/pallas_call | solution.py:45
  92.5 13.7 %collective-permute-done.15.refs_4_ = f32[256,384]{1,0:T(8,128)S(1)} collective-permute-done((f32[256,384]{1,0:T(8,128)S(1)}, f32[256,384]{1,0:T(8,128)S(1)}, u32[]{:S(2)}, u32[]{:S(2)}) %collective-permute-start.15) | collective-permute-done | bytes 393248 | tf_op jit(solution)/shard_map/ppermute | solution.py:61
  106.2 2.5 %collective-permute-done.17.refs_5_ = f32[256,384]{1,0:T(8,128)S(1)} collective-permute-done((f32[256,384]{1,0:T(8,128)S(1)}, f32[256,384]{1,0:T(8,128)S(1)}, u32[]{:S(2)}, u32[]{:S(2)}) %collective-permute-start.17) | collective-permute-done | bytes 393248 | tf_op jit(solution)/shard_map/ppermute | solution.py:61
  108.7 0.0 collective-permute-done.18.refs_7_
  108.7 1.8 %shard_map.118 = (f32[256,256]{1,0:T(8,128)}, f32[256,256]{1,0:T(8,128)}, f32[256,256]{1,0:T(8,128)}, f32[128,1024]{1,0:T(8,128)}) custom-call(s32[3]{0:T(128)S(1)} %copy-done.5, f32[512,384]{1,0:T(8,128)S(1)} %shard_map.107.kept.refs_0_, f32[512,384]{1,0:T(8,128)S(1)} %collective-permute-done.9.got.refs_1_, f32[256,384]{1,0:T(8,128)S(1)} %collective-permute-done.10.refs_2_, ...), custom_call_target="tpu_custom_call" | custom-call | tf_op jit(solution)/shard_map/pallas_call | solution.py:45
  (7 shorter events, 0.1 us)
Async XLA Ops:
  0.6 39.0 %copy-start = (f32[1,128,1024]{2,1,0:T(8,128)S(1)}, f32[1,128,1024]{2,1,0:T(8,128)}, u32[]{:S(2)}) copy-start(f32[1,128,1024]{2,1,0:T(8,128)} %param.7) | copy-start | bytes 1572868
  4.4 22.0 %collective-permute-start.1 = (f32[128,1024]{1,0:T(8,128)}, f32[128,1024]{1,0:T(8,128)S(1)}, u32[]{:S(2)}, u32[]{:S(2)}) collective-permute-start(f32[128,1024]{1,0:T(8,128)} %bitcast.7), channel_id=1, source_target_pairs={{0,2},{1,3},{2,0},{3,1},{4,6},{5,7},{6,4},{7,5},{8,10},{9,11},{10,... | collective-permute-start | bytes 1572872 | tf_op jit(solution)/shard_map/ppermute | solution.py:61
  7.4 19.1 %collective-permute-start.2 = (f32[256,384]{1,0:T(8,128)}, f32[256,384]{1,0:T(8,128)S(1)}, u32[]{:S(2)}, u32[]{:S(2)}) collective-permute-start(f32[256,384]{1,0:T(8,128)} %get-tuple-element.35.refs_0_.refs_1_), channel_id=1, source_target_pairs={{0,4},{4,0},{8,12},{12,8},{1,5},{5,1},{9,13},{13,9},{2,6},{6,2},{1... | collective-permute-start | bytes 1179656 | tf_op jit(solution)/shard_map/ppermute | solution.py:61
  9.0 19.9 %collective-permute-start.4 = (f32[256,384]{1,0:T(8,128)}, f32[256,384]{1,0:T(8,128)S(1)}, u32[]{:S(2)}, u32[]{:S(2)}) collective-permute-start(f32[256,384]{1,0:T(8,128)} %get-tuple-element.35.refs_0_.refs_1_), channel_id=1, source_target_pairs={{0,8},{4,12},{8,0},{12,4},{1,9},{5,13},{9,1},{13,5},{2,10},{6,14},... | collective-permute-start | bytes 1179656 | tf_op jit(solution)/shard_map/ppermute | solution.py:61
  11.6 19.3 %collective-permute-start = (f32[128,1024]{1,0:T(8,128)}, f32[128,1024]{1,0:T(8,128)S(1)}, u32[]{:S(2)}, u32[]{:S(2)}) collective-permute-start(f32[128,1024]{1,0:T(8,128)} %bitcast.8), channel_id=1, source_target_pairs={{0,1},{1,0},{2,3},{3,2},{4,5},{5,4},{6,7},{7,6},{8,9},{9,8},{10,11... | collective-permute-start | bytes 1572872 | tf_op jit(solution)/shard_map/ppermute | solution.py:61
  26.5 4.4 %collective-permute-start.3 = (f32[128,1024]{1,0:T(8,128)S(1)}, f32[128,1024]{1,0:T(8,128)S(1)}, u32[]{:S(2)}, u32[]{:S(2)}) collective-permute-start(f32[128,1024]{1,0:T(8,128)S(1)} %collective-permute-done.1.refs_2_), channel_id=1, source_target_pairs={{0,1},{1,0},{2,3},{3,2},{4,5},{5,4},{6,7},{7,6},{8,9},{9,8},{10,11... | collective-permute-start | bytes 1572872 | tf_op jit(solution)/shard_map/ppermute | solution.py:61
  28.9 9.2 %collective-permute-start.5 = (f32[256,384]{1,0:T(8,128)S(1)}, f32[256,384]{1,0:T(8,128)}, u32[]{:S(2)}, u32[]{:S(2)}) collective-permute-start(f32[256,384]{1,0:T(8,128)S(1)} %collective-permute-done.4.refs_2_.refs_3_), channel_id=1, source_target_pairs={{0,4},{4,0},{8,12},{12,8},{1,5},{5,1},{9,13},{13,9},{2,6},{6,2},{1... | collective-permute-start | bytes 1179656 | tf_op jit(solution)/shard_map/ppermute | solution.py:61
  29.3 13.7 %collective-permute-start.11 = (f32[256,384]{1,0:T(8,128)S(1)}, f32[256,384]{1,0:T(8,128)S(1)}, u32[]{:S(2)}, u32[]{:S(2)}) collective-permute-start(f32[256,384]{1,0:T(8,128)S(1)} %collective-permute-done.2.refs_1_.refs_2_), channel_id=1, source_target_pairs={{0,16},{16,0},{1,17},{17,1},{2,18},{18,2},{3,19},{19,3},{4,20},{20... | collective-permute-start | bytes 1179656 | tf_op jit(solution)/shard_map/ppermute | solution.py:61
  30.8 12.7 %collective-permute-start.6 = (f32[128,256]{1,0:T(8,128)}, f32[128,256]{1,0:T(8,128)S(1)}, u32[]{:S(2)}, u32[]{:S(2)}) collective-permute-start(f32[128,256]{1,0:T(8,128)} %get-tuple-element.40), channel_id=1, source_target_pairs={{0,1},{1,0},{2,3},{3,2},{4,5},{5,4},{6,7},{7,6},{8,9},{9,8},{10,11... | collective-permute-start | bytes 393224 | tf_op jit(solution)/shard_map/ppermute | solution.py:61
  30.8 12.7 %collective-permute-start.7 = (f32[128,256]{1,0:T(8,128)}, f32[128,256]{1,0:T(8,128)S(1)}, u32[]{:S(2)}, u32[]{:S(2)}) collective-permute-start(f32[128,256]{1,0:T(8,128)} %get-tuple-element.42), channel_id=1, source_target_pairs={{0,2},{1,3},{2,0},{3,1},{4,6},{5,7},{6,4},{7,5},{8,10},{9,11},{10,... | collective-permute-start | bytes 393224 | tf_op jit(solution)/shard_map/ppermute | solution.py:61
  31.4 12.1 %collective-permute-start.8 = (f32[128,256]{1,0:T(8,128)}, f32[128,256]{1,0:T(8,128)}, u32[]{:S(2)}, u32[]{:S(2)}) collective-permute-start(f32[128,256]{1,0:T(8,128)} %get-tuple-element.44), channel_id=1, source_target_pairs={{0,3},{1,2},{2,1},{3,0},{4,7},{5,6},{6,5},{7,4},{8,11},{9,10},{10,... | collective-permute-start | bytes 393224 | tf_op jit(solution)/shard_map/ppermute | solution.py:61
  33.5 6.3 %copy-start.1 = (f32[256,384]{1,0:T(8,128)S(1)}, f32[256,384]{1,0:T(8,128)}, u32[]{:S(2)}) copy-start(f32[256,384]{1,0:T(8,128)} %get-tuple-element.35.refs_0_.refs_1_) | copy-start | bytes 1179652
  33.5 6.3 %copy-start.5 = (s32[3]{0:T(128)S(1)}, s32[3]{0:T(128)}, u32[]{:S(2)}) copy-start(s32[3]{0:T(128)} %pad_add_fusion.info) | copy-start | bytes 40
  38.1 16.9 %collective-permute-start.13 = (f32[256,384]{1,0:T(8,128)}, f32[256,384]{1,0:T(8,128)S(1)}, u32[]{:S(2)}, u32[]{:S(2)}) collective-permute-start(f32[256,384]{1,0:T(8,128)} %collective-permute-done.5.refs_4_), channel_id=1, source_target_pairs={{0,16},{16,0},{1,17},{17,1},{2,18},{18,2},{3,19},{19,3},{4,20},{20... | collective-permute-start | bytes 1179656 | tf_op jit(solution)/shard_map/ppermute | solution.py:61
  39.8 3.8 %copy-start.6 = (f32[128,256]{1,0:T(8,128)S(1)}, f32[128,256]{1,0:T(8,128)}, u32[]{:S(2)}) copy-start(f32[128,256]{1,0:T(8,128)} %get-tuple-element.38.refs_5_.refs_7_) | copy-start | bytes 393220
  43.0 12.5 %collective-permute-start.12 = (f32[256,384]{1,0:T(8,128)S(1)}, f32[256,384]{1,0:T(8,128)S(1)}, u32[]{:S(2)}, u32[]{:S(2)}) collective-permute-start(f32[256,384]{1,0:T(8,128)S(1)} %collective-permute-done.4.refs_2_.refs_3_), channel_id=1, source_target_pairs={{0,16},{16,0},{1,17},{17,1},{2,18},{18,2},{3,19},{19,3},{4,20},{20... | collective-permute-start | bytes 1179656 | tf_op jit(solution)/shard_map/ppermute | solution.py:61
  51.6 3.9 %copy-start.2 = (f32[256,256]{1,0:T(8,128)S(1)}, f32[256,256]{1,0:T(8,128)}, u32[]{:S(2)}) copy-start(f32[256,256]{1,0:T(8,128)} %refs_1_.1) | copy-start | bytes 786436
  51.6 3.9 %copy-start.3 = (f32[256,256]{1,0:T(8,128)S(1)}, f32[256,256]{1,0:T(8,128)}, u32[]{:S(2)}) copy-start(f32[256,256]{1,0:T(8,128)} %refs_2_.1) | copy-start | bytes 786436
  51.6 3.9 %copy-start.4 = (f32[256,256]{1,0:T(8,128)S(1)}, f32[256,256]{1,0:T(8,128)}, u32[]{:S(2)}) copy-start(f32[256,256]{1,0:T(8,128)} %refs_3_.1) | copy-start | bytes 786436
  51.6 18.3 %collective-permute-start.9 = (f32[512,384]{1,0:T(8,128)S(1)}, f32[512,384]{1,0:T(8,128)S(1)}, u32[]{:S(2)}, u32[]{:S(2)}) collective-permute-start(f32[512,384]{1,0:T(8,128)S(1)} %shard_map.106), channel_id=1, source_target_pairs={{0,4},{4,0},{8,12},{12,8},{1,5},{5,1},{9,13},{13,9},{2,6},{6,2},{1... | collective-permute-start | bytes 2359304 | tf_op jit(solution)/shard_map/ppermute | solution.py:61
  68.7 6.6 %collective-permute-start.16 = (f32[256,1024]{1,0:T(8,128)S(1)}, f32[256,1024]{1,0:T(8,128)S(1)}, u32[]{:S(2)}, u32[]{:S(2)}) collective-permute-start(f32[256,1024]{1,0:T(8,128)S(1)} %shard_map.115), channel_id=1, source_target_pairs={{0,1},{1,0},{2,3},{3,2},{4,5},{5,4},{6,7},{7,6},{8,9},{9,8},{10,11... | collective-permute-start | bytes 3145736 | tf_op jit(solution)/shard_map/ppermute | solution.py:61
  68.7 19.8 %collective-permute-start.14 = (f32[256,384]{1,0:T(8,128)S(1)}, f32[256,384]{1,0:T(8,128)S(1)}, u32[]{:S(2)}, u32[]{:S(2)}) collective-permute-start(f32[256,384]{1,0:T(8,128)S(1)} %shard_map.110), channel_id=1, source_target_pairs={{0,4},{4,0},{8,12},{12,8},{1,5},{5,1},{9,13},{13,9},{2,6},{6,2},{1... | collective-permute-start | bytes 1179656 | tf_op jit(solution)/shard_map/ppermute | solution.py:61
  70.0 20.4 %collective-permute-start.10 = (f32[256,384]{1,0:T(8,128)S(1)}, f32[256,384]{1,0:T(8,128)S(1)}, u32[]{:S(2)}, u32[]{:S(2)}) collective-permute-start(f32[256,384]{1,0:T(8,128)S(1)} %shard_map.108), channel_id=1, source_target_pairs={{0,8},{4,12},{8,0},{12,4},{1,9},{5,13},{9,1},{13,5},{2,10},{6,14},... | collective-permute-start | bytes 1179656 | tf_op jit(solution)/shard_map/ppermute | solution.py:61
  75.4 33.3 %collective-permute-start.18 = (f32[128,1024]{1,0:T(8,128)S(1)}, f32[128,1024]{1,0:T(8,128)S(1)}, u32[]{:S(2)}, u32[]{:S(2)}) collective-permute-start(f32[128,1024]{1,0:T(8,128)S(1)} %get-tuple-element.61), channel_id=1, source_target_pairs={{0,2},{1,3},{2,0},{3,1},{4,6},{5,7},{6,4},{7,5},{8,10},{9,11},{10,... | collective-permute-start | bytes 1572872 | tf_op jit(solution)/shard_map/ppermute | solution.py:61
  88.5 17.7 %collective-permute-start.15 = (f32[256,384]{1,0:T(8,128)S(1)}, f32[256,384]{1,0:T(8,128)S(1)}, u32[]{:S(2)}, u32[]{:S(2)}) collective-permute-start(f32[256,384]{1,0:T(8,128)S(1)} %shard_map.111), channel_id=1, source_target_pairs={{0,4},{4,0},{8,12},{12,8},{1,5},{5,1},{9,13},{13,9},{2,6},{6,2},{1... | collective-permute-start | bytes 1179656 | tf_op jit(solution)/shard_map/ppermute | solution.py:61
  90.4 18.2 %collective-permute-start.17 = (f32[256,384]{1,0:T(8,128)S(1)}, f32[256,384]{1,0:T(8,128)S(1)}, u32[]{:S(2)}, u32[]{:S(2)}) collective-permute-start(f32[256,384]{1,0:T(8,128)S(1)} %shard_map.117), channel_id=1, source_target_pairs={{0,8},{4,12},{8,0},{12,4},{1,9},{5,13},{9,1},{13,5},{2,10},{6,14},... | collective-permute-start | bytes 1179656 | tf_op jit(solution)/shard_map/ppermute | solution.py:61

commit v6 on v5

--- a/solution.py
+++ b/solution.py
@@ -65,7 +65,8 @@
     return lax.optimization_barrier((value, *others))[0]
 
 
-def entry_body(parts, info, ids, sensors, wq, wk, wv, packed, *refs):
+def entry_body(parts, ids, sensors, wq, wk, wv, packed, *refs):
+    mine = lax.axis_index("ta")
     if packed is not None:
         packed[:, 0:LANES] = wq[...]
         packed[:, LANES : 2 * LANES] = wk[...]
@@ -73,36 +74,36 @@
     outs, rows = refs[:parts], refs[parts]
     count = sensors.shape[0]
     columns = outs[0].shape[1]
-    local = ids[...] - info[2] * count
+    local = ids[...] - mine * count
     chosen = lax.broadcasted_iota(jnp.int32, (count, count), 0) == local
     rows[...] = dot(chosen.astype(F32), sensors[...], NN)
     for r in range(parts):
-        start = pl.multiple_of((info[2] ^ r) * columns, LANES)
+        start = pl.multiple_of((mine ^ r) * columns, LANES)
         outs[r][...] = rows[:, pl.ds(start, columns)]
 
 
-def entry(info, ids, sensors, weights, parts, direct):
+def entry(ids, sensors, weights, parts, direct):
     rows, columns = weights[0].shape
     count, width = sensors.shape
 
     def whole(*shape):
-        return pl.BlockSpec(shape, lambda i, info: (0, 0))
-
-    spec = pl.BlockSpec((rows, LANES), lambda i, info: (0, info[1]))
+        return pl.BlockSpec(shape, lambda i: (0, 0))
+
+    spec = pl.BlockSpec((rows, LANES), lambda i: (0, lax.axis_index("grp")))
     body = entry_body if direct else adjoint_body
     outs = ([(rows, 3 * LANES)] if direct else []) + [(count, columns)] * parts
     return pl.pallas_call(
         functools.partial(body, parts),
         out_shape=[shaped(*o) for o in outs],
         grid_spec=pltpu.PrefetchScalarGridSpec(
-            num_scalar_prefetch=1,
+            num_scalar_prefetch=0,
             grid=(1,),
             in_specs=[whole(1, count), whole(count, width)] + ([spec] * 3 if direct else []),
             out_specs=[whole(*o) for o in outs],
             scratch_shapes=[pltpu.VMEM((count, width), F32)],
         ),
         compiler_params=pltpu.CompilerParams(vmem_limit_bytes=60 << 20),
-    )(info, ids, sensors, *(weights if direct else ()))
+    )(ids, sensors, *(weights if direct else ()))
 
 
 def columns_of(turn, info):
@@ -118,8 +119,8 @@
     return held
 
 
-def adjoint_body(parts, info, ids, sensors, *refs):
-    entry_body(parts, info, ids, sensors, None, None, None, None, *refs)
+def adjoint_body(parts, ids, sensors, *refs):
+    entry_body(parts, ids, sensors, None, None, None, None, *refs)
 
 
 def stack_body(parts, *refs):
@@ -306,7 +307,7 @@
     info = jnp.stack([z, y, t]).astype(jnp.int32)
     direct = rows_here % LANES == 0 and chunks == grp == 2 and wa == 4
 
-    blocks_out = entry(info, sensor_node.reshape(1, -1), sensor_adjoint[0], weights, ta, direct)
+    blocks_out = entry(sensor_node.reshape(1, -1), sensor_adjoint[0], weights, ta, direct)
     held = {0: hour_rows}
     if direct:
         first, *blocks_out = blocks_out

time: 111 us -> 109 us (0.982)
  no operation moved by 1% of the time
where the time goes in v6:
time: 109 us
  waiting for transfers between devices  49.8 us (46%)
  Pallas kernels  39.9 us (37%)
  starting transfers between devices  17.8 us (16%)
    ppermute x19, waiting for transfers between devices, swap(): return lax.ppermute(value, axis, [(i, i ^ step) for i in range(size)])  49.8 us
    pallas_call x16, Pallas kernels, local_call(): pl.pallas_call(body, out_shape=outs, in_specs=[smem] * len(scalars) + [vm...  37.3 us
    ppermute x19, starting transfers between devices, swap(): return lax.ppermute(value, axis, [(i, i ^ step) for i in range(size)])  17.8 us
    pallas_call x1, Pallas kernels, entry(): pl.pallas_call(functools.partial(body, parts), out_shape=[shaped(*o) for...  2.61 us
  transfers between devices with their start and end apart: 19, of which 8 were waited for; matrix products, arithmetic and copies ran while one was open for 1% of the time, Pallas kernels for 32%

profile of v6, /device:TPU:0, one launch (start us, length us, event | category | flops | bytes accessed | tf_op | source)
XLA Modules:
  0.0 109.2 jit_solution(12166309596274871796)
XLA Ops:
  0.6 0.0 copy-start
  0.6 2.6 %shard_map.102 = (f32[256,384]{1,0:T(8,128)}, f32[128,256]{1,0:T(8,128)}, f32[128,256]{1,0:T(8,128)}, f32[128,256]{1,0:T(8,128)}, f32[128,256]{1,0:T(8,128)}) custom-call(s32[1,128]{1,0:T(1,128)} %bitcast.11, f32[128,1024]{1,0:T(8,128)} %bitcast.10, f32[256,256]{1,0:T(8,128)} %refs_1_.1, f32[256,256]{1,0:T(8,128)} %refs_2_.1, f32[256,256]{1,0:T(8,128)} %refs_3_.1), custom_call_target="tpu_custom_call" | custom-call | tf_op jit(solution)/shard_map/pallas_call | solution.py:95
  3.3 2.9 %collective-permute-start.1 = (f32[128,1024]{1,0:T(8,128)}, f32[128,1024]{1,0:T(8,128)S(1)}, u32[]{:S(2)}, u32[]{:S(2)}) collective-permute-start(f32[128,1024]{1,0:T(8,128)} %bitcast.7), channel_id=1, source_target_pairs={{0,2},{1,3},{2,0},{3,1},{4,6},{5,7},{6,4},{7,5},{8,10},{9,11},{10,... | collective-permute-start | bytes 1572872 | tf_op jit(solution)/shard_map/ppermute | solution.py:61
  6.2 1.6 %collective-permute-start.2 = (f32[256,384]{1,0:T(8,128)}, f32[256,384]{1,0:T(8,128)S(1)}, u32[]{:S(2)}, u32[]{:S(2)}) collective-permute-start(f32[256,384]{1,0:T(8,128)} %get-tuple-element.35.refs_0_.refs_1_), channel_id=1, source_target_pairs={{0,4},{4,0},{8,12},{12,8},{1,5},{5,1},{9,13},{13,9},{2,6},{6,2},{1... | collective-permute-start | bytes 1179656 | tf_op jit(solution)/shard_map/ppermute | solution.py:61
  7.8 2.6 %collective-permute-start.4 = (f32[256,384]{1,0:T(8,128)}, f32[256,384]{1,0:T(8,128)S(1)}, u32[]{:S(2)}, u32[]{:S(2)}) collective-permute-start(f32[256,384]{1,0:T(8,128)} %get-tuple-element.35.refs_0_.refs_1_), channel_id=1, source_target_pairs={{0,8},{4,12},{8,0},{12,4},{1,9},{5,13},{9,1},{13,5},{2,10},{6,14},... | collective-permute-start | bytes 1179656 | tf_op jit(solution)/shard_map/ppermute | solution.py:61
  10.4 0.0 collective-permute-start
  10.4 14.9 %collective-permute-done.2.refs_1_.refs_2_ = f32[256,384]{1,0:T(8,128)S(1)} collective-permute-done((f32[256,384]{1,0:T(8,128)}, f32[256,384]{1,0:T(8,128)S(1)}, u32[]{:S(2)}, u32[]{:S(2)}) %collective-permute-start.2) | collective-permute-done | bytes 393248 | tf_op jit(solution)/shard_map/ppermute | solution.py:61
  25.3 0.0 collective-permute-done.1.refs_2_
  25.3 0.0 collective-permute-start.3
  25.3 2.4 %collective-permute-done.4.refs_2_.refs_3_ = f32[256,384]{1,0:T(8,128)S(1)} collective-permute-done((f32[256,384]{1,0:T(8,128)}, f32[256,384]{1,0:T(8,128)S(1)}, u32[]{:S(2)}, u32[]{:S(2)}) %collective-permute-start.4) | collective-permute-done | bytes 393248 | tf_op jit(solution)/shard_map/ppermute | solution.py:61
  27.7 0.4 collective-permute-start.5
  28.1 1.5 %collective-permute-start.11 = (f32[256,384]{1,0:T(8,128)S(1)}, f32[256,384]{1,0:T(8,128)S(1)}, u32[]{:S(2)}, u32[]{:S(2)}) collective-permute-start(f32[256,384]{1,0:T(8,128)S(1)} %collective-permute-done.2.refs_1_.refs_2_), channel_id=1, source_target_pairs={{0,16},{16,0},{1,17},{17,1},{2,18},{18,2},{3,19},{19,3},{4,20},{20... | collective-permute-start | bytes 1179656 | tf_op jit(solution)/shard_map/ppermute | solution.py:61
  29.6 0.0 collective-permute-done.refs_1_
  29.6 0.0 collective-permute-done.3.refs_3_
  29.6 0.0 collective-permute-start.6
  29.6 0.6 collective-permute-start.7
  30.2 1.3 %collective-permute-start.8 = (f32[128,256]{1,0:T(8,128)}, f32[128,256]{1,0:T(8,128)}, u32[]{:S(2)}, u32[]{:S(2)}) collective-permute-start(f32[128,256]{1,0:T(8,128)} %get-tuple-element.44), channel_id=1, source_target_pairs={{0,3},{1,2},{2,1},{3,0},{4,7},{5,6},{6,5},{7,4},{8,11},{9,10},{10,... | collective-permute-start | bytes 393224 | tf_op jit(solution)/shard_map/ppermute | solution.py:61
  31.5 0.1 pad_add_fusion.info
  31.6 0.8 copy.11.neighbours
  32.3 4.6 %collective-permute-done.5.refs_4_ = f32[256,384]{1,0:T(8,128)} collective-permute-done((f32[256,384]{1,0:T(8,128)S(1)}, f32[256,384]{1,0:T(8,128)}, u32[]{:S(2)}, u32[]{:S(2)}) %collective-permute-start.5) | collective-permute-done | bytes 393248 | tf_op jit(solution)/shard_map/ppermute | solution.py:61
  36.9 1.5 %collective-permute-start.13 = (f32[256,384]{1,0:T(8,128)}, f32[256,384]{1,0:T(8,128)S(1)}, u32[]{:S(2)}, u32[]{:S(2)}) collective-permute-start(f32[256,384]{1,0:T(8,128)} %collective-permute-done.5.refs_4_), channel_id=1, source_target_pairs={{0,16},{16,0},{1,17},{17,1},{2,18},{18,2},{3,19},{19,3},{4,20},{20... | collective-permute-start | bytes 1179656 | tf_op jit(solution)/shard_map/ppermute | solution.py:61
  38.4 0.0 copy-done
  38.4 0.1 shard_map.103.x.refs_0_
  38.6 0.0 copy-done.1
  38.6 0.0 copy-start.5
  38.6 3.2 %shard_map.104.refs_9_ = f32[512,384]{1,0:T(8,128)S(1)} custom-call(s32[3]{0:T(128)S(1)} %pad_add_fusion.info, f32[512,1024]{1,0:T(8,128)S(1)} %shard_map.103.x.refs_0_, f32[256,384]{1,0:T(8,128)S(1)} %copy-done.1, f32[256,384]{1,0:T(8,128)S(1)} %collective-permute-done.2.refs_1_.refs_2_, f32[256,384]{1,0:T(8,128)S(1)} %collective-permute-done.4.refs_2_.refs_3_), custom_call_target="tpu_custom_call" | custom-call | tf_op jit(solution)/shard_map/pallas_call | solution.py:45
  41.8 0.0 collective-permute-done.11.refs_4_
  41.8 0.6 collective-permute-start.12
  42.4 0.0 collective-permute-done.6.refs_6_.refs_8_
  42.4 0.0 collective-permute-done.7.refs_7_.refs_9_
  42.4 0.0 collective-permute-done.8.refs_8_.refs_10_
  42.4 5.5 %shard_map.105 = (f32[512,384]{1,0:T(8,128)S(1)}, f32[1024,384]{1,0:T(8,128)S(1)}) custom-call(s32[3]{0:T(128)S(1)} %pad_add_fusion.info, s32[4,2]{1,0:T(4,128)S(1)} %copy.11.neighbours, f32[512,1024]{1,0:T(8,128)S(1)} %shard_map.103.x.refs_0_, f32[256,384]{1,0:T(8,128)S(1)} %copy-done.1, f32[256,384]{1,0:T(8,128)S(1)} %collective-permute-done.2.refs_1_.refs_2_, ...), custom_call_target="tpu_custom_call" | custom-call | flops 6442450944 | bytes 25165824 | tf_op jit(solution)/shard_map/pallas_call | solution.py:45
  47.9 2.4 %shard_map.106 = f32[512,384]{1,0:T(8,128)S(1)} custom-call(s32[3]{0:T(128)S(1)} %pad_add_fusion.info, f32[512,1024]{1,0:T(8,128)S(1)} %shard_map.103.x.refs_0_, f32[512,384]{1,0:T(8,128)S(1)} %get-tuple-element.45.stacked.refs_0_), custom_call_target="tpu_custom_call" | custom-call | tf_op jit(solution)/shard_map/pallas_call | solution.py:45
  50.4 0.0 copy-start.2
  50.4 0.0 copy-start.3
  50.4 0.0 copy-start.4
  50.4 1.0 collective-permute-start.9
  51.3 2.4 %shard_map.107.kept.refs_0_ = f32[512,384]{1,0:T(8,128)S(1)} custom-call(s32[3]{0:T(128)S(1)} %pad_add_fusion.info, f32[512,1024]{1,0:T(8,128)S(1)} %shard_map.103.x.refs_0_, f32[512,384]{1,0:T(8,128)S(1)} %get-tuple-element.45.stacked.refs_0_), custom_call_target="tpu_custom_call" | custom-call | tf_op jit(solution)/shard_map/pallas_call | solution.py:45
  53.8 0.0 collective-permute-done.13.refs_6_
  53.8 0.5 collective-permute-done.12.refs_5_
  54.3 0.0 copy-done.4
  54.3 8.0 %shard_map.109 = (f32[512,384]{1,0:T(8,128)S(1)}, f32[1024,384]{1,0:T(8,128)S(1)}) custom-call(s32[3]{0:T(128)S(1)} %pad_add_fusion.info, s32[4,2]{1,0:T(4,128)S(1)} %copy.11.neighbours, f32[512,1024]{1,0:T(8,128)S(1)} %shard_map.103.x.refs_0_, f32[256,256]{1,0:T(8,128)S(1)} %copy-done.2, f32[256,256]{1,0:T(8,128)S(1)} %copy-done.3, ...), custom_call_target="tpu_custom_call" | custom-call | flops 6442450944 | bytes 25165824 | tf_op jit(solution)/shard_map/pallas_call | solution.py:45
  62.3 1.6 %shard_map.110 = f32[256,384]{1,0:T(8,128)S(1)} custom-call(s32[3]{0:T(128)S(1)} %pad_add_fusion.info, f32[512,1024]{1,0:T(8,128)S(1)} %shard_map.103.x.refs_0_, f32[512,384]{1,0:T(8,128)S(1)} %get-tuple-element.50.stacked.refs_1_), custom_call_target="tpu_custom_call" | custom-call | tf_op jit(solution)/shard_map/pallas_call | solution.py:45
  63.9 3.5 %shard_map.115 = f32[256,1024]{1,0:T(8,128)S(1)} custom-call(f32[512,384]{1,0:T(8,128)S(1)} %get-tuple-element.45.stacked.refs_0_, f32[512,384]{1,0:T(8,128)S(1)} %get-tuple-element.50.stacked.refs_1_, f32[1024,384]{1,0:T(8,128)S(1)} %get-tuple-element.56.refs_2_, f32[1024,384]{1,0:T(8,128)S(1)} %get-tuple-element.58.refs_3_), custom_call_target="tpu_custom_call" | custom-call | tf_op jit(solution)/shard_map/pallas_call | solution.py:45
  67.4 0.1 collective-permute-start.16
  67.5 1.2 %collective-permute-start.14 = (f32[256,384]{1,0:T(8,128)S(1)}, f32[256,384]{1,0:T(8,128)S(1)}, u32[]{:S(2)}, u32[]{:S(2)}) collective-permute-start(f32[256,384]{1,0:T(8,128)S(1)} %shard_map.110), channel_id=1, source_target_pairs={{0,4},{4,0},{8,12},{12,8},{1,5},{5,1},{9,13},{13,9},{2,6},{6,2},{1... | collective-permute-start | bytes 1179656 | tf_op jit(solution)/shard_map/ppermute | solution.py:61
  68.7 0.0 collective-permute-done.9.got.refs_1_
  68.8 1.5 %collective-permute-start.10 = (f32[256,384]{1,0:T(8,128)S(1)}, f32[256,384]{1,0:T(8,128)S(1)}, u32[]{:S(2)}, u32[]{:S(2)}) collective-permute-start(f32[256,384]{1,0:T(8,128)S(1)} %shard_map.108), channel_id=1, source_target_pairs={{0,8},{4,12},{8,0},{12,4},{1,9},{5,13},{9,1},{13,5},{2,10},{6,14},... | collective-permute-start | bytes 1179656 | tf_op jit(solution)/shard_map/ppermute | solution.py:61
  70.3 3.7 %shard_map.114.keep = f32[256,1024]{1,0:T(8,128)S(1)} custom-call(f32[512,384]{1,0:T(8,128)S(1)} %get-tuple-element.45.stacked.refs_0_, f32[512,384]{1,0:T(8,128)S(1)} %get-tuple-element.50.stacked.refs_1_, f32[1024,384]{1,0:T(8,128)S(1)} %get-tuple-element.56.refs_2_, f32[1024,384]{1,0:T(8,128)S(1)} %get-tuple-element.58.refs_3_), custom_call_target="tpu_custom_call" | custom-call | tf_op jit(solution)/shard_map/pallas_call | solution.py:45
  74.0 0.0 collective-permute-done.16.got
  74.0 0.1 shard_map.116
  74.1 0.6 collective-permute-start.18
  74.7 1.6 %shard_map.111 = f32[256,384]{1,0:T(8,128)S(1)} custom-call(s32[3]{0:T(128)S(1)} %pad_add_fusion.info, f32[512,1024]{1,0:T(8,128)S(1)} %shard_map.103.x.refs_0_, f32[512,384]{1,0:T(8,128)S(1)} %get-tuple-element.50.stacked.refs_1_), custom_call_target="tpu_custom_call" | custom-call | tf_op jit(solution)/shard_map/pallas_call | solution.py:45
  76.3 1.6 %shard_map.112.kept = f32[256,384]{1,0:T(8,128)S(1)} custom-call(s32[3]{0:T(128)S(1)} %pad_add_fusion.info, f32[512,1024]{1,0:T(8,128)S(1)} %shard_map.103.x.refs_0_, f32[512,384]{1,0:T(8,128)S(1)} %get-tuple-element.50.stacked.refs_1_), custom_call_target="tpu_custom_call" | custom-call | tf_op jit(solution)/shard_map/pallas_call | solution.py:45
  77.9 9.3 %collective-permute-done.14.got = f32[256,384]{1,0:T(8,128)S(1)} collective-permute-done((f32[256,384]{1,0:T(8,128)S(1)}, f32[256,384]{1,0:T(8,128)S(1)}, u32[]{:S(2)}, u32[]{:S(2)}) %collective-permute-start.14) | collective-permute-done | bytes 393248 | tf_op jit(solution)/shard_map/ppermute | solution.py:61
  87.2 0.0 collective-permute-start.15
  87.2 2.0 %collective-permute-done.10.refs_2_ = f32[256,384]{1,0:T(8,128)S(1)} collective-permute-done((f32[256,384]{1,0:T(8,128)S(1)}, f32[256,384]{1,0:T(8,128)S(1)}, u32[]{:S(2)}, u32[]{:S(2)}) %collective-permute-start.10) | collective-permute-done | bytes 393248 | tf_op jit(solution)/shard_map/ppermute | solution.py:61
  89.2 0.1 shard_map.117
  89.3 0.5 collective-permute-start.17
  89.7 1.6 %shard_map.113.refs_3_ = f32[256,384]{1,0:T(8,128)S(1)} custom-call(s32[3]{0:T(128)S(1)} %pad_add_fusion.info, f32[512,1024]{1,0:T(8,128)S(1)} %shard_map.103.x.refs_0_, f32[512,384]{1,0:T(8,128)S(1)} %get-tuple-element.50.stacked.refs_1_), custom_call_target="tpu_custom_call" | custom-call | tf_op jit(solution)/shard_map/pallas_call | solution.py:45
  91.3 13.7 %collective-permute-done.15.refs_4_ = f32[256,384]{1,0:T(8,128)S(1)} collective-permute-done((f32[256,384]{1,0:T(8,128)S(1)}, f32[256,384]{1,0:T(8,128)S(1)}, u32[]{:S(2)}, u32[]{:S(2)}) %collective-permute-start.15) | collective-permute-done | bytes 393248 | tf_op jit(solution)/shard_map/ppermute | solution.py:61
  105.0 2.4 %collective-permute-done.17.refs_5_ = f32[256,384]{1,0:T(8,128)S(1)} collective-permute-done((f32[256,384]{1,0:T(8,128)S(1)}, f32[256,384]{1,0:T(8,128)S(1)}, u32[]{:S(2)}, u32[]{:S(2)}) %collective-permute-start.17) | collective-permute-done | bytes 393248 | tf_op jit(solution)/shard_map/ppermute | solution.py:61
  107.4 0.0 collective-permute-done.18.refs_7_
  107.4 1.8 %shard_map.118 = (f32[256,256]{1,0:T(8,128)}, f32[256,256]{1,0:T(8,128)}, f32[256,256]{1,0:T(8,128)}, f32[128,1024]{1,0:T(8,128)}) custom-call(s32[3]{0:T(128)S(1)} %pad_add_fusion.info, f32[512,384]{1,0:T(8,128)S(1)} %shard_map.107.kept.refs_0_, f32[512,384]{1,0:T(8,128)S(1)} %collective-permute-done.9.got.refs_1_, ...), custom_call_target="tpu_custom_call" | custom-call | tf_op jit(solution)/shard_map/pallas_call | solution.py:45
  (5 shorter events, 0.0 us)
Async XLA Ops:
  0.6 37.8 %copy-start = (f32[1,128,1024]{2,1,0:T(8,128)S(1)}, f32[1,128,1024]{2,1,0:T(8,128)}, u32[]{:S(2)}) copy-start(f32[1,128,1024]{2,1,0:T(8,128)} %param.7) | copy-start | bytes 1572868
  3.3 22.0 %collective-permute-start.1 = (f32[128,1024]{1,0:T(8,128)}, f32[128,1024]{1,0:T(8,128)S(1)}, u32[]{:S(2)}, u32[]{:S(2)}) collective-permute-start(f32[128,1024]{1,0:T(8,128)} %bitcast.7), channel_id=1, source_target_pairs={{0,2},{1,3},{2,0},{3,1},{4,6},{5,7},{6,4},{7,5},{8,10},{9,11},{10,... | collective-permute-start | bytes 1572872 | tf_op jit(solution)/shard_map/ppermute | solution.py:61
  6.2 19.1 %collective-permute-start.2 = (f32[256,384]{1,0:T(8,128)}, f32[256,384]{1,0:T(8,128)S(1)}, u32[]{:S(2)}, u32[]{:S(2)}) collective-permute-start(f32[256,384]{1,0:T(8,128)} %get-tuple-element.35.refs_0_.refs_1_), channel_id=1, source_target_pairs={{0,4},{4,0},{8,12},{12,8},{1,5},{5,1},{9,13},{13,9},{2,6},{6,2},{1... | collective-permute-start | bytes 1179656 | tf_op jit(solution)/shard_map/ppermute | solution.py:61
  7.8 19.9 %collective-permute-start.4 = (f32[256,384]{1,0:T(8,128)}, f32[256,384]{1,0:T(8,128)S(1)}, u32[]{:S(2)}, u32[]{:S(2)}) collective-permute-start(f32[256,384]{1,0:T(8,128)} %get-tuple-element.35.refs_0_.refs_1_), channel_id=1, source_target_pairs={{0,8},{4,12},{8,0},{12,4},{1,9},{5,13},{9,1},{13,5},{2,10},{6,14},... | collective-permute-start | bytes 1179656 | tf_op jit(solution)/shard_map/ppermute | solution.py:61
  10.4 19.3 %collective-permute-start = (f32[128,1024]{1,0:T(8,128)}, f32[128,1024]{1,0:T(8,128)S(1)}, u32[]{:S(2)}, u32[]{:S(2)}) collective-permute-start(f32[128,1024]{1,0:T(8,128)} %bitcast.8), channel_id=1, source_target_pairs={{0,1},{1,0},{2,3},{3,2},{4,5},{5,4},{6,7},{7,6},{8,9},{9,8},{10,11... | collective-permute-start | bytes 1572872 | tf_op jit(solution)/shard_map/ppermute | solution.py:61
  25.3 4.3 %collective-permute-start.3 = (f32[128,1024]{1,0:T(8,128)S(1)}, f32[128,1024]{1,0:T(8,128)S(1)}, u32[]{:S(2)}, u32[]{:S(2)}) collective-permute-start(f32[128,1024]{1,0:T(8,128)S(1)} %collective-permute-done.1.refs_2_), channel_id=1, source_target_pairs={{0,1},{1,0},{2,3},{3,2},{4,5},{5,4},{6,7},{7,6},{8,9},{9,8},{10,11... | collective-permute-start | bytes 1572872 | tf_op jit(solution)/shard_map/ppermute | solution.py:61
  27.7 9.3 %collective-permute-start.5 = (f32[256,384]{1,0:T(8,128)S(1)}, f32[256,384]{1,0:T(8,128)}, u32[]{:S(2)}, u32[]{:S(2)}) collective-permute-start(f32[256,384]{1,0:T(8,128)S(1)} %collective-permute-done.4.refs_2_.refs_3_), channel_id=1, source_target_pairs={{0,4},{4,0},{8,12},{12,8},{1,5},{5,1},{9,13},{13,9},{2,6},{6,2},{1... | collective-permute-start | bytes 1179656 | tf_op jit(solution)/shard_map/ppermute | solution.py:61
  28.1 13.7 %collective-permute-start.11 = (f32[256,384]{1,0:T(8,128)S(1)}, f32[256,384]{1,0:T(8,128)S(1)}, u32[]{:S(2)}, u32[]{:S(2)}) collective-permute-start(f32[256,384]{1,0:T(8,128)S(1)} %collective-permute-done.2.refs_1_.refs_2_), channel_id=1, source_target_pairs={{0,16},{16,0},{1,17},{17,1},{2,18},{18,2},{3,19},{19,3},{4,20},{20... | collective-permute-start | bytes 1179656 | tf_op jit(solution)/shard_map/ppermute | solution.py:61
  29.6 12.7 %collective-permute-start.6 = (f32[128,256]{1,0:T(8,128)}, f32[128,256]{1,0:T(8,128)S(1)}, u32[]{:S(2)}, u32[]{:S(2)}) collective-permute-start(f32[128,256]{1,0:T(8,128)} %get-tuple-element.40), channel_id=1, source_target_pairs={{0,1},{1,0},{2,3},{3,2},{4,5},{5,4},{6,7},{7,6},{8,9},{9,8},{10,11... | collective-permute-start | bytes 393224 | tf_op jit(solution)/shard_map/ppermute | solution.py:61
  29.6 12.7 %collective-permute-start.7 = (f32[128,256]{1,0:T(8,128)}, f32[128,256]{1,0:T(8,128)S(1)}, u32[]{:S(2)}, u32[]{:S(2)}) collective-permute-start(f32[128,256]{1,0:T(8,128)} %get-tuple-element.42), channel_id=1, source_target_pairs={{0,2},{1,3},{2,0},{3,1},{4,6},{5,7},{6,4},{7,5},{8,10},{9,11},{10,... | collective-permute-start | bytes 393224 | tf_op jit(solution)/shard_map/ppermute | solution.py:61
  30.2 12.1 %collective-permute-start.8 = (f32[128,256]{1,0:T(8,128)}, f32[128,256]{1,0:T(8,128)}, u32[]{:S(2)}, u32[]{:S(2)}) collective-permute-start(f32[128,256]{1,0:T(8,128)} %get-tuple-element.44), channel_id=1, source_target_pairs={{0,3},{1,2},{2,1},{3,0},{4,7},{5,6},{6,5},{7,4},{8,11},{9,10},{10,... | collective-permute-start | bytes 393224 | tf_op jit(solution)/shard_map/ppermute | solution.py:61
  32.3 6.3 %copy-start.1 = (f32[256,384]{1,0:T(8,128)S(1)}, f32[256,384]{1,0:T(8,128)}, u32[]{:S(2)}) copy-start(f32[256,384]{1,0:T(8,128)} %get-tuple-element.35.refs_0_.refs_1_) | copy-start | bytes 1179652
  36.9 16.9 %collective-permute-start.13 = (f32[256,384]{1,0:T(8,128)}, f32[256,384]{1,0:T(8,128)S(1)}, u32[]{:S(2)}, u32[]{:S(2)}) collective-permute-start(f32[256,384]{1,0:T(8,128)} %collective-permute-done.5.refs_4_), channel_id=1, source_target_pairs={{0,16},{16,0},{1,17},{17,1},{2,18},{18,2},{3,19},{19,3},{4,20},{20... | collective-permute-start | bytes 1179656 | tf_op jit(solution)/shard_map/ppermute | solution.py:61
  38.6 3.8 %copy-start.5 = (f32[128,256]{1,0:T(8,128)S(1)}, f32[128,256]{1,0:T(8,128)}, u32[]{:S(2)}) copy-start(f32[128,256]{1,0:T(8,128)} %get-tuple-element.38.refs_5_.refs_7_) | copy-start | bytes 393220
  41.8 12.5 %collective-permute-start.12 = (f32[256,384]{1,0:T(8,128)S(1)}, f32[256,384]{1,0:T(8,128)S(1)}, u32[]{:S(2)}, u32[]{:S(2)}) collective-permute-start(f32[256,384]{1,0:T(8,128)S(1)} %collective-permute-done.4.refs_2_.refs_3_), channel_id=1, source_target_pairs={{0,16},{16,0},{1,17},{17,1},{2,18},{18,2},{3,19},{19,3},{4,20},{20... | collective-permute-start | bytes 1179656 | tf_op jit(solution)/shard_map/ppermute | solution.py:61
  50.4 3.9 %copy-start.2 = (f32[256,256]{1,0:T(8,128)S(1)}, f32[256,256]{1,0:T(8,128)}, u32[]{:S(2)}) copy-start(f32[256,256]{1,0:T(8,128)} %refs_1_.1) | copy-start | bytes 786436
  50.4 3.9 %copy-start.3 = (f32[256,256]{1,0:T(8,128)S(1)}, f32[256,256]{1,0:T(8,128)}, u32[]{:S(2)}) copy-start(f32[256,256]{1,0:T(8,128)} %refs_2_.1) | copy-start | bytes 786436
  50.4 3.9 %copy-start.4 = (f32[256,256]{1,0:T(8,128)S(1)}, f32[256,256]{1,0:T(8,128)}, u32[]{:S(2)}) copy-start(f32[256,256]{1,0:T(8,128)} %refs_3_.1) | copy-start | bytes 786436
  50.4 18.3 %collective-permute-start.9 = (f32[512,384]{1,0:T(8,128)S(1)}, f32[512,384]{1,0:T(8,128)S(1)}, u32[]{:S(2)}, u32[]{:S(2)}) collective-permute-start(f32[512,384]{1,0:T(8,128)S(1)} %shard_map.106), channel_id=1, source_target_pairs={{0,4},{4,0},{8,12},{12,8},{1,5},{5,1},{9,13},{13,9},{2,6},{6,2},{1... | collective-permute-start | bytes 2359304 | tf_op jit(solution)/shard_map/ppermute | solution.py:61
  67.4 6.6 %collective-permute-start.16 = (f32[256,1024]{1,0:T(8,128)S(1)}, f32[256,1024]{1,0:T(8,128)S(1)}, u32[]{:S(2)}, u32[]{:S(2)}) collective-permute-start(f32[256,1024]{1,0:T(8,128)S(1)} %shard_map.115), channel_id=1, source_target_pairs={{0,1},{1,0},{2,3},{3,2},{4,5},{5,4},{6,7},{7,6},{8,9},{9,8},{10,11... | collective-permute-start | bytes 3145736 | tf_op jit(solution)/shard_map/ppermute | solution.py:61
  67.5 19.7 %collective-permute-start.14 = (f32[256,384]{1,0:T(8,128)S(1)}, f32[256,384]{1,0:T(8,128)S(1)}, u32[]{:S(2)}, u32[]{:S(2)}) collective-permute-start(f32[256,384]{1,0:T(8,128)S(1)} %shard_map.110), channel_id=1, source_target_pairs={{0,4},{4,0},{8,12},{12,8},{1,5},{5,1},{9,13},{13,9},{2,6},{6,2},{1... | collective-permute-start | bytes 1179656 | tf_op jit(solution)/shard_map/ppermute | solution.py:61
  68.8 20.5 %collective-permute-start.10 = (f32[256,384]{1,0:T(8,128)S(1)}, f32[256,384]{1,0:T(8,128)S(1)}, u32[]{:S(2)}, u32[]{:S(2)}) collective-permute-start(f32[256,384]{1,0:T(8,128)S(1)} %shard_map.108), channel_id=1, source_target_pairs={{0,8},{4,12},{8,0},{12,4},{1,9},{5,13},{9,1},{13,5},{2,10},{6,14},... | collective-permute-start | bytes 1179656 | tf_op jit(solution)/shard_map/ppermute | solution.py:61
  74.1 33.3 %collective-permute-start.18 = (f32[128,1024]{1,0:T(8,128)S(1)}, f32[128,1024]{1,0:T(8,128)S(1)}, u32[]{:S(2)}, u32[]{:S(2)}) collective-permute-start(f32[128,1024]{1,0:T(8,128)S(1)} %get-tuple-element.61), channel_id=1, source_target_pairs={{0,2},{1,3},{2,0},{3,1},{4,6},{5,7},{6,4},{7,5},{8,10},{9,11},{10,... | collective-permute-start | bytes 1572872 | tf_op jit(solution)/shard_map/ppermute | solution.py:61
  87.2 17.8 %collective-permute-start.15 = (f32[256,384]{1,0:T(8,128)S(1)}, f32[256,384]{1,0:T(8,128)S(1)}, u32[]{:S(2)}, u32[]{:S(2)}) collective-permute-start(f32[256,384]{1,0:T(8,128)S(1)} %shard_map.111), channel_id=1, source_target_pairs={{0,4},{4,0},{8,12},{12,8},{1,5},{5,1},{9,13},{13,9},{2,6},{6,2},{1... | collective-permute-start | bytes 1179656 | tf_op jit(solution)/shard_map/ppermute | solution.py:61
  89.3 18.1 %collective-permute-start.17 = (f32[256,384]{1,0:T(8,128)S(1)}, f32[256,384]{1,0:T(8,128)S(1)}, u32[]{:S(2)}, u32[]{:S(2)}) collective-permute-start(f32[256,384]{1,0:T(8,128)S(1)} %shard_map.117), channel_id=1, source_target_pairs={{0,8},{4,12},{8,0},{12,4},{1,9},{5,13},{9,1},{13,5},{2,10},{6,14},... | collective-permute-start | bytes 1179656 | tf_op jit(solution)/shard_map/ppermute | solution.py:61

commit v7 on v6

--- a/solution.py
+++ b/solution.py
@@ -237,7 +237,9 @@
 def weight_grad_body(shares, rows, info, x, stacked, out):
     for j, r in enumerate(shares):
         start = pl.multiple_of((info[0] ^ r) * rows, LANES)
-        out[j * rows : (j + 1) * rows, :] = dot(x[:, pl.ds(start, rows)], stacked[...], TN)
+        out[j * rows : (j + 1) * rows, :] = dot_halves(
+            halves_of(x[:, pl.ds(start, rows)]), halves_of(stacked[...]), TN
+        )
 
 
 def whole_grad_body(x, stacked, out):

time: 109 us -> 109 us (level)
  Pallas kernels: 39.9 us -> 36.4 us
  waiting for transfers between devices: 49.8 us -> 52.9 us
    pallas_call x16, Pallas kernels: 37.3 us -> 33.8 us  [local_call(): pl.pallas_call(body, out_shape=outs, in_specs=[smem] * len(scalars) + [vm...]
    ppermute x19, waiting for transfers between devices: 49.8 us -> 52.9 us  [swap(): return lax.ppermute(value, axis, [(i, i ^ step) for i in range(size)])]
  transfers between devices with their start and end apart: 19 -> 19, of which waited for: 8 -> 8; matrix products, arithmetic and copies ran while one was open for 1% -> 1% of each run, Pallas kernels for 32% -> 29%
where the time goes in v7:
time: 109 us
  waiting for transfers between devices  52.9 us (49%)
  Pallas kernels  36.4 us (33%)
  starting transfers between devices  17.8 us (16%)
    ppermute x19, waiting for transfers between devices, swap(): return lax.ppermute(value, axis, [(i, i ^ step) for i in range(size)])  52.9 us
    pallas_call x16, Pallas kernels, local_call(): pl.pallas_call(body, out_shape=outs, in_specs=[smem] * len(scalars) + [vm...  33.8 us
    ppermute x19, starting transfers between devices, swap(): return lax.ppermute(value, axis, [(i, i ^ step) for i in range(size)])  17.8 us
    pallas_call x1, Pallas kernels, entry(): pl.pallas_call(functools.partial(body, parts), out_shape=[shaped(*o) for...  2.61 us
  transfers between devices with their start and end apart: 19, of which 8 were waited for; matrix products, arithmetic and copies ran while one was open for 1% of the time, Pallas kernels for 29%

profile of v7, /device:TPU:0, one launch (start us, length us, event | category | flops | bytes accessed | tf_op | source)
XLA Modules:
  0.0 108.9 jit_solution(3100858124699143184)
XLA Ops:
  0.6 0.0 copy-start
  0.6 2.6 %shard_map.102 = (f32[256,384]{1,0:T(8,128)}, f32[128,256]{1,0:T(8,128)}, f32[128,256]{1,0:T(8,128)}, f32[128,256]{1,0:T(8,128)}, f32[128,256]{1,0:T(8,128)}) custom-call(s32[1,128]{1,0:T(1,128)} %bitcast.11, f32[128,1024]{1,0:T(8,128)} %bitcast.10, f32[256,256]{1,0:T(8,128)} %refs_1_.1, f32[256,256]{1,0:T(8,128)} %refs_2_.1, f32[256,256]{1,0:T(8,128)} %refs_3_.1), custom_call_target="tpu_custom_call" | custom-call | tf_op jit(solution)/shard_map/pallas_call | solution.py:95
  3.3 2.9 %collective-permute-start.1 = (f32[128,1024]{1,0:T(8,128)}, f32[128,1024]{1,0:T(8,128)S(1)}, u32[]{:S(2)}, u32[]{:S(2)}) collective-permute-start(f32[128,1024]{1,0:T(8,128)} %bitcast.7), channel_id=1, source_target_pairs={{0,2},{1,3},{2,0},{3,1},{4,6},{5,7},{6,4},{7,5},{8,10},{9,11},{10,... | collective-permute-start | bytes 1572872 | tf_op jit(solution)/shard_map/ppermute | solution.py:61
  6.2 1.6 %collective-permute-start.2 = (f32[256,384]{1,0:T(8,128)}, f32[256,384]{1,0:T(8,128)S(1)}, u32[]{:S(2)}, u32[]{:S(2)}) collective-permute-start(f32[256,384]{1,0:T(8,128)} %get-tuple-element.35.refs_0_.refs_1_), channel_id=1, source_target_pairs={{0,4},{4,0},{8,12},{12,8},{1,5},{5,1},{9,13},{13,9},{2,6},{6,2},{1... | collective-permute-start | bytes 1179656 | tf_op jit(solution)/shard_map/ppermute | solution.py:61
  7.8 2.6 %collective-permute-start.4 = (f32[256,384]{1,0:T(8,128)}, f32[256,384]{1,0:T(8,128)S(1)}, u32[]{:S(2)}, u32[]{:S(2)}) collective-permute-start(f32[256,384]{1,0:T(8,128)} %get-tuple-element.35.refs_0_.refs_1_), channel_id=1, source_target_pairs={{0,8},{4,12},{8,0},{12,4},{1,9},{5,13},{9,1},{13,5},{2,10},{6,14},... | collective-permute-start | bytes 1179656 | tf_op jit(solution)/shard_map/ppermute | solution.py:61
  10.4 0.0 collective-permute-start
  10.4 14.9 %collective-permute-done.2.refs_1_.refs_2_ = f32[256,384]{1,0:T(8,128)S(1)} collective-permute-done((f32[256,384]{1,0:T(8,128)}, f32[256,384]{1,0:T(8,128)S(1)}, u32[]{:S(2)}, u32[]{:S(2)}) %collective-permute-start.2) | collective-permute-done | bytes 393248 | tf_op jit(solution)/shard_map/ppermute | solution.py:61
  25.3 0.0 collective-permute-done.1.refs_2_
  25.3 0.0 collective-permute-start.3
  25.3 2.4 %collective-permute-done.4.refs_2_.refs_3_ = f32[256,384]{1,0:T(8,128)S(1)} collective-permute-done((f32[256,384]{1,0:T(8,128)}, f32[256,384]{1,0:T(8,128)S(1)}, u32[]{:S(2)}, u32[]{:S(2)}) %collective-permute-start.4) | collective-permute-done | bytes 393248 | tf_op jit(solution)/shard_map/ppermute | solution.py:61
  27.7 0.4 collective-permute-start.5
  28.1 1.5 %collective-permute-start.11 = (f32[256,384]{1,0:T(8,128)S(1)}, f32[256,384]{1,0:T(8,128)S(1)}, u32[]{:S(2)}, u32[]{:S(2)}) collective-permute-start(f32[256,384]{1,0:T(8,128)S(1)} %collective-permute-done.2.refs_1_.refs_2_), channel_id=1, source_target_pairs={{0,16},{16,0},{1,17},{17,1},{2,18},{18,2},{3,19},{19,3},{4,20},{20... | collective-permute-start | bytes 1179656 | tf_op jit(solution)/shard_map/ppermute | solution.py:61
  29.6 0.0 collective-permute-done.refs_1_
  29.6 0.0 collective-permute-done.3.refs_3_
  29.6 0.0 collective-permute-start.6
  29.6 0.6 collective-permute-start.7
  30.2 1.3 %collective-permute-start.8 = (f32[128,256]{1,0:T(8,128)}, f32[128,256]{1,0:T(8,128)}, u32[]{:S(2)}, u32[]{:S(2)}) collective-permute-start(f32[128,256]{1,0:T(8,128)} %get-tuple-element.44), channel_id=1, source_target_pairs={{0,3},{1,2},{2,1},{3,0},{4,7},{5,6},{6,5},{7,4},{8,11},{9,10},{10,... | collective-permute-start | bytes 393224 | tf_op jit(solution)/shard_map/ppermute | solution.py:61
  31.5 0.1 pad_add_fusion.info
  31.6 0.8 copy.11.neighbours
  32.3 4.6 %collective-permute-done.5.refs_4_ = f32[256,384]{1,0:T(8,128)} collective-permute-done((f32[256,384]{1,0:T(8,128)S(1)}, f32[256,384]{1,0:T(8,128)}, u32[]{:S(2)}, u32[]{:S(2)}) %collective-permute-start.5) | collective-permute-done | bytes 393248 | tf_op jit(solution)/shard_map/ppermute | solution.py:61
  36.9 1.5 %collective-permute-start.13 = (f32[256,384]{1,0:T(8,128)}, f32[256,384]{1,0:T(8,128)S(1)}, u32[]{:S(2)}, u32[]{:S(2)}) collective-permute-start(f32[256,384]{1,0:T(8,128)} %collective-permute-done.5.refs_4_), channel_id=1, source_target_pairs={{0,16},{16,0},{1,17},{17,1},{2,18},{18,2},{3,19},{19,3},{4,20},{20... | collective-permute-start | bytes 1179656 | tf_op jit(solution)/shard_map/ppermute | solution.py:61
  38.4 0.0 copy-done
  38.4 0.1 shard_map.103.x.refs_0_
  38.6 0.0 copy-start.5
  38.6 3.2 %shard_map.104.refs_9_ = f32[512,384]{1,0:T(8,128)S(1)} custom-call(s32[3]{0:T(128)S(1)} %pad_add_fusion.info, f32[512,1024]{1,0:T(8,128)S(1)} %shard_map.103.x.refs_0_, f32[256,384]{1,0:T(8,128)S(1)} %copy-done.1, f32[256,384]{1,0:T(8,128)S(1)} %collective-permute-done.2.refs_1_.refs_2_, f32[256,384]{1,0:T(8,128)S(1)} %collective-permute-done.4.refs_2_.refs_3_), custom_call_target="tpu_custom_call" | custom-call | tf_op jit(solution)/shard_map/pallas_call | solution.py:45
  41.8 0.0 collective-permute-done.11.refs_4_
  41.8 0.6 collective-permute-start.12
  42.4 0.0 collective-permute-done.6.refs_6_.refs_8_
  42.4 0.0 collective-permute-done.7.refs_7_.refs_9_
  42.4 0.0 collective-permute-done.8.refs_8_.refs_10_
  42.4 0.0 copy-done.5
  42.4 5.5 %shard_map.105 = (f32[512,384]{1,0:T(8,128)S(1)}, f32[1024,384]{1,0:T(8,128)S(1)}) custom-call(s32[3]{0:T(128)S(1)} %pad_add_fusion.info, s32[4,2]{1,0:T(4,128)S(1)} %copy.11.neighbours, f32[512,1024]{1,0:T(8,128)S(1)} %shard_map.103.x.refs_0_, f32[256,384]{1,0:T(8,128)S(1)} %copy-done.1, f32[256,384]{1,0:T(8,128)S(1)} %collective-permute-done.2.refs_1_.refs_2_, ...), custom_call_target="tpu_custom_call" | custom-call | flops 6442450944 | bytes 25165824 | tf_op jit(solution)/shard_map/pallas_call | solution.py:45
  47.9 1.6 %shard_map.106 = f32[512,384]{1,0:T(8,128)S(1)} custom-call(s32[3]{0:T(128)S(1)} %pad_add_fusion.info, f32[512,1024]{1,0:T(8,128)S(1)} %shard_map.103.x.refs_0_, f32[512,384]{1,0:T(8,128)S(1)} %get-tuple-element.45.stacked.refs_0_), custom_call_target="tpu_custom_call" | custom-call | tf_op jit(solution)/shard_map/pallas_call | solution.py:45
  49.6 0.0 copy-start.2
  49.6 0.0 copy-start.3
  49.6 0.0 copy-start.4
  49.6 0.9 collective-permute-start.9
  50.5 1.6 %shard_map.107.kept.refs_0_ = f32[512,384]{1,0:T(8,128)S(1)} custom-call(s32[3]{0:T(128)S(1)} %pad_add_fusion.info, f32[512,1024]{1,0:T(8,128)S(1)} %shard_map.103.x.refs_0_, f32[512,384]{1,0:T(8,128)S(1)} %get-tuple-element.45.stacked.refs_0_), custom_call_target="tpu_custom_call" | custom-call | tf_op jit(solution)/shard_map/pallas_call | solution.py:45
  52.1 0.0 collective-permute-done.13.refs_6_
  52.1 2.1 %collective-permute-done.12.refs_5_ = f32[256,384]{1,0:T(8,128)S(1)} collective-permute-done((f32[256,384]{1,0:T(8,128)S(1)}, f32[256,384]{1,0:T(8,128)S(1)}, u32[]{:S(2)}, u32[]{:S(2)}) %collective-permute-start.12) | collective-permute-done | bytes 393248 | tf_op jit(solution)/shard_map/ppermute | solution.py:61
  54.3 0.0 copy-done.2
  54.3 8.0 %shard_map.109 = (f32[512,384]{1,0:T(8,128)S(1)}, f32[1024,384]{1,0:T(8,128)S(1)}) custom-call(s32[3]{0:T(128)S(1)} %pad_add_fusion.info, s32[4,2]{1,0:T(4,128)S(1)} %copy.11.neighbours, f32[512,1024]{1,0:T(8,128)S(1)} %shard_map.103.x.refs_0_, f32[256,256]{1,0:T(8,128)S(1)} %copy-done.2, f32[256,256]{1,0:T(8,128)S(1)} %copy-done.3, ...), custom_call_target="tpu_custom_call" | custom-call | flops 6442450944 | bytes 25165824 | tf_op jit(solution)/shard_map/pallas_call | solution.py:45
  62.3 1.2 %shard_map.110 = f32[256,384]{1,0:T(8,128)S(1)} custom-call(s32[3]{0:T(128)S(1)} %pad_add_fusion.info, f32[512,1024]{1,0:T(8,128)S(1)} %shard_map.103.x.refs_0_, f32[512,384]{1,0:T(8,128)S(1)} %get-tuple-element.50.stacked.refs_1_), custom_call_target="tpu_custom_call" | custom-call | tf_op jit(solution)/shard_map/pallas_call | solution.py:45
  63.5 3.5 %shard_map.115 = f32[256,1024]{1,0:T(8,128)S(1)} custom-call(f32[512,384]{1,0:T(8,128)S(1)} %get-tuple-element.45.stacked.refs_0_, f32[512,384]{1,0:T(8,128)S(1)} %get-tuple-element.50.stacked.refs_1_, f32[1024,384]{1,0:T(8,128)S(1)} %get-tuple-element.56.refs_2_, f32[1024,384]{1,0:T(8,128)S(1)} %get-tuple-element.58.refs_3_), custom_call_target="tpu_custom_call" | custom-call | tf_op jit(solution)/shard_map/pallas_call | solution.py:45
  67.0 0.1 collective-permute-start.16
  67.1 1.2 %collective-permute-start.14 = (f32[256,384]{1,0:T(8,128)S(1)}, f32[256,384]{1,0:T(8,128)S(1)}, u32[]{:S(2)}, u32[]{:S(2)}) collective-permute-start(f32[256,384]{1,0:T(8,128)S(1)} %shard_map.110), channel_id=1, source_target_pairs={{0,4},{4,0},{8,12},{12,8},{1,5},{5,1},{9,13},{13,9},{2,6},{6,2},{1... | collective-permute-start | bytes 1179656 | tf_op jit(solution)/shard_map/ppermute | solution.py:61
  68.3 0.0 collective-permute-done.9.got.refs_1_
  68.4 1.5 %collective-permute-start.10 = (f32[256,384]{1,0:T(8,128)S(1)}, f32[256,384]{1,0:T(8,128)S(1)}, u32[]{:S(2)}, u32[]{:S(2)}) collective-permute-start(f32[256,384]{1,0:T(8,128)S(1)} %shard_map.108), channel_id=1, source_target_pairs={{0,8},{4,12},{8,0},{12,4},{1,9},{5,13},{9,1},{13,5},{2,10},{6,14},... | collective-permute-start | bytes 1179656 | tf_op jit(solution)/shard_map/ppermute | solution.py:61
  69.9 3.5 %shard_map.114.keep = f32[256,1024]{1,0:T(8,128)S(1)} custom-call(f32[512,384]{1,0:T(8,128)S(1)} %get-tuple-element.45.stacked.refs_0_, f32[512,384]{1,0:T(8,128)S(1)} %get-tuple-element.50.stacked.refs_1_, f32[1024,384]{1,0:T(8,128)S(1)} %get-tuple-element.56.refs_2_, f32[1024,384]{1,0:T(8,128)S(1)} %get-tuple-element.58.refs_3_), custom_call_target="tpu_custom_call" | custom-call | tf_op jit(solution)/shard_map/pallas_call | solution.py:45
  73.4 0.0 collective-permute-done.16.got
  73.4 0.1 shard_map.116
  73.5 0.6 collective-permute-start.18
  74.1 1.2 %shard_map.111 = f32[256,384]{1,0:T(8,128)S(1)} custom-call(s32[3]{0:T(128)S(1)} %pad_add_fusion.info, f32[512,1024]{1,0:T(8,128)S(1)} %shard_map.103.x.refs_0_, f32[512,384]{1,0:T(8,128)S(1)} %get-tuple-element.50.stacked.refs_1_), custom_call_target="tpu_custom_call" | custom-call | tf_op jit(solution)/shard_map/pallas_call | solution.py:45
  75.3 1.2 %shard_map.112.kept = f32[256,384]{1,0:T(8,128)S(1)} custom-call(s32[3]{0:T(128)S(1)} %pad_add_fusion.info, f32[512,1024]{1,0:T(8,128)S(1)} %shard_map.103.x.refs_0_, f32[512,384]{1,0:T(8,128)S(1)} %get-tuple-element.50.stacked.refs_1_), custom_call_target="tpu_custom_call" | custom-call | tf_op jit(solution)/shard_map/pallas_call | solution.py:45
  76.5 10.4 %collective-permute-done.14.got = f32[256,384]{1,0:T(8,128)S(1)} collective-permute-done((f32[256,384]{1,0:T(8,128)S(1)}, f32[256,384]{1,0:T(8,128)S(1)}, u32[]{:S(2)}, u32[]{:S(2)}) %collective-permute-start.14) | collective-permute-done | bytes 393248 | tf_op jit(solution)/shard_map/ppermute | solution.py:61
  86.9 0.0 collective-permute-start.15
  86.9 1.9 %collective-permute-done.10.refs_2_ = f32[256,384]{1,0:T(8,128)S(1)} collective-permute-done((f32[256,384]{1,0:T(8,128)S(1)}, f32[256,384]{1,0:T(8,128)S(1)}, u32[]{:S(2)}, u32[]{:S(2)}) %collective-permute-start.10) | collective-permute-done | bytes 393248 | tf_op jit(solution)/shard_map/ppermute | solution.py:61
  88.8 0.1 shard_map.117
  88.8 0.5 collective-permute-start.17
  89.3 1.2 %shard_map.113.refs_3_ = f32[256,384]{1,0:T(8,128)S(1)} custom-call(s32[3]{0:T(128)S(1)} %pad_add_fusion.info, f32[512,1024]{1,0:T(8,128)S(1)} %shard_map.103.x.refs_0_, f32[512,384]{1,0:T(8,128)S(1)} %get-tuple-element.50.stacked.refs_1_), custom_call_target="tpu_custom_call" | custom-call | tf_op jit(solution)/shard_map/pallas_call | solution.py:45
  90.5 14.1 %collective-permute-done.15.refs_4_ = f32[256,384]{1,0:T(8,128)S(1)} collective-permute-done((f32[256,384]{1,0:T(8,128)S(1)}, f32[256,384]{1,0:T(8,128)S(1)}, u32[]{:S(2)}, u32[]{:S(2)}) %collective-permute-start.15) | collective-permute-done | bytes 393248 | tf_op jit(solution)/shard_map/ppermute | solution.py:61
  104.6 2.4 %collective-permute-done.17.refs_5_ = f32[256,384]{1,0:T(8,128)S(1)} collective-permute-done((f32[256,384]{1,0:T(8,128)S(1)}, f32[256,384]{1,0:T(8,128)S(1)}, u32[]{:S(2)}, u32[]{:S(2)}) %collective-permute-start.17) | collective-permute-done | bytes 393248 | tf_op jit(solution)/shard_map/ppermute | solution.py:61
  107.1 0.0 collective-permute-done.18.refs_7_
  107.1 1.8 %shard_map.118 = (f32[256,256]{1,0:T(8,128)}, f32[256,256]{1,0:T(8,128)}, f32[256,256]{1,0:T(8,128)}, f32[128,1024]{1,0:T(8,128)}) custom-call(s32[3]{0:T(128)S(1)} %pad_add_fusion.info, f32[512,384]{1,0:T(8,128)S(1)} %shard_map.107.kept.refs_0_, f32[512,384]{1,0:T(8,128)S(1)} %collective-permute-done.9.got.refs_1_, ...), custom_call_target="tpu_custom_call" | custom-call | tf_op jit(solution)/shard_map/pallas_call | solution.py:45
  (5 shorter events, 0.0 us)
Async XLA Ops:
  0.6 37.8 %copy-start = (f32[1,128,1024]{2,1,0:T(8,128)S(1)}, f32[1,128,1024]{2,1,0:T(8,128)}, u32[]{:S(2)}) copy-start(f32[1,128,1024]{2,1,0:T(8,128)} %param.7) | copy-start | bytes 1572868
  3.3 22.0 %collective-permute-start.1 = (f32[128,1024]{1,0:T(8,128)}, f32[128,1024]{1,0:T(8,128)S(1)}, u32[]{:S(2)}, u32[]{:S(2)}) collective-permute-start(f32[128,1024]{1,0:T(8,128)} %bitcast.7), channel_id=1, source_target_pairs={{0,2},{1,3},{2,0},{3,1},{4,6},{5,7},{6,4},{7,5},{8,10},{9,11},{10,... | collective-permute-start | bytes 1572872 | tf_op jit(solution)/shard_map/ppermute | solution.py:61
  6.2 19.1 %collective-permute-start.2 = (f32[256,384]{1,0:T(8,128)}, f32[256,384]{1,0:T(8,128)S(1)}, u32[]{:S(2)}, u32[]{:S(2)}) collective-permute-start(f32[256,384]{1,0:T(8,128)} %get-tuple-element.35.refs_0_.refs_1_), channel_id=1, source_target_pairs={{0,4},{4,0},{8,12},{12,8},{1,5},{5,1},{9,13},{13,9},{2,6},{6,2},{1... | collective-permute-start | bytes 1179656 | tf_op jit(solution)/shard_map/ppermute | solution.py:61
  7.8 19.9 %collective-permute-start.4 = (f32[256,384]{1,0:T(8,128)}, f32[256,384]{1,0:T(8,128)S(1)}, u32[]{:S(2)}, u32[]{:S(2)}) collective-permute-start(f32[256,384]{1,0:T(8,128)} %get-tuple-element.35.refs_0_.refs_1_), channel_id=1, source_target_pairs={{0,8},{4,12},{8,0},{12,4},{1,9},{5,13},{9,1},{13,5},{2,10},{6,14},... | collective-permute-start | bytes 1179656 | tf_op jit(solution)/shard_map/ppermute | solution.py:61
  10.4 19.3 %collective-permute-start = (f32[128,1024]{1,0:T(8,128)}, f32[128,1024]{1,0:T(8,128)S(1)}, u32[]{:S(2)}, u32[]{:S(2)}) collective-permute-start(f32[128,1024]{1,0:T(8,128)} %bitcast.8), channel_id=1, source_target_pairs={{0,1},{1,0},{2,3},{3,2},{4,5},{5,4},{6,7},{7,6},{8,9},{9,8},{10,11... | collective-permute-start | bytes 1572872 | tf_op jit(solution)/shard_map/ppermute | solution.py:61
  25.3 4.3 %collective-permute-start.3 = (f32[128,1024]{1,0:T(8,128)S(1)}, f32[128,1024]{1,0:T(8,128)S(1)}, u32[]{:S(2)}, u32[]{:S(2)}) collective-permute-start(f32[128,1024]{1,0:T(8,128)S(1)} %collective-permute-done.1.refs_2_), channel_id=1, source_target_pairs={{0,1},{1,0},{2,3},{3,2},{4,5},{5,4},{6,7},{7,6},{8,9},{9,8},{10,11... | collective-permute-start | bytes 1572872 | tf_op jit(solution)/shard_map/ppermute | solution.py:61
  27.7 9.3 %collective-permute-start.5 = (f32[256,384]{1,0:T(8,128)S(1)}, f32[256,384]{1,0:T(8,128)}, u32[]{:S(2)}, u32[]{:S(2)}) collective-permute-start(f32[256,384]{1,0:T(8,128)S(1)} %collective-permute-done.4.refs_2_.refs_3_), channel_id=1, source_target_pairs={{0,4},{4,0},{8,12},{12,8},{1,5},{5,1},{9,13},{13,9},{2,6},{6,2},{1... | collective-permute-start | bytes 1179656 | tf_op jit(solution)/shard_map/ppermute | solution.py:61
  28.1 13.7 %collective-permute-start.11 = (f32[256,384]{1,0:T(8,128)S(1)}, f32[256,384]{1,0:T(8,128)S(1)}, u32[]{:S(2)}, u32[]{:S(2)}) collective-permute-start(f32[256,384]{1,0:T(8,128)S(1)} %collective-permute-done.2.refs_1_.refs_2_), channel_id=1, source_target_pairs={{0,16},{16,0},{1,17},{17,1},{2,18},{18,2},{3,19},{19,3},{4,20},{20... | collective-permute-start | bytes 1179656 | tf_op jit(solution)/shard_map/ppermute | solution.py:61
  29.6 12.7 %collective-permute-start.6 = (f32[128,256]{1,0:T(8,128)}, f32[128,256]{1,0:T(8,128)S(1)}, u32[]{:S(2)}, u32[]{:S(2)}) collective-permute-start(f32[128,256]{1,0:T(8,128)} %get-tuple-element.40), channel_id=1, source_target_pairs={{0,1},{1,0},{2,3},{3,2},{4,5},{5,4},{6,7},{7,6},{8,9},{9,8},{10,11... | collective-permute-start | bytes 393224 | tf_op jit(solution)/shard_map/ppermute | solution.py:61
  29.6 12.7 %collective-permute-start.7 = (f32[128,256]{1,0:T(8,128)}, f32[128,256]{1,0:T(8,128)S(1)}, u32[]{:S(2)}, u32[]{:S(2)}) collective-permute-start(f32[128,256]{1,0:T(8,128)} %get-tuple-element.42), channel_id=1, source_target_pairs={{0,2},{1,3},{2,0},{3,1},{4,6},{5,7},{6,4},{7,5},{8,10},{9,11},{10,... | collective-permute-start | bytes 393224 | tf_op jit(solution)/shard_map/ppermute | solution.py:61
  30.2 12.1 %collective-permute-start.8 = (f32[128,256]{1,0:T(8,128)}, f32[128,256]{1,0:T(8,128)}, u32[]{:S(2)}, u32[]{:S(2)}) collective-permute-start(f32[128,256]{1,0:T(8,128)} %get-tuple-element.44), channel_id=1, source_target_pairs={{0,3},{1,2},{2,1},{3,0},{4,7},{5,6},{6,5},{7,4},{8,11},{9,10},{10,... | collective-permute-start | bytes 393224 | tf_op jit(solution)/shard_map/ppermute | solution.py:61
  32.3 6.3 %copy-start.1 = (f32[256,384]{1,0:T(8,128)S(1)}, f32[256,384]{1,0:T(8,128)}, u32[]{:S(2)}) copy-start(f32[256,384]{1,0:T(8,128)} %get-tuple-element.35.refs_0_.refs_1_) | copy-start | bytes 1179652
  36.9 15.2 %collective-permute-start.13 = (f32[256,384]{1,0:T(8,128)}, f32[256,384]{1,0:T(8,128)S(1)}, u32[]{:S(2)}, u32[]{:S(2)}) collective-permute-start(f32[256,384]{1,0:T(8,128)} %collective-permute-done.5.refs_4_), channel_id=1, source_target_pairs={{0,16},{16,0},{1,17},{17,1},{2,18},{18,2},{3,19},{19,3},{4,20},{20... | collective-permute-start | bytes 1179656 | tf_op jit(solution)/shard_map/ppermute | solution.py:61
  38.6 3.8 %copy-start.5 = (f32[128,256]{1,0:T(8,128)S(1)}, f32[128,256]{1,0:T(8,128)}, u32[]{:S(2)}) copy-start(f32[128,256]{1,0:T(8,128)} %get-tuple-element.38.refs_5_.refs_7_) | copy-start | bytes 393220
  41.8 12.5 %collective-permute-start.12 = (f32[256,384]{1,0:T(8,128)S(1)}, f32[256,384]{1,0:T(8,128)S(1)}, u32[]{:S(2)}, u32[]{:S(2)}) collective-permute-start(f32[256,384]{1,0:T(8,128)S(1)} %collective-permute-done.4.refs_2_.refs_3_), channel_id=1, source_target_pairs={{0,16},{16,0},{1,17},{17,1},{2,18},{18,2},{3,19},{19,3},{4,20},{20... | collective-permute-start | bytes 1179656 | tf_op jit(solution)/shard_map/ppermute | solution.py:61
  49.6 4.7 %copy-start.2 = (f32[256,256]{1,0:T(8,128)S(1)}, f32[256,256]{1,0:T(8,128)}, u32[]{:S(2)}) copy-start(f32[256,256]{1,0:T(8,128)} %refs_1_.1) | copy-start | bytes 786436
  49.6 4.7 %copy-start.3 = (f32[256,256]{1,0:T(8,128)S(1)}, f32[256,256]{1,0:T(8,128)}, u32[]{:S(2)}) copy-start(f32[256,256]{1,0:T(8,128)} %refs_2_.1) | copy-start | bytes 786436
  49.6 4.7 %copy-start.4 = (f32[256,256]{1,0:T(8,128)S(1)}, f32[256,256]{1,0:T(8,128)}, u32[]{:S(2)}) copy-start(f32[256,256]{1,0:T(8,128)} %refs_3_.1) | copy-start | bytes 786436
  49.6 18.7 %collective-permute-start.9 = (f32[512,384]{1,0:T(8,128)S(1)}, f32[512,384]{1,0:T(8,128)S(1)}, u32[]{:S(2)}, u32[]{:S(2)}) collective-permute-start(f32[512,384]{1,0:T(8,128)S(1)} %shard_map.106), channel_id=1, source_target_pairs={{0,4},{4,0},{8,12},{12,8},{1,5},{5,1},{9,13},{13,9},{2,6},{6,2},{1... | collective-permute-start | bytes 2359304 | tf_op jit(solution)/shard_map/ppermute | solution.py:61
  67.0 6.3 %collective-permute-start.16 = (f32[256,1024]{1,0:T(8,128)S(1)}, f32[256,1024]{1,0:T(8,128)S(1)}, u32[]{:S(2)}, u32[]{:S(2)}) collective-permute-start(f32[256,1024]{1,0:T(8,128)S(1)} %shard_map.115), channel_id=1, source_target_pairs={{0,1},{1,0},{2,3},{3,2},{4,5},{5,4},{6,7},{7,6},{8,9},{9,8},{10,11... | collective-permute-start | bytes 3145736 | tf_op jit(solution)/shard_map/ppermute | solution.py:61
  67.1 19.8 %collective-permute-start.14 = (f32[256,384]{1,0:T(8,128)S(1)}, f32[256,384]{1,0:T(8,128)S(1)}, u32[]{:S(2)}, u32[]{:S(2)}) collective-permute-start(f32[256,384]{1,0:T(8,128)S(1)} %shard_map.110), channel_id=1, source_target_pairs={{0,4},{4,0},{8,12},{12,8},{1,5},{5,1},{9,13},{13,9},{2,6},{6,2},{1... | collective-permute-start | bytes 1179656 | tf_op jit(solution)/shard_map/ppermute | solution.py:61
  68.4 20.4 %collective-permute-start.10 = (f32[256,384]{1,0:T(8,128)S(1)}, f32[256,384]{1,0:T(8,128)S(1)}, u32[]{:S(2)}, u32[]{:S(2)}) collective-permute-start(f32[256,384]{1,0:T(8,128)S(1)} %shard_map.108), channel_id=1, source_target_pairs={{0,8},{4,12},{8,0},{12,4},{1,9},{5,13},{9,1},{13,5},{2,10},{6,14},... | collective-permute-start | bytes 1179656 | tf_op jit(solution)/shard_map/ppermute | solution.py:61
  73.5 33.6 %collective-permute-start.18 = (f32[128,1024]{1,0:T(8,128)S(1)}, f32[128,1024]{1,0:T(8,128)S(1)}, u32[]{:S(2)}, u32[]{:S(2)}) collective-permute-start(f32[128,1024]{1,0:T(8,128)S(1)} %get-tuple-element.61), channel_id=1, source_target_pairs={{0,2},{1,3},{2,0},{3,1},{4,6},{5,7},{6,4},{7,5},{8,10},{9,11},{10,... | collective-permute-start | bytes 1572872 | tf_op jit(solution)/shard_map/ppermute | solution.py:61
  86.9 17.7 %collective-permute-start.15 = (f32[256,384]{1,0:T(8,128)S(1)}, f32[256,384]{1,0:T(8,128)S(1)}, u32[]{:S(2)}, u32[]{:S(2)}) collective-permute-start(f32[256,384]{1,0:T(8,128)S(1)} %shard_map.111), channel_id=1, source_target_pairs={{0,4},{4,0},{8,12},{12,8},{1,5},{5,1},{9,13},{13,9},{2,6},{6,2},{1... | collective-permute-start | bytes 1179656 | tf_op jit(solution)/shard_map/ppermute | solution.py:61
  88.8 18.2 %collective-permute-start.17 = (f32[256,384]{1,0:T(8,128)S(1)}, f32[256,384]{1,0:T(8,128)S(1)}, u32[]{:S(2)}, u32[]{:S(2)}) collective-permute-start(f32[256,384]{1,0:T(8,128)S(1)} %shard_map.117), channel_id=1, source_target_pairs={{0,8},{4,12},{8,0},{12,4},{1,9},{5,13},{9,1},{13,5},{2,10},{6,14},... | collective-permute-start | bytes 1179656 | tf_op jit(solution)/shard_map/ppermute | solution.py:61
